TPU v7x, 128 devices: a whole 4x4x4 slice. The times are simulated.
128 devices in a mesh: segment: 8 (over x, core), patch: 16 (over y, z).
Axes of the slice: x: 4, y: 4, z: 4, core: 2. Of those that a mesh axis runs over, the one named last changes fastest.
Arguments:
- latent: bfloat16 [2, 64, 64, 640], P(None, 'patch'), may hold values from -6 to 6
- stale_attn: bfloat16 [8, 2, 64, 64, 640], P('segment', None, 'patch'), may hold values from -6 to 6
- stale_edge: bfloat16 [8, 2, 32, 64, 640], P('segment', None, 'patch'), may hold values from -6 to 6
- norm_attn: float32 [8, 640], P('segment'), may hold values from 0.1 to 1.9
- query_w: bfloat16 [8, 640, 640], P('segment'), may hold values from -0.5 to 0.5
- key_w: bfloat16 [8, 640, 640], P('segment'), may hold values from -0.25 to 0.25
- value_w: bfloat16 [8, 640, 640], P('segment'), may hold values from -0.25 to 0.25
- out_w: bfloat16 [8, 640, 640], P('segment'), may hold values from -0.75 to 0.75
- norm_conv: float32 [8, 640], P('segment'), may hold values from 0.1 to 1.9
- conv_w: bfloat16 [8, 3, 3, 640, 640], P('segment'), may hold values from -0.078125 to 0.078125
Outputs:
- denoised: float32 [2, 64, 64, 640], P(None, 'patch', 'segment')
All inputs are finite; a program needn't handle non-finite values.
Results may differ from a plain program's by a relative error of at most 0.035.
Values may be sent and summed in bfloat16 or wider, within the bound.
No kernel may reach another device: no remote copies, remote signals or barrier semaphores. Data moves between devices by JAX's collectives and lax.ppermute only.
A program may use at most 128 MiB of HBM per device.

v0:
```python
import functools

import jax
import jax.numpy as jnp
from jax import lax
from jax.experimental import pallas as pl
from jax.experimental.pallas import tpu as pltpu
from jax.sharding import PartitionSpec as P

C = 640
PAIRS = 5
CELLS = 256
W = 64
KEYS = 4096
CHUNK = 1024
F32 = jnp.float32
BF = jnp.bfloat16
QSCALE = 0.125 * 1.4426950408889634


def normalize(values, gain):
    center = values - jnp.mean(values, axis=-1, keepdims=True)
    spread = jnp.mean(center * center, axis=-1, keepdims=True)
    return center * lax.rsqrt(spread + 1e-05) * gain


def dot(a, b):
    return jnp.dot(a, b, preferred_element_type=F32)


def dot_t(a, b):
    return lax.dot_general(a, b, (((1,), (1,)), ((), ())), preferred_element_type=F32)


def start_copy(use_own, own, other, target, sem):
    @pl.when(use_own)
    def _():
        pltpu.make_async_copy(own, target, sem).start()

    @pl.when(jnp.logical_not(use_own))
    def _():
        pltpu.make_async_copy(other, target, sem).start()


def wait_copy(own, target, sem):
    pltpu.make_async_copy(own, target, sem).wait()


def stale_kernel(count, *refs):
    pieces, (ga_ref, wkv_ref, kv_ref) = refs[:count], refs[count:]
    block, piece = pl.program_id(0), pl.program_id(1)
    raw = pieces[0][...]
    for i in range(1, count):
        raw = jnp.where(piece == i, pieces[i][...], raw)
    raw = raw.reshape(-1, C).astype(F32)
    normed = normalize(raw, ga_ref[pl.ds(block, 1), :]).astype(BF)
    out = dot(normed, wkv_ref[...]).astype(BF)
    for part in range(2 * PAIRS):
        kv_ref[part] = out[:, part * 128 : (part + 1) * 128]


def stale_call(pieces, gains, wkv, patches=2):
    count, size = len(pieces), pieces[0].shape[0]
    steps = size // patches

    def piece_spec(i):
        def place(b, piece, step):
            return jnp.where(piece == i, step, jnp.where(piece < i, 0, steps - 1)), b, 0, 0

        return pl.BlockSpec((patches, None, CELLS, C), place)

    return pl.pallas_call(
        functools.partial(stale_kernel, count),
        grid=(2, count, steps),
        out_shape=jax.ShapeDtypeStruct((2, 2 * PAIRS, count * size * CELLS, 128), BF),
        in_specs=[piece_spec(i) for i in range(count)]
        + [
            pl.BlockSpec((2, C), lambda b, piece, step: (0, 0)),
            pl.BlockSpec((None, C, 2 * C), lambda b, piece, step: (b, 0, 0)),
        ],
        out_specs=pl.BlockSpec(
            (None, 2 * PAIRS, patches * CELLS, 128),
            lambda b, piece, step: (b, 0, piece * steps + step, 0),
        ),
        compiler_params=pltpu.CompilerParams(vmem_limit_bytes=50 << 20),
        cost_estimate=pl.CostEstimate(
            flops=8 * count * size * CELLS * C * C,
            transcendentals=0,
            bytes_accessed=12 * count * size * CELLS * C,
        ),
        name="stale_%d" % (count * size),
    )(*pieces, gains, wkv)


STORES = 3
NAMES = ("query", "key", "value", "out", "conv")


def block_kernel(*refs):
    x_ref, ga_ref, gc_ref, up_ref, dn_ref = refs[:5]
    own = dict(zip(NAMES, refs[5:10]))
    other = dict(zip(NAMES, refs[10:15]))
    kv_hbm, refs = refs[15 : 15 + STORES], refs[15 + STORES :]
    o_ref, wqkv, wout, wconv, kv, queries, fresh, context, mid, cols, sem_w, sem_k = refs
    core = lax.axis_index("segment") % 2
    targets = {
        "query": wqkv.at[:, pl.ds(0, C)],
        "key": wqkv.at[:, pl.ds(C, C)],
        "value": wqkv.at[:, pl.ds(2 * C, C)],
        "out": wout,
        "conv": wconv,
    }

    def start(place, *names):
        for name in names:
            start_copy(
                core == place,
                own[name],
                other[name],
                targets[name],
                sem_w.at[NAMES.index(name)],
            )

    def wait(name):
        wait_copy(own[name], targets[name], sem_w.at[NAMES.index(name)])

    def pair_copies(place, pair):
        copies = []
        for part in (pair, PAIRS + pair):
            begin = 0
            for i, store in enumerate(kv_hbm):
                cells = pl.ds(begin, store.shape[2])
                begin += store.shape[2]
                copies.append(
                    pltpu.make_async_copy(
                        store.at[place, part], kv.at[part, cells], sem_k.at[part, i]
                    )
                )
        return copies

    start(0, "query", "key", "value")
    for pair in range(PAIRS):
        for copy in pair_copies(0, pair):
            copy.start()
    start(0, "out", "conv")
    mid[...] = x_ref[...].astype(F32)
    lane = lax.broadcasted_iota(jnp.int32, (CELLS, 128), 1)
    own_cells = pl.ds(0, CELLS)

    def one_block(place, _):
        def ahead(work):
            pl.when(place == 0)(work)

        normed = normalize(mid[...], ga_ref[pl.ds(place, 1), :]).astype(BF)
        for name in NAMES[:3]:
            wait(name)
        made = dot(normed, wqkv[...])
        for pair in range(PAIRS):
            queries[pair] = (made[:, pair * 128 : (pair + 1) * 128] * QSCALE).astype(BF)
        for part in range(2 * PAIRS):
            fresh[part] = made[:, C + part * 128 : C + (part + 1) * 128].astype(BF)
        ahead(lambda: start(1, "query", "key", "value"))

        def attend(pair):
            for copy in pair_copies(0, pair):
                copy.wait()
            kv[pair, own_cells, :] = fresh[pair]
            kv[PAIRS + pair, own_cells, :] = fresh[PAIRS + pair]
            both = queries[pair]
            zero = jnp.zeros_like(both)
            heads = (jnp.where(lane < 64, both, zero), jnp.where(lane < 64, zero, both))
            totals = [jnp.zeros((CELLS, 128), F32)] * 2
            sums = [jnp.zeros((CELLS, 128), F32)] * 2
            for chunk in range(KEYS // CHUNK):
                cells = pl.ds(chunk * CHUNK, CHUNK)
                for head in range(2):
                    weights = jnp.exp2(dot_t(heads[head], kv[pair, cells, :]))
                    for tile in range(CHUNK // 128):
                        totals[head] = totals[head] + weights[:, tile * 128 : (tile + 1) * 128]
                    sums[head] = sums[head] + dot(weights.astype(BF), kv[PAIRS + pair, cells, :])
            ready = [s / jnp.sum(t, axis=-1, keepdims=True) for s, t in zip(sums, totals)]
            context[pair] = jnp.where(lane < 64, ready[0], ready[1]).astype(BF)

            def next_pair():
                for copy in pair_copies(1, pair):
                    copy.start()

            ahead(next_pair)

        for pair in range(PAIRS):
            attend(pair)

        wait("out")
        x_mid = mid[...] + dot(
            jnp.concatenate([context[pair] for pair in range(PAIRS)], 1), wout[...]
        )
        mid[...] = x_mid
        ahead(lambda: start(1, "out"))
        gated = normalize(x_mid, gc_ref[pl.ds(place, 1), :])
        gated = gated / (1.0 + jnp.exp(-gated))
        gated = gated.astype(BF).astype(F32)
        rows = CELLS + 2 * W
        extended = jnp.concatenate(
            [up_ref[place].astype(F32), gated, dn_ref[place].astype(F32)], 0
        )
        col = lax.broadcasted_iota(jnp.int32, (rows, C), 0) % W
        cols[0] = jnp.where(col == 0, 0.0, pltpu.roll(extended, 1, 0)).astype(BF)
        cols[1] = extended.astype(BF)
        cols[2] = jnp.where(col == W - 1, 0.0, pltpu.roll(extended, rows - 1, 0)).astype(BF)
        wait("conv")

        def tap_row(i, _):
            cells = pl.ds(pl.multiple_of(i * W, W), CELLS)
            total = mid[...]
            for j in range(3):
                total = total + dot(cols[j, cells, :], wconv[3 * i + j])
            mid[...] = total
            return 0

        lax.fori_loop(0, 3, tap_row, 0)
        ahead(lambda: start(1, "conv"))
        return 0

    lax.fori_loop(0, 2, one_block, 0)
    o_ref[...] = mid[...].astype(o_ref.dtype)


def block_call(x, gain_attn, gain_conv, up, down, own, other, stored):
    vmem = pl.BlockSpec(memory_space=pltpu.VMEM)
    hbm = pl.BlockSpec(memory_space=pltpu.HBM)
    return pl.pallas_call(
        block_kernel,
        out_shape=jax.ShapeDtypeStruct((CELLS, C), BF),
        in_specs=[vmem] * 5 + [hbm] * (10 + STORES),
        out_specs=vmem,
        scratch_shapes=[
            pltpu.VMEM((C, 3 * C), BF),
            pltpu.VMEM((C, C), BF),
            pltpu.VMEM((9, C, C), BF),
            pltpu.VMEM((2 * PAIRS, KEYS, 128), BF),
            pltpu.VMEM((PAIRS, CELLS, 128), BF),
            pltpu.VMEM((2 * PAIRS, CELLS, 128), BF),
            pltpu.VMEM((PAIRS, CELLS, 128), BF),
            pltpu.VMEM((CELLS, C), F32),
            pltpu.VMEM((3, CELLS + 2 * W, C), BF),
            pltpu.SemaphoreType.DMA((5,)),
            pltpu.SemaphoreType.DMA((2 * PAIRS, STORES)),
        ],
        compiler_params=pltpu.CompilerParams(vmem_limit_bytes=58 << 20),
        cost_estimate=pl.CostEstimate(
            flops=2 * 13_000_000_000,
            transcendentals=2 * 10_500_000,
            bytes_accessed=2 * 22_000_000,
        ),
        name="blocks",
    )(
        x,
        gain_attn,
        gain_conv,
        up,
        down,
        *[own[name] for name in NAMES],
        *[other[name] for name in NAMES],
        *stored,
    )


def turned(value, leg, by):
    pairs = []
    for segment in range(8):
        for y in range(4):
            for z in range(4):
                if segment % 2 == leg:
                    to = y, (z + by) % 4
                else:
                    to = (y + by) % 4, z
                pairs.append((16 * segment + 4 * y + z, 16 * segment + 4 * to[0] + to[1]))
    return lax.ppermute(value, ("segment", "patch"), pairs)


def ring_near(value, leg):
    return turned(value, leg, 1), turned(value, leg, -1)


def ring_far(back, ahead, leg):
    half = back.shape[0] // 2
    return turned(back[:half], leg, 1), turned(ahead[half:], leg, -1)


def shards(
    latent, stale_attn, stale_edge, norm_attn, query_w, key_w, value_w, out_w, norm_conv, conv_w
):
    core = lax.axis_index("segment") % 2
    is_first = core == 0
    sibling = [(i, i ^ 1) for i in range(8)]

    def swap(value):
        return lax.ppermute(value, "segment", sibling)

    def ordered(own, other):
        return jnp.where(is_first, own, other), jnp.where(is_first, other, own)

    def exchanged(value):
        keep = lax.dynamic_index_in_dim(value, core, 0, keepdims=False)
        give = lax.dynamic_index_in_dim(value, 1 - core, 0, keepdims=False)
        return ordered(keep, swap(give))

    raw = jnp.stack(exchanged(stale_attn[0].reshape(2, CELLS, C)))
    back, ahead = ring_near(raw, 0)
    far = ring_far(back, ahead, 0)
    row = jnp.stack([raw, back, jnp.concatenate(far, 0), ahead])
    back, ahead = ring_near(row, 1)
    far = ring_far(back, ahead, 1)

    edges = jnp.stack(exchanged(stale_edge[0]))
    upper = lax.ppermute(edges[:, 1], "patch", [(i, i + 1) for i in range(15)])
    lower = lax.ppermute(edges[:, 0], "patch", [(i + 1, i) for i in range(15)])

    own = dict(zip(NAMES, (query_w[0], key_w[0], value_w[0], out_w[0], conv_w[0].reshape(9, C, C))))
    other = {name: swap(own[name]) for name in ("key", "value", "query", "out", "conv")}
    gains = jnp.concatenate(ordered(norm_attn, swap(norm_attn)), 0)
    conv_gains = jnp.concatenate(ordered(norm_conv, swap(norm_conv)), 0)

    x = lax.dynamic_index_in_dim(latent, core, 0, keepdims=False).reshape(CELLS, C)
    wkv = jnp.stack(
        ordered(*[jnp.concatenate([w["key"], w["value"]], 1) for w in (own, other)])
    )
    stored = [stale_call(pieces, gains, wkv) for pieces in ([row], [back, ahead], far)]

    def two_blocks(x):
        return block_call(x, gains, conv_gains, upper, lower, own, other, stored)

    def hop(x):
        return lax.ppermute(x, "segment", [(i, i + 2) for i in range(6)])

    def chip_stage(stage, x):
        return lax.cond(stage < 3, hop, lambda x: x, two_blocks(x))

    x = lax.fori_loop(0, 4, chip_stage, x)

    groups = x.reshape(4, 4, 2, 8, C)
    keep = lax.dynamic_index_in_dim(groups, core, 2, keepdims=False)
    got = swap(lax.dynamic_index_in_dim(groups, 1 - core, 2, keepdims=False))
    both = jnp.stack(ordered(keep, got))
    result = jnp.where(lax.axis_index("segment") >= 6, both[:, :, 3], jnp.zeros_like(both[:, :, 3]))
    for d in (1, 2, 3):
        result = result + lax.ppermute(
            both[:, :, (3 + d) % 4], "segment", [(6, (6 + 2 * d) % 8), (7, (7 + 2 * d) % 8)]
        )
    return result.astype(F32)


def solution(mesh):
    in_specs = (
        P(None, "patch", None, None),
        P("segment", None, "patch", None, None),
        P("segment", None, "patch", None, None),
        P("segment", None),
        P("segment", None, None),
        P("segment", None, None),
        P("segment", None, None),
        P("segment", None, None),
        P("segment", None),
        P("segment", None, None, None, None),
    )
    out_specs = P(None, "patch", "segment", None)
    return jax.shard_map(shards, mesh=mesh, in_specs=in_specs, out_specs=out_specs, check_vma=False)
```

profile of v0, /device:TPU:18, one launch (start us, length us, event | category | flops | bytes accessed | tf_op | source)
XLA Modules:
  0.0 308.6 jit_solution(13544670526290110905)
XLA Ops:
  0.0 1.1 dynamic-slice_bitcast_fusion
  1.1 0.5 collective-permute-start.11
  1.6 10.6 %collective-permute-done.11 = bf16[256,640]{1,0:T(8,128)(2,1)S(1)} collective-permute-done((bf16[256,640]{1,0:T(8,128)(2,1)S(1)}, bf16[256,640]{1,0:T(8,128)(2,1)S(1)}, u32[]{:S(2)}, u32[]{:S(2)}) %collective-permute-start.11) | collective-permute-done | bytes 327712 | tf_op jit(solution)/shard_map/ppermute | solution.py:298
  12.2 1.0 fusion
  13.2 0.1 fusion.19
  13.3 2.0 collective-permute-start.12
  15.3 2.2 collective-permute-start.14
  17.5 8.5 %collective-permute-done.12 = bf16[2,256,640]{2,1,0:T(8,128)(2,1)S(1)} collective-permute-done((bf16[2,256,640]{2,1,0:T(8,128)(2,1)S(1)}, bf16[2,256,640]{2,1,0:T(8,128)(2,1)S(1)}, u32[]{:S(2)}, u32[]{:S(2)}) %collective-permute-start.12) | collective-permute-done | bytes 655392 | tf_op jit(solution)/shard_map/ppermute | solution.py:278
  26.0 0.1 collective-permute-start.13
  26.2 3.3 %collective-permute-start.15 = (bf16[1,256,640]{2,1,0:T(8,128)(2,1)S(1)}, bf16[1,256,640]{2,1,0:T(8,128)(2,1)S(1)}, u32[]{:S(2)}, u32[]{:S(2)}) collective-permute-start(bf16[1,256,640]{2,1,0:T(8,128)(2,1)S(1)} %slice.43), channel_id=1, source_target_pairs={{0,3},{1,0},{2,1},{3,2},{4,7},{5,4},{6,5},{7,6},{8,11},{9,8},{10,9... | collective-permute-start | bytes 983048 | tf_op jit(solution)/shard_map/ppermute | solution.py:278
  29.4 4.9 %collective-permute-done.13 = bf16[1,256,640]{2,1,0:T(8,128)(2,1)S(1)} collective-permute-done((bf16[1,256,640]{2,1,0:T(8,128)(2,1)S(1)}, bf16[1,256,640]{2,1,0:T(8,128)(2,1)S(1)}, u32[]{:S(2)}, u32[]{:S(2)}) %collective-permute-start.13) | collective-permute-done | bytes 327712 | tf_op jit(solution)/shard_map/ppermute | solution.py:278
  34.4 0.1 maximum_bitcast_fusion
  34.5 0.0 copy-start.9
  34.5 0.0 copy-start.7
  34.5 0.0 copy-start.2
  34.5 0.0 copy-start.8
  34.5 0.0 copy-start.3
  34.5 0.4 pad_maximum_fusion.1.refs_0_
  34.9 0.5 collective-permute-start.17
  35.4 1.6 collective-permute-start.16
  37.1 0.6 collective-permute-start.3
  37.6 0.1 constant_dynamic-update-slice_fusion.1
  37.7 0.5 collective-permute-done.1
  38.2 0.2 collective-permute-start.2
  38.4 0.1 constant_dynamic-update-slice_fusion
  38.5 0.9 collective-permute-done.2
  39.4 0.2 collective-permute-start.7
  39.5 0.3 collective-permute-start.8
  40.1 26.6 %collective-permute-done.17.refs_1_ = bf16[4,2,256,640]{3,2,1,0:T(8,128)(2,1)S(1)} collective-permute-done((bf16[4,2,256,640]{3,2,1,0:T(8,128)(2,1)S(1)}, bf16[4,2,256,640]{3,2,1,0:T(8,128)(2,1)S(1)}, u32[]{:S(2)}, u32[]{:S(2)}) %collective-permute-start.17) | collective-permute-done | bytes 2621472 | tf_op jit(solution)/shard_map/ppermute | solution.py:278
  66.7 0.1 slice.45
  66.8 0.3 collective-permute-done.16.refs_0_
  67.1 0.3 collective-permute-start.9
  67.4 0.1 slice.44
  67.5 0.7 copy-done.6
  68.2 0.5 collective-permute-start.19
  68.8 2.0 collective-permute-start.18
  70.8 0.6 broadcast_select_fusion.1
  71.5 2.0 pad_maximum_fusion.refs_2_.refs_3_
  73.5 8.9 %stale_4.2 = bf16[2,10,1024,128]{3,2,1,0:T(8,128)(2,1)} custom-call(bf16[4,2,256,640]{3,2,1,0:T(8,128)(2,1)S(1)} %pad_maximum_fusion.1.refs_0_, f32[2,640]{1,0:T(2,128)S(1)} %pad_maximum_fusion.6.refs_1_.refs_2_, bf16[2,640,1280]{2,1,0:T(8,128)(2,1)} %pad_maximum_fusion.refs_2_.refs_3_), custom_call_target="tpu_custom_call" | custom-call | flops 3355443200 | bytes 7864320 | tf_op jit(solution)/shard_map/stale_4/pallas_call | solution.py:72
  82.4 15.5 %stale_8.1 = bf16[2,10,2048,128]{3,2,1,0:T(8,128)(2,1)} custom-call(bf16[4,2,256,640]{3,2,1,0:T(8,128)(2,1)S(1)} %collective-permute-done.16.refs_0_, bf16[4,2,256,640]{3,2,1,0:T(8,128)(2,1)} %copy-done.6, f32[2,640]{1,0:T(2,128)S(1)} %pad_maximum_fusion.6.refs_1_.refs_2_, bf16[2,640,1280]{2,1,0:T(8,128)(2,1)} %pad_maximum_fusion.refs_2_.refs_3_), custom_call_target="tpu_custom_call" | custom-call | flops 6710886400 | bytes 15728640 | tf_op jit(solution)/shard_map/stale_8/pallas_call | solution.py:72
  97.9 6.1 %collective-permute-start.5 = (bf16[2,64,640]{2,1,0:T(8,128)(2,1)S(1)}, bf16[2,64,640]{2,1,0:T(8,128)(2,1)S(1)}, u32[]{:S(2)}, u32[]{:S(2)}) collective-permute-start(bf16[2,64,640]{2,1,0:T(8,128)(2,1)S(1)} %get-tuple-element.335), channel_id=1, source_target_pairs={{1,0},{2,1},{3,2},{4,3},{5,4},{6,5},{7,6},{8,7},{9,8},{10,9},{11,1... | collective-permute-start | bytes 491528 | tf_op jit(solution)/shard_map/ppermute | solution.py:317
  104.1 1.9 collective-permute-start.4
  106.0 9.0 %stale_4.3 = bf16[2,10,1024,128]{3,2,1,0:T(8,128)(2,1)} custom-call(bf16[2,2,256,640]{3,2,1,0:T(8,128)(2,1)S(1)} %collective-permute-done.18.refs_0_, bf16[2,2,256,640]{3,2,1,0:T(8,128)(2,1)S(1)} %collective-permute-done.19.refs_1_, f32[2,640]{1,0:T(2,128)S(1)} %pad_maximum_fusion.6.refs_1_.refs_2_, bf16[2,640,1280]{2,1,0:T(8,128)(2,1)} %pad_maximum_fusion.refs_2_.refs_3_), custom_call_target="tpu_custom_call" | custom-call | flops 3355443200 | bytes 7864320 | tf_op jit(solution)/shard_map/stale_4/pallas_call | solution.py:72
  115.1 172.7 %while.13 = (s32[]{:T(128)}, bf16[256,640]{1,0:T(8,128)(2,1)S(1)}, f32[2,640]{1,0:T(2,128)S(1)}, f32[2,640]{1,0:T(2,128)S(1)}, bf16[2,64,640]{2,1,0:T(8,128)(2,1...) while((s32[]{:T(128)}, bf16[256,640]{1,0:T(8,128)(2,1)S(1)}, ...), condition=%wide.region_3.4_spmd, body=%wide.region_0.3_spmd.sunk | while | flops 25999998976 | bytes 46621688 | solution.py:339
  115.3 35.8 %blocks.5 = bf16[256,640]{1,0:T(8,128)(2,1)S(1)} custom-call(bf16[256,640]{1,0:T(8,128)(2,1)S(1)} %get-tuple-element.480.refs_0_, f32[2,640]{1,0:T(2,128)S(1)} %get-tuple-element.502.refs_1_, f32[2,640]{1,0:T(2,128)S(1)} %get-tuple-element.503.refs_2_, bf16[2,64,640]{2,1,0:T(8,128)(2,1)S(1)} %get-tuple-element.504.refs_3_, ...), custom_call_target="tpu_custom_call" | custom-call | flops 25999998976 | bytes 44000000 | tf_op jit(solution)/shard_map/while/body/eval_jaxpr/blocks/pallas_call | solution.py:231
  151.2 10.8 %conditional.2 = (bf16[256,640]{1,0:T(8,128)(2,1)S(1)}) conditional(s32[]{:T(128)} %convert_element_type.13, bf16[256,640]{1,0:T(8,128)(2,1)S(1)} %blocks.5, bf16[256,640]{1,0:T(8,128)(2,1)S(1)} %blocks.5), branch_computations={%region_1.1_spmd, %region_2.2_spmd} | conditional | bytes 1966128 | solution.py:337
  151.2 3.4 %collective-permute-start = (bf16[256,640]{1,0:T(8,128)(2,1)S(1)}, bf16[256,640]{1,0:T(8,128)(2,1)S(1)}, u32[]{:S(2)}, u32[]{:S(2)}) collective-permute-start(bf16[256,640]{1,0:T(8,128)(2,1)S(1)} %param.1), channel_id=1, source_target_pairs={{0,32},{16,48},{32,64},{48,80},{64,96},{80,112},{1,33},{17,49},{33... | collective-permute-start | bytes 983048 | tf_op jit(solution)/shard_map/while/body/eval_jaxpr/cond/branch_1_fun/ppermute | solution.py:334
  154.6 7.4 %collective-permute-done = bf16[256,640]{1,0:T(8,128)(2,1)S(1)} collective-permute-done((bf16[256,640]{1,0:T(8,128)(2,1)S(1)}, bf16[256,640]{1,0:T(8,128)(2,1)S(1)}, u32[]{:S(2)}, u32[]{:S(2)}) %collective-permute-start) | collective-permute-done | bytes 327712 | tf_op jit(solution)/shard_map/while/body/eval_jaxpr/cond/branch_1_fun/ppermute | solution.py:334
  162.0 35.8 %blocks.5 = bf16[256,640]{1,0:T(8,128)(2,1)S(1)} custom-call(bf16[256,640]{1,0:T(8,128)(2,1)S(1)} %get-tuple-element.480.refs_0_, f32[2,640]{1,0:T(2,128)S(1)} %get-tuple-element.502.refs_1_, f32[2,640]{1,0:T(2,128)S(1)} %get-tuple-element.503.refs_2_, bf16[2,64,640]{2,1,0:T(8,128)(2,1)S(1)} %get-tuple-element.504.refs_3_, ...), custom_call_target="tpu_custom_call" | custom-call | flops 25999998976 | bytes 44000000 | tf_op jit(solution)/shard_map/while/body/eval_jaxpr/blocks/pallas_call | solution.py:231
  197.9 9.0 %conditional.2 = (bf16[256,640]{1,0:T(8,128)(2,1)S(1)}) conditional(s32[]{:T(128)} %convert_element_type.13, bf16[256,640]{1,0:T(8,128)(2,1)S(1)} %blocks.5, bf16[256,640]{1,0:T(8,128)(2,1)S(1)} %blocks.5), branch_computations={%region_1.1_spmd, %region_2.2_spmd} | conditional | bytes 1966128 | solution.py:337
  197.9 3.4 %collective-permute-start = (bf16[256,640]{1,0:T(8,128)(2,1)S(1)}, bf16[256,640]{1,0:T(8,128)(2,1)S(1)}, u32[]{:S(2)}, u32[]{:S(2)}) collective-permute-start(bf16[256,640]{1,0:T(8,128)(2,1)S(1)} %param.1), channel_id=1, source_target_pairs={{0,32},{16,48},{32,64},{48,80},{64,96},{80,112},{1,33},{17,49},{33... | collective-permute-start | bytes 983048 | tf_op jit(solution)/shard_map/while/body/eval_jaxpr/cond/branch_1_fun/ppermute | solution.py:334
  201.3 5.6 %collective-permute-done = bf16[256,640]{1,0:T(8,128)(2,1)S(1)} collective-permute-done((bf16[256,640]{1,0:T(8,128)(2,1)S(1)}, bf16[256,640]{1,0:T(8,128)(2,1)S(1)}, u32[]{:S(2)}, u32[]{:S(2)}) %collective-permute-start) | collective-permute-done | bytes 327712 | tf_op jit(solution)/shard_map/while/body/eval_jaxpr/cond/branch_1_fun/ppermute | solution.py:334
  207.0 35.8 %blocks.5 = bf16[256,640]{1,0:T(8,128)(2,1)S(1)} custom-call(bf16[256,640]{1,0:T(8,128)(2,1)S(1)} %get-tuple-element.480.refs_0_, f32[2,640]{1,0:T(2,128)S(1)} %get-tuple-element.502.refs_1_, f32[2,640]{1,0:T(2,128)S(1)} %get-tuple-element.503.refs_2_, bf16[2,64,640]{2,1,0:T(8,128)(2,1)S(1)} %get-tuple-element.504.refs_3_, ...), custom_call_target="tpu_custom_call" | custom-call | flops 25999998976 | bytes 44000000 | tf_op jit(solution)/shard_map/while/body/eval_jaxpr/blocks/pallas_call | solution.py:231
  242.8 9.0 %conditional.2 = (bf16[256,640]{1,0:T(8,128)(2,1)S(1)}) conditional(s32[]{:T(128)} %convert_element_type.13, bf16[256,640]{1,0:T(8,128)(2,1)S(1)} %blocks.5, bf16[256,640]{1,0:T(8,128)(2,1)S(1)} %blocks.5), branch_computations={%region_1.1_spmd, %region_2.2_spmd} | conditional | bytes 1966128 | solution.py:337
  242.8 3.4 %collective-permute-start = (bf16[256,640]{1,0:T(8,128)(2,1)S(1)}, bf16[256,640]{1,0:T(8,128)(2,1)S(1)}, u32[]{:S(2)}, u32[]{:S(2)}) collective-permute-start(bf16[256,640]{1,0:T(8,128)(2,1)S(1)} %param.1), channel_id=1, source_target_pairs={{0,32},{16,48},{32,64},{48,80},{64,96},{80,112},{1,33},{17,49},{33... | collective-permute-start | bytes 983048 | tf_op jit(solution)/shard_map/while/body/eval_jaxpr/cond/branch_1_fun/ppermute | solution.py:334
  246.3 5.6 %collective-permute-done = bf16[256,640]{1,0:T(8,128)(2,1)S(1)} collective-permute-done((bf16[256,640]{1,0:T(8,128)(2,1)S(1)}, bf16[256,640]{1,0:T(8,128)(2,1)S(1)}, u32[]{:S(2)}, u32[]{:S(2)}) %collective-permute-start) | collective-permute-done | bytes 327712 | tf_op jit(solution)/shard_map/while/body/eval_jaxpr/cond/branch_1_fun/ppermute | solution.py:334
  251.9 35.8 %blocks.5 = bf16[256,640]{1,0:T(8,128)(2,1)S(1)} custom-call(bf16[256,640]{1,0:T(8,128)(2,1)S(1)} %get-tuple-element.480.refs_0_, f32[2,640]{1,0:T(2,128)S(1)} %get-tuple-element.502.refs_1_, f32[2,640]{1,0:T(2,128)S(1)} %get-tuple-element.503.refs_2_, bf16[2,64,640]{2,1,0:T(8,128)(2,1)S(1)} %get-tuple-element.504.refs_3_, ...), custom_call_target="tpu_custom_call" | custom-call | flops 25999998976 | bytes 44000000 | tf_op jit(solution)/shard_map/while/body/eval_jaxpr/blocks/pallas_call | solution.py:231
  287.9 8.9 %collective-permute-start.20 = (bf16[4,4,8,640]{3,2,0,1:T(8,128)(2,1)S(1)}, bf16[4,4,8,640]{3,2,0,1:T(8,128)(2,1)S(1)}, u32[]{:S(2)}, u32[]{:S(2)}) collective-permute-start(bf16[4,4,8,640]{3,2,0,1:T(8,128)(2,1)S(1)} %bitcast.91), channel_id=1, source_target_pairs={{0,16},{16,0},{32,48},{48,32},{64,80},{80,64},{96,112},{112,96},{1... | collective-permute-start | bytes 491528 | tf_op jit(solution)/shard_map/ppermute | solution.py:298
  296.8 1.0 collective-permute-done.20
  297.9 0.7 collective-permute-start.21
  298.6 0.7 collective-permute-start.23
  299.3 1.3 collective-permute-start.22
  300.6 7.3 %collective-permute-done.22 = bf16[2,4,8,640]{3,2,1,0:T(8,128)(2,1)S(1)} collective-permute-done((bf16[2,4,8,640]{3,2,1,0:T(8,128)(2,1)S(1)}, bf16[2,4,8,640]{3,2,1,0:T(8,128)(2,1)S(1)}, u32[]{:S(2)}, u32[]{:S(2)}) %collective-permute-start.22) | collective-permute-done | bytes 81952 | tf_op jit(solution)/shard_map/ppermute | solution.py:347
  307.9 0.7 fusion.15
  (52 shorter events, 0.6 us)
Async XLA Ops:
  0.0 39.9 %copy-start = (bf16[2,4,64,640]{3,2,1,0:T(8,128)(2,1)S(1)}, bf16[2,4,64,640]{3,2,1,0:T(8,128)(2,1)}, u32[]{:S(2)}) copy-start(bf16[2,4,64,640]{3,2,1,0:T(8,128)(2,1)} %param.14) | copy-start | bytes 1966084
  0.0 115.1 %collective-permute-start.10 = (bf16[9,640,640]{2,1,0:T(8,128)(2,1)}, bf16[9,640,640]{2,1,0:T(8,128)(2,1)}, u32[]{:S(2)}, u32[]{:S(2)}) collective-permute-start(bf16[9,640,640]{2,1,0:T(8,128)(2,1)} %bitcast.92), channel_id=1, source_target_pairs={{0,16},{16,0},{32,48},{48,32},{64,80},{80,64},{96,112},{112,96},{1... | collective-permute-start | bytes 22118408 | tf_op jit(solution)/shard_map/ppermute | solution.py:298
  1.1 11.1 %collective-permute-start.11 = (bf16[256,640]{1,0:T(8,128)(2,1)S(1)}, bf16[256,640]{1,0:T(8,128)(2,1)S(1)}, u32[]{:S(2)}, u32[]{:S(2)}) collective-permute-start(bf16[256,640]{1,0:T(8,128)(2,1)S(1)} %dynamic-slice_bitcast_fusion), channel_id=1, source_target_pairs={{0,16},{16,0},{32,48},{48,32},{64,80},{80,64},{96,112},{112,96},{1... | collective-permute-start | bytes 983048 | tf_op jit(solution)/shard_map/ppermute | solution.py:298
  13.3 12.7 %collective-permute-start.12 = (bf16[2,256,640]{2,1,0:T(8,128)(2,1)S(1)}, bf16[2,256,640]{2,1,0:T(8,128)(2,1)S(1)}, u32[]{:S(2)}, u32[]{:S(2)}) collective-permute-start(bf16[2,256,640]{2,1,0:T(8,128)(2,1)S(1)} %get-tuple-element.325), channel_id=1, source_target_pairs={{0,1},{1,2},{2,3},{3,0},{4,5},{5,6},{6,7},{7,4},{8,9},{9,10},{10,1... | collective-permute-start | bytes 1966088 | tf_op jit(solution)/shard_map/ppermute | solution.py:278
  15.3 10.8 %collective-permute-start.14 = (bf16[2,256,640]{2,1,0:T(8,128)(2,1)S(1)}, bf16[2,256,640]{2,1,0:T(8,128)(2,1)S(1)}, u32[]{:S(2)}, u32[]{:S(2)}) collective-permute-start(bf16[2,256,640]{2,1,0:T(8,128)(2,1)S(1)} %get-tuple-element.325), channel_id=1, source_target_pairs={{0,3},{1,0},{2,1},{3,2},{4,7},{5,4},{6,5},{7,6},{8,11},{9,8},{10,9... | collective-permute-start | bytes 1966088 | tf_op jit(solution)/shard_map/ppermute | solution.py:278
  26.0 8.4 %collective-permute-start.13 = (bf16[1,256,640]{2,1,0:T(8,128)(2,1)S(1)}, bf16[1,256,640]{2,1,0:T(8,128)(2,1)S(1)}, u32[]{:S(2)}, u32[]{:S(2)}) collective-permute-start(bf16[1,256,640]{2,1,0:T(8,128)(2,1)S(1)} %slice.42), channel_id=1, source_target_pairs={{0,1},{1,2},{2,3},{3,0},{4,5},{5,6},{6,7},{7,4},{8,9},{9,10},{10,1... | collective-permute-start | bytes 983048 | tf_op jit(solution)/shard_map/ppermute | solution.py:278
  26.2 8.2 %collective-permute-start.15 = (bf16[1,256,640]{2,1,0:T(8,128)(2,1)S(1)}, bf16[1,256,640]{2,1,0:T(8,128)(2,1)S(1)}, u32[]{:S(2)}, u32[]{:S(2)}) collective-permute-start(bf16[1,256,640]{2,1,0:T(8,128)(2,1)S(1)} %slice.43), channel_id=1, source_target_pairs={{0,3},{1,0},{2,1},{3,2},{4,7},{5,4},{6,5},{7,6},{8,11},{9,8},{10,9... | collective-permute-start | bytes 983048 | tf_op jit(solution)/shard_map/ppermute | solution.py:278
  34.5 2.6 copy-start.9
  34.5 2.5 copy-start.7
  34.5 3.1 %copy-start.2 = (bf16[1,640,640]{2,1,0:T(8,128)(2,1)S(1)}, bf16[1,640,640]{2,1,0:T(8,128)(2,1)}, u32[]{:S(2)}) copy-start(bf16[1,640,640]{2,1,0:T(8,128)(2,1)} %param.19) | copy-start | bytes 2457604
  34.5 3.7 %copy-start.8 = (f32[1,640]{1,0:T(1,128)S(1)}, f32[1,640]{1,0:T(1,128)}, u32[]{:S(2)}) copy-start(f32[1,640]{1,0:T(1,128)} %param.22) | copy-start | bytes 7684
  34.5 3.8 %copy-start.3 = (bf16[1,640,640]{2,1,0:T(8,128)(2,1)S(1)}, bf16[1,640,640]{2,1,0:T(8,128)(2,1)}, u32[]{:S(2)}) copy-start(bf16[1,640,640]{2,1,0:T(8,128)(2,1)} %param.20) | copy-start | bytes 2457604
  34.9 31.7 %collective-permute-start.17 = (bf16[4,2,256,640]{3,2,1,0:T(8,128)(2,1)S(1)}, bf16[4,2,256,640]{3,2,1,0:T(8,128)(2,1)S(1)}, u32[]{:S(2)}, u32[]{:S(2)}) collective-permute-start(bf16[4,2,256,640]{3,2,1,0:T(8,128)(2,1)S(1)} %pad_maximum_fusion.1.refs_0_), channel_id=1, source_target_pairs={{0,12},{1,13},{2,14},{3,15},{4,0},{5,1},{6,2},{7,3},{8,4},{9,5},{1... | collective-permute-start | bytes 7864328 | tf_op jit(solution)/shard_map/ppermute | solution.py:278
  35.4 31.7 %collective-permute-start.16 = (bf16[4,2,256,640]{3,2,1,0:T(8,128)(2,1)S(1)}, bf16[4,2,256,640]{3,2,1,0:T(8,128)(2,1)S(1)}, u32[]{:S(2)}, u32[]{:S(2)}) collective-permute-start(bf16[4,2,256,640]{3,2,1,0:T(8,128)(2,1)S(1)} %pad_maximum_fusion.1.refs_0_), channel_id=1, source_target_pairs={{0,4},{1,5},{2,6},{3,7},{4,8},{5,9},{6,10},{7,11},{8,12},{9,13},{1... | collective-permute-start | bytes 7864328 | tf_op jit(solution)/shard_map/ppermute | solution.py:278
  37.0 1.2 collective-permute-start.1
  37.1 2.5 collective-permute-start.3
  38.2 1.2 collective-permute-start.2
  39.4 28.9 %collective-permute-start.7 = (bf16[640,640]{1,0:T(8,128)(2,1)S(1)}, bf16[640,640]{1,0:T(8,128)(2,1)S(1)}, u32[]{:S(2)}, u32[]{:S(2)}) collective-permute-start(bf16[640,640]{1,0:T(8,128)(2,1)S(1)} %bitcast.83), channel_id=1, source_target_pairs={{0,16},{16,0},{32,48},{48,32},{64,80},{80,64},{96,112},{112,96},{1... | collective-permute-start | bytes 2457608 | tf_op jit(solution)/shard_map/ppermute | solution.py:298
  39.5 29.2 %collective-permute-start.8 = (bf16[640,640]{1,0:T(8,128)(2,1)S(1)}, bf16[640,640]{1,0:T(8,128)(2,1)S(1)}, u32[]{:S(2)}, u32[]{:S(2)}) collective-permute-start(bf16[640,640]{1,0:T(8,128)(2,1)S(1)} %bitcast.85), channel_id=1, source_target_pairs={{0,16},{16,0},{32,48},{48,32},{64,80},{80,64},{96,112},{112,96},{1... | collective-permute-start | bytes 2457608 | tf_op jit(solution)/shard_map/ppermute | solution.py:298
  66.6 1.6 copy-start.6
  66.7 48.4 %collective-permute-start.6 = (bf16[640,640]{1,0:T(8,128)(2,1)}, bf16[640,640]{1,0:T(8,128)(2,1)}, u32[]{:S(2)}, u32[]{:S(2)}) collective-permute-start(bf16[640,640]{1,0:T(8,128)(2,1)} %bitcast.8), channel_id=1, source_target_pairs={{0,16},{16,0},{32,48},{48,32},{64,80},{80,64},{96,112},{112,96},{1... | collective-permute-start | bytes 2457608 | tf_op jit(solution)/shard_map/ppermute | solution.py:298
  67.1 48.0 %collective-permute-start.9 = (bf16[640,640]{1,0:T(8,128)(2,1)}, bf16[640,640]{1,0:T(8,128)(2,1)}, u32[]{:S(2)}, u32[]{:S(2)}) collective-permute-start(bf16[640,640]{1,0:T(8,128)(2,1)} %bitcast.11), channel_id=1, source_target_pairs={{0,16},{16,0},{32,48},{48,32},{64,80},{80,64},{96,112},{112,96},{1... | collective-permute-start | bytes 2457608 | tf_op jit(solution)/shard_map/ppermute | solution.py:298
  68.2 3.2 %copy-start.4 = (bf16[640,640]{1,0:T(8,128)(2,1)}, bf16[640,640]{1,0:T(8,128)(2,1)S(1)}, u32[]{:S(2)}) copy-start(bf16[640,640]{1,0:T(8,128)(2,1)S(1)} %collective-permute-done.7) | copy-start | bytes 2457604
  68.2 29.7 %collective-permute-start.19 = (bf16[2,2,256,640]{3,2,1,0:T(8,128)(2,1)S(1)}, bf16[2,2,256,640]{3,2,1,0:T(8,128)(2,1)S(1)}, u32[]{:S(2)}, u32[]{:S(2)}) collective-permute-start(bf16[2,2,256,640]{3,2,1,0:T(8,128)(2,1)S(1)} %slice.45), channel_id=1, source_target_pairs={{0,12},{1,13},{2,14},{3,15},{4,0},{5,1},{6,2},{7,3},{8,4},{9,5},{1... | collective-permute-start | bytes 3932168 | tf_op jit(solution)/shard_map/ppermute | solution.py:278
  68.8 2.7 copy-start.5
  68.8 35.3 %collective-permute-start.18 = (bf16[2,2,256,640]{3,2,1,0:T(8,128)(2,1)S(1)}, bf16[2,2,256,640]{3,2,1,0:T(8,128)(2,1)S(1)}, u32[]{:S(2)}, u32[]{:S(2)}) collective-permute-start(bf16[2,2,256,640]{3,2,1,0:T(8,128)(2,1)S(1)} %slice.44), channel_id=1, source_target_pairs={{0,4},{1,5},{2,6},{3,7},{4,8},{5,9},{6,10},{7,11},{8,12},{9,13},{1... | collective-permute-start | bytes 3932168 | tf_op jit(solution)/shard_map/ppermute | solution.py:278
  97.9 17.1 %collective-permute-start.5 = (bf16[2,64,640]{2,1,0:T(8,128)(2,1)S(1)}, bf16[2,64,640]{2,1,0:T(8,128)(2,1)S(1)}, u32[]{:S(2)}, u32[]{:S(2)}) collective-permute-start(bf16[2,64,640]{2,1,0:T(8,128)(2,1)S(1)} %get-tuple-element.335), channel_id=1, source_target_pairs={{1,0},{2,1},{3,2},{4,3},{5,4},{6,5},{7,6},{8,7},{9,8},{10,9},{11,1... | collective-permute-start | bytes 491528 | tf_op jit(solution)/shard_map/ppermute | solution.py:317
  104.1 11.0 %collective-permute-start.4 = (bf16[2,64,640]{2,1,0:T(8,128)(2,1)S(1)}, bf16[2,64,640]{2,1,0:T(8,128)(2,1)S(1)}, u32[]{:S(2)}, u32[]{:S(2)}) collective-permute-start(bf16[2,64,640]{2,1,0:T(8,128)(2,1)S(1)} %get-tuple-element.336), channel_id=1, source_target_pairs={{0,1},{1,2},{2,3},{3,4},{4,5},{5,6},{6,7},{7,8},{8,9},{9,10},{10,1... | collective-permute-start | bytes 491528 | tf_op jit(solution)/shard_map/ppermute | solution.py:316
  151.2 10.8 %collective-permute-start = (bf16[256,640]{1,0:T(8,128)(2,1)S(1)}, bf16[256,640]{1,0:T(8,128)(2,1)S(1)}, u32[]{:S(2)}, u32[]{:S(2)}) collective-permute-start(bf16[256,640]{1,0:T(8,128)(2,1)S(1)} %param.1), channel_id=1, source_target_pairs={{0,32},{16,48},{32,64},{48,80},{64,96},{80,112},{1,33},{17,49},{33... | collective-permute-start | bytes 983048 | tf_op jit(solution)/shard_map/while/body/eval_jaxpr/cond/branch_1_fun/ppermute | solution.py:334
  197.9 9.0 %collective-permute-start = (bf16[256,640]{1,0:T(8,128)(2,1)S(1)}, bf16[256,640]{1,0:T(8,128)(2,1)S(1)}, u32[]{:S(2)}, u32[]{:S(2)}) collective-permute-start(bf16[256,640]{1,0:T(8,128)(2,1)S(1)} %param.1), channel_id=1, source_target_pairs={{0,32},{16,48},{32,64},{48,80},{64,96},{80,112},{1,33},{17,49},{33... | collective-permute-start | bytes 983048 | tf_op jit(solution)/shard_map/while/body/eval_jaxpr/cond/branch_1_fun/ppermute | solution.py:334
  242.8 9.0 %collective-permute-start = (bf16[256,640]{1,0:T(8,128)(2,1)S(1)}, bf16[256,640]{1,0:T(8,128)(2,1)S(1)}, u32[]{:S(2)}, u32[]{:S(2)}) collective-permute-start(bf16[256,640]{1,0:T(8,128)(2,1)S(1)} %param.1), channel_id=1, source_target_pairs={{0,32},{16,48},{32,64},{48,80},{64,96},{80,112},{1,33},{17,49},{33... | collective-permute-start | bytes 983048 | tf_op jit(solution)/shard_map/while/body/eval_jaxpr/cond/branch_1_fun/ppermute | solution.py:334
  287.8 20.7 %copy-start.1 = (bf16[2,4,64,640]{3,2,1,0:T(8,128)(2,1)S(1)}, bf16[2,4,64,640]{3,2,1,0:T(8,128)(2,1)}, u32[]{:S(2)}) copy-start(bf16[2,4,64,640]{3,2,1,0:T(8,128)(2,1)} %param.14) | copy-start | bytes 1966084
  287.9 9.9 %collective-permute-start.20 = (bf16[4,4,8,640]{3,2,0,1:T(8,128)(2,1)S(1)}, bf16[4,4,8,640]{3,2,0,1:T(8,128)(2,1)S(1)}, u32[]{:S(2)}, u32[]{:S(2)}) collective-permute-start(bf16[4,4,8,640]{3,2,0,1:T(8,128)(2,1)S(1)} %bitcast.91), channel_id=1, source_target_pairs={{0,16},{16,0},{32,48},{48,32},{64,80},{80,64},{96,112},{112,96},{1... | collective-permute-start | bytes 491528 | tf_op jit(solution)/shard_map/ppermute | solution.py:298
  297.9 2.7 collective-permute-start.21
  298.6 2.0 collective-permute-start.23
  299.3 8.6 %collective-permute-start.22 = (bf16[2,4,8,640]{3,2,1,0:T(8,128)(2,1)S(1)}, bf16[2,4,8,640]{3,2,1,0:T(8,128)(2,1)S(1)}, u32[]{:S(2)}, u32[]{:S(2)}) collective-permute-start(bf16[2,4,8,640]{3,2,1,0:T(8,128)(2,1)S(1)} %get-tuple-element.330), channel_id=1, source_target_pairs={{96,32},{112,48},{97,33},{113,49},{98,34},{114,50},{99,35},{115,51... | collective-permute-start | bytes 245768 | tf_op jit(solution)/shard_map/ppermute | solution.py:347
where the time goes:
time: 311 us; the launch traced here: 309 us
  Pallas kernels  177 us (57%)
  waiting for transfers between devices  79.1 us (25%)
  starting transfers between devices  44 us (14%)
  other arithmetic  5.11 us (2%)
    pallas_call x4, Pallas kernels, block_call(): pl.pallas_call(block_kernel, out_shape=jax.ShapeDtypeStruct((CELLS, C), B...  143 us
    ppermute x8, waiting for transfers between devices, turned(): return lax.ppermute(value, ('segment', 'patch'), pairs)  40.4 us
    pallas_call x3, Pallas kernels, stale_call(): pl.pallas_call(functools.partial(stale_kernel, count), grid=(2, count, st...  33.5 us
    ppermute x3, waiting for transfers between devices, hop(): return lax.ppermute(x, 'segment', [(i, i + 2) for i in range(6)])  18.5 us
    ppermute x10, waiting for transfers between devices, swap(): return lax.ppermute(value, 'segment', sibling)  13 us
    ppermute x8, starting transfers between devices, turned(): return lax.ppermute(value, ('segment', 'patch'), pairs)  12.2 us
    ppermute x10, starting transfers between devices, swap(): return lax.ppermute(value, 'segment', sibling)  10.9 us
    ppermute x3, starting transfers between devices, hop(): return lax.ppermute(x, 'segment', [(i, i + 2) for i in range(6)])  10.2 us
  transfers between devices with their start and end apart: 26, of which 12 were waited for; matrix products, arithmetic and copies ran while one was open for 2% of the time, Pallas kernels for 11%

commit v1 on v0

--- a/solution.py
+++ b/solution.py
@@ -59,8 +59,9 @@
         kv_ref[part] = out[:, part * 128 : (part + 1) * 128]
 
 
-def stale_call(pieces, gains, wkv, patches=2):
+def stale_call(pieces, gains, wkv):
     count, size = len(pieces), pieces[0].shape[0]
+    patches = min(size, 4)
     steps = size // patches
 
     def piece_spec(i):
@@ -139,10 +140,6 @@
         return copies
 
     start(0, "query", "key", "value")
-    for pair in range(PAIRS):
-        for copy in pair_copies(0, pair):
-            copy.start()
-    start(0, "out", "conv")
     mid[...] = x_ref[...].astype(F32)
     lane = lax.broadcasted_iota(jnp.int32, (CELLS, 128), 1)
     own_cells = pl.ds(0, CELLS)
@@ -154,6 +151,14 @@
         normed = normalize(mid[...], ga_ref[pl.ds(place, 1), :]).astype(BF)
         for name in NAMES[:3]:
             wait(name)
+
+        @pl.when(place == 0)
+        def _():
+            for pair in range(PAIRS):
+                for copy in pair_copies(0, pair):
+                    copy.start()
+            start(0, "out", "conv")
+
         made = dot(normed, wqkv[...])
         for pair in range(PAIRS):
             queries[pair] = (made[:, pair * 128 : (pair + 1) * 128] * QSCALE).astype(BF)
@@ -305,27 +310,40 @@
         give = lax.dynamic_index_in_dim(value, 1 - core, 0, keepdims=False)
         return ordered(keep, swap(give))
 
-    raw = jnp.stack(exchanged(stale_attn[0].reshape(2, CELLS, C)))
+    own = dict(zip(NAMES, (query_w[0], key_w[0], value_w[0], out_w[0], conv_w[0].reshape(9, C, C))))
+    mine = jnp.concatenate(
+        [stale_attn[0].reshape(2, CELLS, C), stale_edge[0].reshape(2, 2 * W, C)], 1
+    )
+    mine = jnp.stack(exchanged(mine))
+    raw, edges = mine[:, :CELLS], mine[:, CELLS:].reshape(2, 2, W, C)
+    raw, first_sent, norm_attn = lax.optimization_barrier(
+        (raw, {name: own[name] for name in ("key", "value")}, norm_attn)
+    )
+    other = {name: swap(value) for name, value in first_sent.items()}
+    gains = jnp.concatenate(ordered(norm_attn, swap(norm_attn)), 0)
+    wkv = jnp.stack(
+        ordered(*[jnp.concatenate([w["key"], w["value"]], 1) for w in (own, other)])
+    )
     back, ahead = ring_near(raw, 0)
     far = ring_far(back, ahead, 0)
     row = jnp.stack([raw, back, jnp.concatenate(far, 0), ahead])
+    row, sent, edges, norm_conv = lax.optimization_barrier(
+        (row, {name: own[name] for name in ("query", "out", "conv")}, edges, norm_conv)
+    )
     back, ahead = ring_near(row, 1)
-    far = ring_far(back, ahead, 1)
-
-    edges = jnp.stack(exchanged(stale_edge[0]))
     upper = lax.ppermute(edges[:, 1], "patch", [(i, i + 1) for i in range(15)])
     lower = lax.ppermute(edges[:, 0], "patch", [(i + 1, i) for i in range(15)])
-
-    own = dict(zip(NAMES, (query_w[0], key_w[0], value_w[0], out_w[0], conv_w[0].reshape(9, C, C))))
-    other = {name: swap(own[name]) for name in ("key", "value", "query", "out", "conv")}
-    gains = jnp.concatenate(ordered(norm_attn, swap(norm_attn)), 0)
+    stored = stale_call([row], gains, wkv)
+    back, ahead, upper, lower, stored = lax.optimization_barrier(
+        (back, ahead, upper, lower, stored)
+    )
+    far = ring_far(back, ahead, 1)
+
+    other |= {name: swap(value) for name, value in sent.items()}
     conv_gains = jnp.concatenate(ordered(norm_conv, swap(norm_conv)), 0)
 
     x = lax.dynamic_index_in_dim(latent, core, 0, keepdims=False).reshape(CELLS, C)
-    wkv = jnp.stack(
-        ordered(*[jnp.concatenate([w["key"], w["value"]], 1) for w in (own, other)])
-    )
-    stored = [stale_call(pieces, gains, wkv) for pieces in ([row], [back, ahead], far)]
+    stored = [stored] + [stale_call(pieces, gains, wkv) for pieces in ([back, ahead], far)]
 
     def two_blocks(x):
         return block_call(x, gains, conv_gains, upper, lower, own, other, stored)

time: 311 us -> 292 us (0.939)
  waiting for transfers between devices: 79.1 us -> 61.2 us
  starting transfers between devices: 44 us -> 35.3 us
  Pallas kernels: 177 us -> 181 us
    ppermute x8, waiting for transfers between devices: 40.4 us -> 14 us  [turned(): return lax.ppermute(value, ('segment', 'patch'), pairs)]
    ppermute x10 -> x9, starting transfers between devices: 10.9 us -> 2.69 us  [swap(): return lax.ppermute(value, 'segment', sibling)]
    pallas_call x4, Pallas kernels: 143 us -> 149 us  [block_call(): pl.pallas_call(block_kernel, out_shape=jax.ShapeDtypeStruct((CELLS, C), B...]
    ppermute x1, waiting for transfers between devices: 0.01 us -> 4.47 us  [shards(): upper = lax.ppermute(edges[:, 1], 'patch', [(i, i + 1) for i in range(15)])]
    ppermute x3, waiting for transfers between devices: 18.5 us -> 22.5 us  [hop(): return lax.ppermute(x, 'segment', [(i, i + 2) for i in range(6)])]
    ppermute x10 -> x9, waiting for transfers between devices: 13 us -> 13.8 us  [swap(): return lax.ppermute(value, 'segment', sibling)]
  transfers between devices with their start and end apart: 26 -> 25, of which waited for: 12 -> 14; matrix products, arithmetic and copies ran while one was open for 2% -> 2% of each run, Pallas kernels for 11% -> 11%
where the time goes in v1:
time: 292 us; the launch traced here: 288 us
  Pallas kernels  181 us (62%)
  waiting for transfers between devices  61.2 us (21%)
  starting transfers between devices  35.3 us (12%)
  other arithmetic  6.64 us (2%)
  local copies, waits for them, and re-layouts  3.34 us (1%)
    pallas_call x4, Pallas kernels, block_call(): pl.pallas_call(block_kernel, out_shape=jax.ShapeDtypeStruct((CELLS, C), B...  149 us
    pallas_call x3, Pallas kernels, stale_call(): pl.pallas_call(functools.partial(stale_kernel, count), grid=(2, count, st...  32.4 us
    ppermute x3, waiting for transfers between devices, hop(): return lax.ppermute(x, 'segment', [(i, i + 2) for i in range(6)])  22.5 us
    ppermute x8, waiting for transfers between devices, turned(): return lax.ppermute(value, ('segment', 'patch'), pairs)  14 us
    ppermute x9, waiting for transfers between devices, swap(): return lax.ppermute(value, 'segment', sibling)  13.8 us
    ppermute x8, starting transfers between devices, turned(): return lax.ppermute(value, ('segment', 'patch'), pairs)  11.8 us
    ppermute x3, starting transfers between devices, hop(): return lax.ppermute(x, 'segment', [(i, i + 2) for i in range(6)])  10.2 us
    ppermute x3, waiting for transfers between devices, shards(): lax.ppermute(both[:, :, (3 + d) % 4], 'segment', [(6, (6 + 2 * d) % 8), (...  6.43 us
  transfers between devices with their start and end apart: 25, of which 14 were waited for; matrix products, arithmetic and copies ran while one was open for 2% of the time, Pallas kernels for 11%

profile of v1, /device:TPU:18, one launch (start us, length us, event | category | flops | bytes accessed | tf_op | source)
XLA Modules:
  0.0 288.4 jit_solution(15513530593595124967)
XLA Ops:
  0.0 1.1 fusion.2
  1.1 0.1 collective-permute-start.1
  1.2 1.8 collective-permute-done.1
  3.1 1.5 select_bitcast_fusion
  4.6 0.1 fusion
  4.7 2.0 collective-permute-start.3
  6.7 2.2 collective-permute-start.5
  8.9 8.5 %collective-permute-done.3 = bf16[2,256,640]{2,1,0:T(8,128)(2,1)S(1)} collective-permute-done((bf16[2,256,640]{2,1,0:T(8,128)(2,1)S(1)}, bf16[2,256,640]{2,1,0:T(8,128)(2,1)S(1)}, u32[]{:S(2)}, u32[]{:S(2)}) %collective-permute-start.3) | collective-permute-done | bytes 655392 | tf_op jit(solution)/shard_map/ppermute | solution.py:283
  17.4 0.1 collective-permute-start.4
  17.5 3.3 %collective-permute-start.6 = (bf16[1,256,640]{2,1,0:T(8,128)(2,1)S(1)}, bf16[1,256,640]{2,1,0:T(8,128)(2,1)S(1)}, u32[]{:S(2)}, u32[]{:S(2)}) collective-permute-start(bf16[1,256,640]{2,1,0:T(8,128)(2,1)S(1)} %slice.51), channel_id=1, source_target_pairs={{0,3},{1,0},{2,1},{3,2},{4,7},{5,4},{6,5},{7,6},{8,11},{9,8},{10,9... | collective-permute-start | bytes 983048 | tf_op jit(solution)/shard_map/ppermute | solution.py:283
  20.8 4.9 %collective-permute-done.4 = bf16[1,256,640]{2,1,0:T(8,128)(2,1)S(1)} collective-permute-done((bf16[1,256,640]{2,1,0:T(8,128)(2,1)S(1)}, bf16[1,256,640]{2,1,0:T(8,128)(2,1)S(1)}, u32[]{:S(2)}, u32[]{:S(2)}) %collective-permute-start.4) | collective-permute-done | bytes 327712 | tf_op jit(solution)/shard_map/ppermute | solution.py:283
  25.7 0.1 maximum_bitcast_fusion
  25.8 0.0 copy-start.5
  25.8 0.4 pad_maximum_fusion.1.refs_0_
  26.2 0.1 collective-permute-start.16
  26.3 1.4 collective-permute-start.8
  27.7 0.7 collective-permute-start.9
  28.4 1.5 collective-permute-start.2
  29.9 0.1 collective-permute-start.12
  30.0 8.0 %collective-permute-done.2 = f32[1,640]{1,0:T(1,128)S(1)} collective-permute-done((f32[1,640]{1,0:T(1,128)S(1)}, f32[1,640]{1,0:T(1,128)S(1)}, u32[]{:S(2)}, u32[]{:S(2)}) %collective-permute-start.2) | collective-permute-done | bytes 2592 | tf_op jit(solution)/shard_map/ppermute | solution.py:303
  38.0 0.1 collective-permute-start.13
  38.2 0.1 constant_dynamic-update-slice_fusion.1
  38.2 0.1 constant_dynamic-update-slice_fusion
  38.4 0.8 collective-permute-done.12
  39.2 1.2 collective-permute-done.13
  40.4 0.6 broadcast_select_fusion.1
  41.0 0.2 copy-done.4
  41.3 2.0 pad_maximum_fusion.refs_2_.refs_3_
  43.3 2.6 collective-permute-start.10
  45.9 5.3 %collective-permute-start.11 = (bf16[2,64,640]{2,1,0:T(8,128)(2,1)S(1)}, bf16[2,64,640]{2,1,0:T(8,128)(2,1)S(1)}, u32[]{:S(2)}, u32[]{:S(2)}) collective-permute-start(bf16[2,64,640]{2,1,0:T(8,128)(2,1)S(1)} %get-tuple-element.361), channel_id=1, source_target_pairs={{1,0},{2,1},{3,2},{4,3},{5,4},{6,5},{7,6},{8,7},{9,8},{10,9},{11,1... | collective-permute-start | bytes 491528 | tf_op jit(solution)/shard_map/ppermute | solution.py:335
  51.3 8.6 %stale_4.2 = bf16[2,10,1024,128]{3,2,1,0:T(8,128)(2,1)} custom-call(bf16[4,2,256,640]{3,2,1,0:T(8,128)(2,1)S(1)} %pad_maximum_fusion.1.refs_0_, f32[2,640]{1,0:T(2,128)S(1)} %pad_maximum_fusion.5.refs_1_.refs_2_, bf16[2,640,1280]{2,1,0:T(8,128)(2,1)} %pad_maximum_fusion.refs_2_.refs_3_), custom_call_target="tpu_custom_call" | custom-call | flops 3355443200 | bytes 7864320 | tf_op jit(solution)/shard_map/stale_4/pallas_call | solution.py:73
  59.9 4.5 %collective-permute-done.10 = bf16[2,64,640]{2,1,0:T(8,128)(2,1)S(1)} collective-permute-done((bf16[2,64,640]{2,1,0:T(8,128)(2,1)S(1)}, bf16[2,64,640]{2,1,0:T(8,128)(2,1)S(1)}, u32[]{:S(2)}, u32[]{:S(2)}) %collective-permute-start.10) | collective-permute-done | bytes 163872 | tf_op jit(solution)/shard_map/ppermute | solution.py:334
  64.4 0.1 slice.42
  64.5 1.4 collective-permute-start.17
  65.8 1.4 slice.43
  67.3 0.8 collective-permute-start.18
  68.2 0.6 collective-permute-start.14
  68.8 0.5 collective-permute-done.7
  69.3 0.2 collective-permute-start.15
  69.5 14.9 %stale_8.1 = bf16[2,10,2048,128]{3,2,1,0:T(8,128)(2,1)} custom-call(bf16[4,2,256,640]{3,2,1,0:T(8,128)(2,1)S(1)} %collective-permute-done.8.refs_0_, bf16[4,2,256,640]{3,2,1,0:T(8,128)(2,1)} %collective-permute-done.9.refs_1_, f32[2,640]{1,0:T(2,128)S(1)} %pad_maximum_fusion.5.refs_1_.refs_2_, bf16[2,640,1280]{2,1,0:T(8,128)(2,1)} %pad_maximum_fusion.refs_2_.refs_3_), custom_call_target="tpu_custom_call" | custom-call | flops 6710886400 | bytes 15728640 | tf_op jit(solution)/shard_map/stale_8/pallas_call | solution.py:73
  84.3 0.6 collective-permute-done.18.refs_1_
  85.0 9.0 %stale_4.3 = bf16[2,10,1024,128]{3,2,1,0:T(8,128)(2,1)} custom-call(bf16[2,2,256,640]{3,2,1,0:T(8,128)(2,1)S(1)} %collective-permute-done.17.refs_0_, bf16[2,2,256,640]{3,2,1,0:T(8,128)(2,1)S(1)} %collective-permute-done.18.refs_1_, f32[2,640]{1,0:T(2,128)S(1)} %pad_maximum_fusion.5.refs_1_.refs_2_, bf16[2,640,1280]{2,1,0:T(8,128)(2,1)} %pad_maximum_fusion.refs_2_.refs_3_), custom_call_target="tpu_custom_call" | custom-call | flops 3355443200 | bytes 7864320 | tf_op jit(solution)/shard_map/stale_4/pallas_call | solution.py:73
  94.0 0.9 copy-done.9
  94.9 182.1 %while.13 = (s32[]{:T(128)}, bf16[256,640]{1,0:T(8,128)(2,1)S(1)}, f32[2,640]{1,0:T(2,128)S(1)}, f32[2,640]{1,0:T(2,128)S(1)}, bf16[2,64,640]{2,1,0:T(8,128)(2,1...) while((s32[]{:T(128)}, bf16[256,640]{1,0:T(8,128)(2,1)S(1)}, ...), condition=%wide.region_3.4_spmd, body=%wide.region_0.3_spmd.sunk | while | flops 25999998976 | bytes 46621688 | solution.py:357
  94.9 37.2 %blocks.5 = bf16[256,640]{1,0:T(8,128)(2,1)S(1)} custom-call(bf16[256,640]{1,0:T(8,128)(2,1)S(1)} %get-tuple-element.504.refs_0_, f32[2,640]{1,0:T(2,128)S(1)} %get-tuple-element.526.refs_1_, f32[2,640]{1,0:T(2,128)S(1)} %get-tuple-element.527.refs_2_, bf16[2,64,640]{2,1,0:T(8,128)(2,1)S(1)} %get-tuple-element.528.refs_3_, ...), custom_call_target="tpu_custom_call" | custom-call | flops 25999998976 | bytes 44000000 | tf_op jit(solution)/shard_map/while/body/eval_jaxpr/blocks/pallas_call | solution.py:236
  132.1 11.6 %conditional.2 = (bf16[256,640]{1,0:T(8,128)(2,1)S(1)}) conditional(s32[]{:T(128)} %convert_element_type.13, bf16[256,640]{1,0:T(8,128)(2,1)S(1)} %blocks.5, bf16[256,640]{1,0:T(8,128)(2,1)S(1)} %blocks.5), branch_computations={%region_1.1_spmd, %region_2.2_spmd} | conditional | bytes 1966128 | solution.py:355
  132.1 3.4 %collective-permute-start = (bf16[256,640]{1,0:T(8,128)(2,1)S(1)}, bf16[256,640]{1,0:T(8,128)(2,1)S(1)}, u32[]{:S(2)}, u32[]{:S(2)}) collective-permute-start(bf16[256,640]{1,0:T(8,128)(2,1)S(1)} %param.1), channel_id=1, source_target_pairs={{0,32},{16,48},{32,64},{48,80},{64,96},{80,112},{1,33},{17,49},{33... | collective-permute-start | bytes 983048 | tf_op jit(solution)/shard_map/while/body/eval_jaxpr/cond/branch_1_fun/ppermute | solution.py:352
  135.5 8.1 %collective-permute-done = bf16[256,640]{1,0:T(8,128)(2,1)S(1)} collective-permute-done((bf16[256,640]{1,0:T(8,128)(2,1)S(1)}, bf16[256,640]{1,0:T(8,128)(2,1)S(1)}, u32[]{:S(2)}, u32[]{:S(2)}) %collective-permute-start) | collective-permute-done | bytes 327712 | tf_op jit(solution)/shard_map/while/body/eval_jaxpr/cond/branch_1_fun/ppermute | solution.py:352
  143.7 37.3 %blocks.5 = bf16[256,640]{1,0:T(8,128)(2,1)S(1)} custom-call(bf16[256,640]{1,0:T(8,128)(2,1)S(1)} %get-tuple-element.504.refs_0_, f32[2,640]{1,0:T(2,128)S(1)} %get-tuple-element.526.refs_1_, f32[2,640]{1,0:T(2,128)S(1)} %get-tuple-element.527.refs_2_, bf16[2,64,640]{2,1,0:T(8,128)(2,1)S(1)} %get-tuple-element.528.refs_3_, ...), custom_call_target="tpu_custom_call" | custom-call | flops 25999998976 | bytes 44000000 | tf_op jit(solution)/shard_map/while/body/eval_jaxpr/blocks/pallas_call | solution.py:236
  181.0 11.0 %conditional.2 = (bf16[256,640]{1,0:T(8,128)(2,1)S(1)}) conditional(s32[]{:T(128)} %convert_element_type.13, bf16[256,640]{1,0:T(8,128)(2,1)S(1)} %blocks.5, bf16[256,640]{1,0:T(8,128)(2,1)S(1)} %blocks.5), branch_computations={%region_1.1_spmd, %region_2.2_spmd} | conditional | bytes 1966128 | solution.py:355
  181.0 3.4 %collective-permute-start = (bf16[256,640]{1,0:T(8,128)(2,1)S(1)}, bf16[256,640]{1,0:T(8,128)(2,1)S(1)}, u32[]{:S(2)}, u32[]{:S(2)}) collective-permute-start(bf16[256,640]{1,0:T(8,128)(2,1)S(1)} %param.1), channel_id=1, source_target_pairs={{0,32},{16,48},{32,64},{48,80},{64,96},{80,112},{1,33},{17,49},{33... | collective-permute-start | bytes 983048 | tf_op jit(solution)/shard_map/while/body/eval_jaxpr/cond/branch_1_fun/ppermute | solution.py:352
  184.4 7.5 %collective-permute-done = bf16[256,640]{1,0:T(8,128)(2,1)S(1)} collective-permute-done((bf16[256,640]{1,0:T(8,128)(2,1)S(1)}, bf16[256,640]{1,0:T(8,128)(2,1)S(1)}, u32[]{:S(2)}, u32[]{:S(2)}) %collective-permute-start) | collective-permute-done | bytes 327712 | tf_op jit(solution)/shard_map/while/body/eval_jaxpr/cond/branch_1_fun/ppermute | solution.py:352
  192.0 37.3 %blocks.5 = bf16[256,640]{1,0:T(8,128)(2,1)S(1)} custom-call(bf16[256,640]{1,0:T(8,128)(2,1)S(1)} %get-tuple-element.504.refs_0_, f32[2,640]{1,0:T(2,128)S(1)} %get-tuple-element.526.refs_1_, f32[2,640]{1,0:T(2,128)S(1)} %get-tuple-element.527.refs_2_, bf16[2,64,640]{2,1,0:T(8,128)(2,1)S(1)} %get-tuple-element.528.refs_3_, ...), custom_call_target="tpu_custom_call" | custom-call | flops 25999998976 | bytes 44000000 | tf_op jit(solution)/shard_map/while/body/eval_jaxpr/blocks/pallas_call | solution.py:236
  229.3 10.3 %conditional.2 = (bf16[256,640]{1,0:T(8,128)(2,1)S(1)}) conditional(s32[]{:T(128)} %convert_element_type.13, bf16[256,640]{1,0:T(8,128)(2,1)S(1)} %blocks.5, bf16[256,640]{1,0:T(8,128)(2,1)S(1)} %blocks.5), branch_computations={%region_1.1_spmd, %region_2.2_spmd} | conditional | bytes 1966128 | solution.py:355
  229.3 3.4 %collective-permute-start = (bf16[256,640]{1,0:T(8,128)(2,1)S(1)}, bf16[256,640]{1,0:T(8,128)(2,1)S(1)}, u32[]{:S(2)}, u32[]{:S(2)}) collective-permute-start(bf16[256,640]{1,0:T(8,128)(2,1)S(1)} %param.1), channel_id=1, source_target_pairs={{0,32},{16,48},{32,64},{48,80},{64,96},{80,112},{1,33},{17,49},{33... | collective-permute-start | bytes 983048 | tf_op jit(solution)/shard_map/while/body/eval_jaxpr/cond/branch_1_fun/ppermute | solution.py:352
  232.7 6.9 %collective-permute-done = bf16[256,640]{1,0:T(8,128)(2,1)S(1)} collective-permute-done((bf16[256,640]{1,0:T(8,128)(2,1)S(1)}, bf16[256,640]{1,0:T(8,128)(2,1)S(1)}, u32[]{:S(2)}, u32[]{:S(2)}) %collective-permute-start) | collective-permute-done | bytes 327712 | tf_op jit(solution)/shard_map/while/body/eval_jaxpr/cond/branch_1_fun/ppermute | solution.py:352
  239.7 37.3 %blocks.5 = bf16[256,640]{1,0:T(8,128)(2,1)S(1)} custom-call(bf16[256,640]{1,0:T(8,128)(2,1)S(1)} %get-tuple-element.504.refs_0_, f32[2,640]{1,0:T(2,128)S(1)} %get-tuple-element.526.refs_1_, f32[2,640]{1,0:T(2,128)S(1)} %get-tuple-element.527.refs_2_, bf16[2,64,640]{2,1,0:T(8,128)(2,1)S(1)} %get-tuple-element.528.refs_3_, ...), custom_call_target="tpu_custom_call" | custom-call | flops 25999998976 | bytes 44000000 | tf_op jit(solution)/shard_map/while/body/eval_jaxpr/blocks/pallas_call | solution.py:236
  277.1 0.1 collective-permute-start.19
  277.2 1.4 collective-permute-done.19
  278.6 0.7 collective-permute-start.20
  279.3 1.3 collective-permute-start.21
  280.6 0.7 collective-permute-start.22
  281.3 6.4 %collective-permute-done.21 = bf16[2,4,8,640]{3,2,1,0:T(8,128)(2,1)S(1)} collective-permute-done((bf16[2,4,8,640]{3,2,1,0:T(8,128)(2,1)S(1)}, bf16[2,4,8,640]{3,2,1,0:T(8,128)(2,1)S(1)}, u32[]{:S(2)}, u32[]{:S(2)}) %collective-permute-start.21) | collective-permute-done | bytes 81952 | tf_op jit(solution)/shard_map/ppermute | solution.py:365
  287.7 0.7 fusion.13
  (56 shorter events, 0.6 us)
Async XLA Ops:
  0.0 68.1 %copy-start = (bf16[2,4,64,640]{3,2,1,0:T(8,128)(2,1)S(1)}, bf16[2,4,64,640]{3,2,1,0:T(8,128)(2,1)}, u32[]{:S(2)}) copy-start(bf16[2,4,64,640]{3,2,1,0:T(8,128)(2,1)} %param.14) | copy-start | bytes 1966084
  1.1 1.9 collective-permute-start.1
  4.7 12.7 %collective-permute-start.3 = (bf16[2,256,640]{2,1,0:T(8,128)(2,1)S(1)}, bf16[2,256,640]{2,1,0:T(8,128)(2,1)S(1)}, u32[]{:S(2)}, u32[]{:S(2)}) collective-permute-start(bf16[2,256,640]{2,1,0:T(8,128)(2,1)S(1)} %fusion), channel_id=1, source_target_pairs={{0,1},{1,2},{2,3},{3,0},{4,5},{5,6},{6,7},{7,4},{8,9},{9,10},{10,1... | collective-permute-start | bytes 1966088 | tf_op jit(solution)/shard_map/ppermute | solution.py:283
  6.7 10.8 %collective-permute-start.5 = (bf16[2,256,640]{2,1,0:T(8,128)(2,1)S(1)}, bf16[2,256,640]{2,1,0:T(8,128)(2,1)S(1)}, u32[]{:S(2)}, u32[]{:S(2)}) collective-permute-start(bf16[2,256,640]{2,1,0:T(8,128)(2,1)S(1)} %fusion), channel_id=1, source_target_pairs={{0,3},{1,0},{2,1},{3,2},{4,7},{5,4},{6,5},{7,6},{8,11},{9,8},{10,9... | collective-permute-start | bytes 1966088 | tf_op jit(solution)/shard_map/ppermute | solution.py:283
  17.4 8.4 %collective-permute-start.4 = (bf16[1,256,640]{2,1,0:T(8,128)(2,1)S(1)}, bf16[1,256,640]{2,1,0:T(8,128)(2,1)S(1)}, u32[]{:S(2)}, u32[]{:S(2)}) collective-permute-start(bf16[1,256,640]{2,1,0:T(8,128)(2,1)S(1)} %slice.50), channel_id=1, source_target_pairs={{0,1},{1,2},{2,3},{3,0},{4,5},{5,6},{6,7},{7,4},{8,9},{9,10},{10,1... | collective-permute-start | bytes 983048 | tf_op jit(solution)/shard_map/ppermute | solution.py:283
  17.5 8.2 %collective-permute-start.6 = (bf16[1,256,640]{2,1,0:T(8,128)(2,1)S(1)}, bf16[1,256,640]{2,1,0:T(8,128)(2,1)S(1)}, u32[]{:S(2)}, u32[]{:S(2)}) collective-permute-start(bf16[1,256,640]{2,1,0:T(8,128)(2,1)S(1)} %slice.51), channel_id=1, source_target_pairs={{0,3},{1,0},{2,1},{3,2},{4,7},{5,4},{6,5},{7,6},{8,11},{9,8},{10,9... | collective-permute-start | bytes 983048 | tf_op jit(solution)/shard_map/ppermute | solution.py:283
  25.8 2.6 copy-start.5
  25.8 4.1 %copy-start.2 = (bf16[1,640,640]{2,1,0:T(8,128)(2,1)S(1)}, bf16[1,640,640]{2,1,0:T(8,128)(2,1)}, u32[]{:S(2)}) copy-start(bf16[1,640,640]{2,1,0:T(8,128)(2,1)} %param.19) | copy-start | bytes 2457604
  25.8 12.2 %copy-start.3 = (bf16[1,640,640]{2,1,0:T(8,128)(2,1)S(1)}, bf16[1,640,640]{2,1,0:T(8,128)(2,1)}, u32[]{:S(2)}) copy-start(bf16[1,640,640]{2,1,0:T(8,128)(2,1)} %param.20) | copy-start | bytes 2457604
  26.2 67.7 %collective-permute-start.16 = (bf16[9,640,640]{2,1,0:T(8,128)(2,1)}, bf16[9,640,640]{2,1,0:T(8,128)(2,1)}, u32[]{:S(2)}, u32[]{:S(2)}) collective-permute-start(bf16[9,640,640]{2,1,0:T(8,128)(2,1)} %bitcast.13), channel_id=1, source_target_pairs={{0,16},{16,0},{32,48},{48,32},{64,80},{80,64},{96,112},{112,96},{1... | collective-permute-start | bytes 22118408 | tf_op jit(solution)/shard_map/ppermute | solution.py:303
  26.3 38.0 %collective-permute-start.8 = (bf16[4,2,256,640]{3,2,1,0:T(8,128)(2,1)S(1)}, bf16[4,2,256,640]{3,2,1,0:T(8,128)(2,1)S(1)}, u32[]{:S(2)}, u32[]{:S(2)}) collective-permute-start(bf16[4,2,256,640]{3,2,1,0:T(8,128)(2,1)S(1)} %pad_maximum_fusion.1.refs_0_), channel_id=1, source_target_pairs={{0,4},{1,5},{2,6},{3,7},{4,8},{5,9},{6,10},{7,11},{8,12},{9,13},{1... | collective-permute-start | bytes 7864328 | tf_op jit(solution)/shard_map/ppermute | solution.py:283
  27.7 36.7 %collective-permute-start.9 = (bf16[4,2,256,640]{3,2,1,0:T(8,128)(2,1)S(1)}, bf16[4,2,256,640]{3,2,1,0:T(8,128)(2,1)}, u32[]{:S(2)}, u32[]{:S(2)}) collective-permute-start(bf16[4,2,256,640]{3,2,1,0:T(8,128)(2,1)S(1)} %pad_maximum_fusion.1.refs_0_), channel_id=1, source_target_pairs={{0,12},{1,13},{2,14},{3,15},{4,0},{5,1},{6,2},{7,3},{8,4},{9,5},{1... | collective-permute-start | bytes 7864328 | tf_op jit(solution)/shard_map/ppermute | solution.py:283
  28.4 9.6 %collective-permute-start.2 = (f32[1,640]{1,0:T(1,128)S(1)}, f32[1,640]{1,0:T(1,128)S(1)}, u32[]{:S(2)}, u32[]{:S(2)}) collective-permute-start(f32[1,640]{1,0:T(1,128)S(1)} %copy-done.5), channel_id=1, source_target_pairs={{0,16},{16,0},{32,48},{48,32},{64,80},{80,64},{96,112},{112,96},{1... | collective-permute-start | bytes 7688 | tf_op jit(solution)/shard_map/ppermute | solution.py:303
  29.9 9.3 %collective-permute-start.12 = (bf16[640,640]{1,0:T(8,128)(2,1)S(1)}, bf16[640,640]{1,0:T(8,128)(2,1)S(1)}, u32[]{:S(2)}, u32[]{:S(2)}) collective-permute-start(bf16[640,640]{1,0:T(8,128)(2,1)S(1)} %bitcast.74), channel_id=1, source_target_pairs={{0,16},{16,0},{32,48},{48,32},{64,80},{80,64},{96,112},{112,96},{1... | collective-permute-start | bytes 2457608 | tf_op jit(solution)/shard_map/ppermute | solution.py:303
  38.0 2.3 collective-permute-start.13
  40.4 0.9 copy-start.4
  43.3 21.0 %collective-permute-start.10 = (bf16[2,64,640]{2,1,0:T(8,128)(2,1)S(1)}, bf16[2,64,640]{2,1,0:T(8,128)(2,1)S(1)}, u32[]{:S(2)}, u32[]{:S(2)}) collective-permute-start(bf16[2,64,640]{2,1,0:T(8,128)(2,1)S(1)} %get-tuple-element.362), channel_id=1, source_target_pairs={{0,1},{1,2},{2,3},{3,4},{4,5},{5,6},{6,7},{7,8},{8,9},{9,10},{10,1... | collective-permute-start | bytes 491528 | tf_op jit(solution)/shard_map/ppermute | solution.py:334
  45.9 18.4 %collective-permute-start.11 = (bf16[2,64,640]{2,1,0:T(8,128)(2,1)S(1)}, bf16[2,64,640]{2,1,0:T(8,128)(2,1)S(1)}, u32[]{:S(2)}, u32[]{:S(2)}) collective-permute-start(bf16[2,64,640]{2,1,0:T(8,128)(2,1)S(1)} %get-tuple-element.361), channel_id=1, source_target_pairs={{1,0},{2,1},{3,2},{4,3},{5,4},{6,5},{7,6},{8,7},{9,8},{10,9},{11,1... | collective-permute-start | bytes 491528 | tf_op jit(solution)/shard_map/ppermute | solution.py:335
  59.9 8.2 %copy-start.6 = (f32[1,640]{1,0:T(1,128)S(1)}, f32[1,640]{1,0:T(1,128)}, u32[]{:S(2)}) copy-start(f32[1,640]{1,0:T(1,128)} %param.22) | copy-start | bytes 7684
  59.9 8.3 %copy-start.7 = (bf16[1,640,640]{2,1,0:T(8,128)(2,1)S(1)}, bf16[1,640,640]{2,1,0:T(8,128)(2,1)}, u32[]{:S(2)}) copy-start(bf16[1,640,640]{2,1,0:T(8,128)(2,1)} %param.18) | copy-start | bytes 2457604
  59.9 9.4 %copy-start.8 = (bf16[1,640,640]{2,1,0:T(8,128)(2,1)S(1)}, bf16[1,640,640]{2,1,0:T(8,128)(2,1)}, u32[]{:S(2)}) copy-start(bf16[1,640,640]{2,1,0:T(8,128)(2,1)} %param.21) | copy-start | bytes 2457604
  64.3 2.9 %copy-start.10 = (bf16[2,64,640]{2,1,0:T(8,128)(2,1)}, bf16[2,64,640]{2,1,0:T(8,128)(2,1)S(1)}, u32[]{:S(2)}) copy-start(bf16[2,64,640]{2,1,0:T(8,128)(2,1)S(1)} %collective-permute-done.10) | copy-start | bytes 491524
  64.4 2.9 %copy-start.12 = (bf16[2,64,640]{2,1,0:T(8,128)(2,1)}, bf16[2,64,640]{2,1,0:T(8,128)(2,1)S(1)}, u32[]{:S(2)}) copy-start(bf16[2,64,640]{2,1,0:T(8,128)(2,1)S(1)} %collective-permute-done.11) | copy-start | bytes 491524
  64.5 19.9 %collective-permute-start.17 = (bf16[2,2,256,640]{3,2,1,0:T(8,128)(2,1)S(1)}, bf16[2,2,256,640]{3,2,1,0:T(8,128)(2,1)S(1)}, u32[]{:S(2)}, u32[]{:S(2)}) collective-permute-start(bf16[2,2,256,640]{3,2,1,0:T(8,128)(2,1)S(1)} %slice.42), channel_id=1, source_target_pairs={{0,4},{1,5},{2,6},{3,7},{4,8},{5,9},{6,10},{7,11},{8,12},{9,13},{1... | collective-permute-start | bytes 3932168 | tf_op jit(solution)/shard_map/ppermute | solution.py:283
  67.3 17.7 %collective-permute-start.18 = (bf16[2,2,256,640]{3,2,1,0:T(8,128)(2,1)S(1)}, bf16[2,2,256,640]{3,2,1,0:T(8,128)(2,1)S(1)}, u32[]{:S(2)}, u32[]{:S(2)}) collective-permute-start(bf16[2,2,256,640]{3,2,1,0:T(8,128)(2,1)S(1)} %slice.43), channel_id=1, source_target_pairs={{0,12},{1,13},{2,14},{3,15},{4,0},{5,1},{6,2},{7,3},{8,4},{9,5},{1... | collective-permute-start | bytes 3932168 | tf_op jit(solution)/shard_map/ppermute | solution.py:283
  68.1 1.2 collective-permute-start.7
  68.2 25.8 %collective-permute-start.14 = (bf16[640,640]{1,0:T(8,128)(2,1)S(1)}, bf16[640,640]{1,0:T(8,128)(2,1)S(1)}, u32[]{:S(2)}, u32[]{:S(2)}) collective-permute-start(bf16[640,640]{1,0:T(8,128)(2,1)S(1)} %bitcast.82), channel_id=1, source_target_pairs={{0,16},{16,0},{32,48},{48,32},{64,80},{80,64},{96,112},{112,96},{1... | collective-permute-start | bytes 2457608 | tf_op jit(solution)/shard_map/ppermute | solution.py:303
  69.3 24.7 %collective-permute-start.15 = (bf16[640,640]{1,0:T(8,128)(2,1)S(1)}, bf16[640,640]{1,0:T(8,128)(2,1)}, u32[]{:S(2)}, u32[]{:S(2)}) collective-permute-start(bf16[640,640]{1,0:T(8,128)(2,1)S(1)} %bitcast.84), channel_id=1, source_target_pairs={{0,16},{16,0},{32,48},{48,32},{64,80},{80,64},{96,112},{112,96},{1... | collective-permute-start | bytes 2457608 | tf_op jit(solution)/shard_map/ppermute | solution.py:303
  84.3 10.5 %copy-start.11 = (bf16[2,64,640]{2,1,0:T(8,128)(2,1)S(1)}, bf16[2,64,640]{2,1,0:T(8,128)(2,1)}, u32[]{:S(2)}) copy-start(bf16[2,64,640]{2,1,0:T(8,128)(2,1)} %copy-done.10) | copy-start | bytes 491524
  93.9 0.9 copy-start.9
  132.1 11.5 %collective-permute-start = (bf16[256,640]{1,0:T(8,128)(2,1)S(1)}, bf16[256,640]{1,0:T(8,128)(2,1)S(1)}, u32[]{:S(2)}, u32[]{:S(2)}) collective-permute-start(bf16[256,640]{1,0:T(8,128)(2,1)S(1)} %param.1), channel_id=1, source_target_pairs={{0,32},{16,48},{32,64},{48,80},{64,96},{80,112},{1,33},{17,49},{33... | collective-permute-start | bytes 983048 | tf_op jit(solution)/shard_map/while/body/eval_jaxpr/cond/branch_1_fun/ppermute | solution.py:352
  181.0 10.9 %collective-permute-start = (bf16[256,640]{1,0:T(8,128)(2,1)S(1)}, bf16[256,640]{1,0:T(8,128)(2,1)S(1)}, u32[]{:S(2)}, u32[]{:S(2)}) collective-permute-start(bf16[256,640]{1,0:T(8,128)(2,1)S(1)} %param.1), channel_id=1, source_target_pairs={{0,32},{16,48},{32,64},{48,80},{64,96},{80,112},{1,33},{17,49},{33... | collective-permute-start | bytes 983048 | tf_op jit(solution)/shard_map/while/body/eval_jaxpr/cond/branch_1_fun/ppermute | solution.py:352
  229.3 10.3 %collective-permute-start = (bf16[256,640]{1,0:T(8,128)(2,1)S(1)}, bf16[256,640]{1,0:T(8,128)(2,1)S(1)}, u32[]{:S(2)}, u32[]{:S(2)}) collective-permute-start(bf16[256,640]{1,0:T(8,128)(2,1)S(1)} %param.1), channel_id=1, source_target_pairs={{0,32},{16,48},{32,64},{48,80},{64,96},{80,112},{1,33},{17,49},{33... | collective-permute-start | bytes 983048 | tf_op jit(solution)/shard_map/while/body/eval_jaxpr/cond/branch_1_fun/ppermute | solution.py:352
  277.0 11.4 %copy-start.1 = (bf16[2,4,64,640]{3,2,1,0:T(8,128)(2,1)S(1)}, bf16[2,4,64,640]{3,2,1,0:T(8,128)(2,1)}, u32[]{:S(2)}) copy-start(bf16[2,4,64,640]{3,2,1,0:T(8,128)(2,1)} %param.14) | copy-start | bytes 1966084
  277.1 1.5 collective-permute-start.19
  278.6 2.7 collective-permute-start.20
  279.3 8.4 %collective-permute-start.21 = (bf16[2,4,8,640]{3,2,1,0:T(8,128)(2,1)S(1)}, bf16[2,4,8,640]{3,2,1,0:T(8,128)(2,1)S(1)}, u32[]{:S(2)}, u32[]{:S(2)}) collective-permute-start(bf16[2,4,8,640]{3,2,1,0:T(8,128)(2,1)S(1)} %get-tuple-element.356), channel_id=1, source_target_pairs={{96,32},{112,48},{97,33},{113,49},{98,34},{114,50},{99,35},{115,51... | collective-permute-start | bytes 245768 | tf_op jit(solution)/shard_map/ppermute | solution.py:365
  280.6 7.1 %collective-permute-start.22 = (bf16[2,4,8,640]{3,2,1,0:T(8,128)(2,1)S(1)}, bf16[2,4,8,640]{3,2,1,0:T(8,128)(2,1)S(1)}, u32[]{:S(2)}, u32[]{:S(2)}) collective-permute-start(bf16[2,4,8,640]{3,2,1,0:T(8,128)(2,1)S(1)} %get-tuple-element.355), channel_id=1, source_target_pairs={{96,64},{112,80},{97,65},{113,81},{98,66},{114,82},{99,67},{115,83... | collective-permute-start | bytes 245768 | tf_op jit(solution)/shard_map/ppermute | solution.py:365

commit v2 on v1

--- a/solution.py
+++ b/solution.py
@@ -12,7 +12,7 @@
 CELLS = 256
 W = 64
 KEYS = 4096
-CHUNK = 1024
+CHUNK = 2048
 F32 = jnp.float32
 BF = jnp.bfloat16
 QSCALE = 0.125 * 1.4426950408889634
@@ -32,6 +32,10 @@
     return lax.dot_general(a, b, (((1,), (1,)), ((), ())), preferred_element_type=F32)
 
 
+def dot_turned(a, b):
+    return lax.dot_general(a, b, (((0,), (1,)), ((), ())), preferred_element_type=F32)
+
+
 def start_copy(use_own, own, other, target, sem):
     @pl.when(use_own)
     def _():
@@ -47,22 +51,24 @@
 
 
 def stale_kernel(count, *refs):
-    pieces, (ga_ref, wkv_ref, kv_ref) = refs[:count], refs[count:]
+    pieces, (ga_ref, wk_ref, wv_ref, k_ref, vt_ref) = refs[:count], refs[count:]
     block, piece = pl.program_id(0), pl.program_id(1)
     raw = pieces[0][...]
     for i in range(1, count):
         raw = jnp.where(piece == i, pieces[i][...], raw)
     raw = raw.reshape(-1, C).astype(F32)
     normed = normalize(raw, ga_ref[pl.ds(block, 1), :]).astype(BF)
-    out = dot(normed, wkv_ref[...]).astype(BF)
-    for part in range(2 * PAIRS):
-        kv_ref[part] = out[:, part * 128 : (part + 1) * 128]
-
-
-def stale_call(pieces, gains, wkv):
+    keys = dot(normed, wk_ref[...]).astype(BF)
+    values = dot_turned(wv_ref[...], normed).astype(BF)
+    for pair in range(PAIRS):
+        k_ref[pair] = keys[:, pair * 128 : (pair + 1) * 128]
+        vt_ref[pair] = values[pair * 128 : (pair + 1) * 128]
+
+
+def stale_call(pieces, gains, wk, wv):
     count, size = len(pieces), pieces[0].shape[0]
-    patches = min(size, 4)
-    steps = size // patches
+    patches, steps = size, 1
+    cells = count * size * CELLS
 
     def piece_spec(i):
         def place(b, piece, step):
@@ -73,24 +79,32 @@
     return pl.pallas_call(
         functools.partial(stale_kernel, count),
         grid=(2, count, steps),
-        out_shape=jax.ShapeDtypeStruct((2, 2 * PAIRS, count * size * CELLS, 128), BF),
+        out_shape=[
+            jax.ShapeDtypeStruct((2, PAIRS, cells, 128), BF),
+            jax.ShapeDtypeStruct((2, PAIRS, 128, cells), BF),
+        ],
         in_specs=[piece_spec(i) for i in range(count)]
         + [
             pl.BlockSpec((2, C), lambda b, piece, step: (0, 0)),
-            pl.BlockSpec((None, C, 2 * C), lambda b, piece, step: (b, 0, 0)),
+            pl.BlockSpec((None, C, C), lambda b, piece, step: (b, 0, 0)),
+            pl.BlockSpec((None, C, C), lambda b, piece, step: (b, 0, 0)),
         ],
-        out_specs=pl.BlockSpec(
-            (None, 2 * PAIRS, patches * CELLS, 128),
-            lambda b, piece, step: (b, 0, piece * steps + step, 0),
-        ),
+        out_specs=[
+            pl.BlockSpec(
+                (None, PAIRS, patches * CELLS, 128),
+                lambda b, piece, step: (b, 0, piece * steps + step, 0),
+            ),
+            pl.BlockSpec(
+                (None, PAIRS, 128, patches * CELLS),
+                lambda b, piece, step: (b, 0, 0, piece * steps + step),
+            ),
+        ],
         compiler_params=pltpu.CompilerParams(vmem_limit_bytes=50 << 20),
         cost_estimate=pl.CostEstimate(
-            flops=8 * count * size * CELLS * C * C,
-            transcendentals=0,
-            bytes_accessed=12 * count * size * CELLS * C,
+            flops=8 * cells * C * C, transcendentals=0, bytes_accessed=12 * cells * C
         ),
         name="stale_%d" % (count * size),
-    )(*pieces, gains, wkv)
+    )(*pieces, gains, wk, wv)
 
 
 STORES = 3
@@ -101,13 +115,14 @@
     x_ref, ga_ref, gc_ref, up_ref, dn_ref = refs[:5]
     own = dict(zip(NAMES, refs[5:10]))
     other = dict(zip(NAMES, refs[10:15]))
-    kv_hbm, refs = refs[15 : 15 + STORES], refs[15 + STORES :]
-    o_ref, wqkv, wout, wconv, kv, queries, fresh, context, mid, cols, sem_w, sem_k = refs
+    k_hbm, v_hbm = refs[15 : 15 + STORES], refs[15 + STORES : 15 + 2 * STORES]
+    o_ref, wqk, wv, wout, wconv, keys, values = refs[15 + 2 * STORES : 22 + 2 * STORES]
+    queries, fresh, fresh_t, context, mid, cols, sem_w, sem_k = refs[22 + 2 * STORES :]
     core = lax.axis_index("segment") % 2
     targets = {
-        "query": wqkv.at[:, pl.ds(0, C)],
-        "key": wqkv.at[:, pl.ds(C, C)],
-        "value": wqkv.at[:, pl.ds(2 * C, C)],
+        "query": wqk.at[:, pl.ds(0, C)],
+        "key": wqk.at[:, pl.ds(C, C)],
+        "value": wv,
         "out": wout,
         "conv": wconv,
     }
@@ -126,17 +141,16 @@
         wait_copy(own[name], targets[name], sem_w.at[NAMES.index(name)])
 
     def pair_copies(place, pair):
-        copies = []
-        for part in (pair, PAIRS + pair):
-            begin = 0
-            for i, store in enumerate(kv_hbm):
-                cells = pl.ds(begin, store.shape[2])
-                begin += store.shape[2]
-                copies.append(
-                    pltpu.make_async_copy(
-                        store.at[place, part], kv.at[part, cells], sem_k.at[part, i]
-                    )
-                )
+        copies, begin = [], 0
+        for i in range(STORES):
+            size = k_hbm[i].shape[2]
+            cells = pl.ds(begin, size)
+            begin += size
+            for source, target, j in (
+                (k_hbm[i].at[place, pair], keys.at[pair, cells, :], i),
+                (v_hbm[i].at[place, pair], values.at[pair, :, cells], STORES + i),
+            ):
+                copies.append(pltpu.make_async_copy(source, target, sem_k.at[pair, j]))
         return copies
 
     start(0, "query", "key", "value")
@@ -159,32 +173,40 @@
                     copy.start()
             start(0, "out", "conv")
 
-        made = dot(normed, wqkv[...])
+        made = dot(normed, wqk[...])
+        turned_values = dot_turned(wv[...], normed).astype(BF)
         for pair in range(PAIRS):
-            queries[pair] = (made[:, pair * 128 : (pair + 1) * 128] * QSCALE).astype(BF)
-        for part in range(2 * PAIRS):
-            fresh[part] = made[:, C + part * 128 : C + (part + 1) * 128].astype(BF)
+            lanes = slice(pair * 128, (pair + 1) * 128)
+            queries[pair] = (made[:, lanes] * QSCALE).astype(BF)
+            fresh[pair] = made[:, C + pair * 128 : C + (pair + 1) * 128].astype(BF)
+            fresh_t[pair] = turned_values[lanes]
         ahead(lambda: start(1, "query", "key", "value"))
 
         def attend(pair):
             for copy in pair_copies(0, pair):
                 copy.wait()
-            kv[pair, own_cells, :] = fresh[pair]
-            kv[PAIRS + pair, own_cells, :] = fresh[PAIRS + pair]
+            keys[pair, own_cells, :] = fresh[pair]
+            values[pair, :, own_cells] = fresh_t[pair]
             both = queries[pair]
             zero = jnp.zeros_like(both)
-            heads = (jnp.where(lane < 64, both, zero), jnp.where(lane < 64, zero, both))
-            totals = [jnp.zeros((CELLS, 128), F32)] * 2
-            sums = [jnp.zeros((CELLS, 128), F32)] * 2
+            heads = jnp.concatenate(
+                [jnp.where(lane < 64, both, zero), jnp.where(lane < 64, zero, both)], 0
+            )
+            totals = jnp.zeros((8, 2 * CELLS), F32)
+            sums = [jnp.zeros((64, CELLS), F32)] * 2
             for chunk in range(KEYS // CHUNK):
                 cells = pl.ds(chunk * CHUNK, CHUNK)
+                weights = jnp.exp2(dot_t(keys[pair, cells, :], heads))
+                totals = totals + jnp.sum(weights.reshape(CHUNK // 8, 8, 2 * CELLS), 0)
+                weights = weights.astype(BF)
                 for head in range(2):
-                    weights = jnp.exp2(dot_t(heads[head], kv[pair, cells, :]))
-                    for tile in range(CHUNK // 128):
-                        totals[head] = totals[head] + weights[:, tile * 128 : (tile + 1) * 128]
-                    sums[head] = sums[head] + dot(weights.astype(BF), kv[PAIRS + pair, cells, :])
-            ready = [s / jnp.sum(t, axis=-1, keepdims=True) for s, t in zip(sums, totals)]
-            context[pair] = jnp.where(lane < 64, ready[0], ready[1]).astype(BF)
+                    sums[head] = sums[head] + dot(
+                        values[pair, head * 64 : (head + 1) * 64, cells],
+                        weights[:, head * CELLS : (head + 1) * CELLS],
+                    )
+            totals = jnp.sum(totals, axis=0, keepdims=True)
+            ready = [sums[i] / totals[:, i * CELLS : (i + 1) * CELLS] for i in range(2)]
+            context[pair] = jnp.concatenate(ready, 0).T.astype(BF)
 
             def next_pair():
                 for copy in pair_copies(1, pair):
@@ -236,20 +258,23 @@
     return pl.pallas_call(
         block_kernel,
         out_shape=jax.ShapeDtypeStruct((CELLS, C), BF),
-        in_specs=[vmem] * 5 + [hbm] * (10 + STORES),
+        in_specs=[vmem] * 5 + [hbm] * (10 + 2 * STORES),
         out_specs=vmem,
         scratch_shapes=[
-            pltpu.VMEM((C, 3 * C), BF),
+            pltpu.VMEM((C, 2 * C), BF),
+            pltpu.VMEM((C, C), BF),
             pltpu.VMEM((C, C), BF),
             pltpu.VMEM((9, C, C), BF),
-            pltpu.VMEM((2 * PAIRS, KEYS, 128), BF),
+            pltpu.VMEM((PAIRS, KEYS, 128), BF),
+            pltpu.VMEM((PAIRS, 128, KEYS), BF),
             pltpu.VMEM((PAIRS, CELLS, 128), BF),
-            pltpu.VMEM((2 * PAIRS, CELLS, 128), BF),
+            pltpu.VMEM((PAIRS, CELLS, 128), BF),
+            pltpu.VMEM((PAIRS, 128, CELLS), BF),
             pltpu.VMEM((PAIRS, CELLS, 128), BF),
             pltpu.VMEM((CELLS, C), F32),
             pltpu.VMEM((3, CELLS + 2 * W, C), BF),
             pltpu.SemaphoreType.DMA((5,)),
-            pltpu.SemaphoreType.DMA((2 * PAIRS, STORES)),
+            pltpu.SemaphoreType.DMA((PAIRS, 2 * STORES)),
         ],
         compiler_params=pltpu.CompilerParams(vmem_limit_bytes=58 << 20),
         cost_estimate=pl.CostEstimate(
@@ -266,7 +291,8 @@
         down,
         *[own[name] for name in NAMES],
         *[other[name] for name in NAMES],
-        *stored,
+        *[pair[0] for pair in stored],
+        *[pair[1] for pair in stored],
     )
 
 
@@ -321,29 +347,32 @@
     )
     other = {name: swap(value) for name, value in first_sent.items()}
     gains = jnp.concatenate(ordered(norm_attn, swap(norm_attn)), 0)
-    wkv = jnp.stack(
-        ordered(*[jnp.concatenate([w["key"], w["value"]], 1) for w in (own, other)])
-    )
+    wk, wv = [jnp.stack(ordered(own[name], other[name])) for name in ("key", "value")]
     back, ahead = ring_near(raw, 0)
+    own_back, own_ahead = ring_near(raw, 1)
     far = ring_far(back, ahead, 0)
-    row = jnp.stack([raw, back, jnp.concatenate(far, 0), ahead])
-    row, sent, edges, norm_conv = lax.optimization_barrier(
-        (row, {name: own[name] for name in ("query", "out", "conv")}, edges, norm_conv)
-    )
-    back, ahead = ring_near(row, 1)
+    rest = jnp.stack([back, jnp.concatenate(far, 0), ahead])
+    first = jnp.stack([raw, own_back, own_ahead])
+    rest, first, sent, edges, norm_conv = lax.optimization_barrier(
+        (rest, first, {name: own[name] for name in ("query", "out", "conv")}, edges, norm_conv)
+    )
+    back, ahead = ring_near(rest, 1)
     upper = lax.ppermute(edges[:, 1], "patch", [(i, i + 1) for i in range(15)])
     lower = lax.ppermute(edges[:, 0], "patch", [(i + 1, i) for i in range(15)])
-    stored = stale_call([row], gains, wkv)
+    stored = stale_call([first, rest], gains, wk, wv)
     back, ahead, upper, lower, stored = lax.optimization_barrier(
         (back, ahead, upper, lower, stored)
     )
-    far = ring_far(back, ahead, 1)
+    far = (
+        turned(jnp.concatenate([first[1:2], back[:1]], 0), 1, 1),
+        turned(ahead[1:], 1, -1),
+    )
 
     other |= {name: swap(value) for name, value in sent.items()}
     conv_gains = jnp.concatenate(ordered(norm_conv, swap(norm_conv)), 0)
 
     x = lax.dynamic_index_in_dim(latent, core, 0, keepdims=False).reshape(CELLS, C)
-    stored = [stored] + [stale_call(pieces, gains, wkv) for pieces in ([back, ahead], far)]
+    stored = [stored] + [stale_call(pieces, gains, wk, wv) for pieces in ([back, ahead], far)]
 
     def two_blocks(x):
         return block_call(x, gains, conv_gains, upper, lower, own, other, stored)

time: 292 us -> 290 us (level)
  waiting for transfers between devices: 61.2 us -> 76.9 us
  Pallas kernels: 181 us -> 167 us
    pallas_call x4, Pallas kernels: 149 us -> 134 us  [block_call(): pl.pallas_call(block_kernel, out_shape=jax.ShapeDtypeStruct((CELLS, C), B...]
    ppermute x8 -> x10, waiting for transfers between devices: 14 us -> 21.9 us  [turned(): return lax.ppermute(value, ('segment', 'patch'), pairs)]
    unnamed x28 -> x47, local copies, waits for them, and re-layouts: 1.29 us -> 5.24 us
    ppermute x1, waiting for transfers between devices: 4.47 us -> 7.82 us  [shards(): upper = lax.ppermute(edges[:, 1], 'patch', [(i, i + 1) for i in range(15)])]
    ppermute x8 -> x10, starting transfers between devices: 11.8 us -> 12.4 us  [turned(): return lax.ppermute(value, ('segment', 'patch'), pairs)]
  transfers between devices with their start and end apart: 25 -> 27, of which waited for: 14 -> 15; matrix products, arithmetic and copies ran while one was open for 2% -> 1% of each run, Pallas kernels for 11% -> 12%
where the time goes in v2:
time: 290 us; the launch traced here: 289 us
  Pallas kernels  167 us (58%)
  waiting for transfers between devices  76.9 us (27%)
  starting transfers between devices  32.6 us (11%)
  other arithmetic  5.91 us (2%)
  local copies, waits for them, and re-layouts  5.89 us (2%)
    pallas_call x4, Pallas kernels, block_call(): pl.pallas_call(block_kernel, out_shape=jax.ShapeDtypeStruct((CELLS, C), B...  134 us
    pallas_call x3, Pallas kernels, stale_call(): pl.pallas_call(functools.partial(stale_kernel, count), grid=(2, count, st...  33.5 us
    ppermute x3, waiting for transfers between devices, hop(): return lax.ppermute(x, 'segment', [(i, i + 2) for i in range(6)])  25.3 us
    ppermute x10, waiting for transfers between devices, turned(): return lax.ppermute(value, ('segment', 'patch'), pairs)  21.9 us
    ppermute x9, waiting for transfers between devices, swap(): return lax.ppermute(value, 'segment', sibling)  14.8 us
    ppermute x10, starting transfers between devices, turned(): return lax.ppermute(value, ('segment', 'patch'), pairs)  12.4 us
    ppermute x3, starting transfers between devices, hop(): return lax.ppermute(x, 'segment', [(i, i + 2) for i in range(6)])  10.2 us
    ppermute x1, waiting for transfers between devices, shards(): upper = lax.ppermute(edges[:, 1], 'patch', [(i, i + 1) for i in range(15)])  7.82 us
  transfers between devices with their start and end apart: 27, of which 15 were waited for; matrix products, arithmetic and copies ran while one was open for 1% of the time, Pallas kernels for 12%

profile of v2, /device:TPU:18, one launch (start us, length us, event | category | flops | bytes accessed | tf_op | source)
XLA Modules:
  0.0 289.1 jit_solution(12206078106336916827)
XLA Ops:
  0.0 1.2 fusion.2
  1.3 1.8 collective-permute-done.1
  3.1 1.2 select_bitcast_fusion.4
  4.4 4.1 %collective-permute-start.5 = (bf16[2,256,640]{2,1,0:T(8,128)(2,1)S(1)}, bf16[2,256,640]{2,1,0:T(8,128)(2,1)S(1)}, u32[]{:S(2)}, u32[]{:S(2)}) collective-permute-start(bf16[2,256,640]{2,1,0:T(8,128)(2,1)S(1)} %fusion), channel_id=1, source_target_pairs={{0,3},{1,0},{2,1},{3,2},{4,7},{5,4},{6,5},{7,6},{8,11},{9,8},{10,9... | collective-permute-start | bytes 1966088 | tf_op jit(solution)/shard_map/ppermute | solution.py:309
  8.5 0.4 collective-permute-start.8
  9.0 1.6 collective-permute-start.7
  10.5 12.5 %collective-permute-done.5 = bf16[2,256,640]{2,1,0:T(8,128)(2,1)S(1)} collective-permute-done((bf16[2,256,640]{2,1,0:T(8,128)(2,1)S(1)}, bf16[2,256,640]{2,1,0:T(8,128)(2,1)S(1)}, u32[]{:S(2)}, u32[]{:S(2)}) %collective-permute-start.5) | collective-permute-done | bytes 655392 | tf_op jit(solution)/shard_map/ppermute | solution.py:309
  23.1 3.8 %collective-permute-start.6 = (bf16[1,256,640]{2,1,0:T(8,128)(2,1)S(1)}, bf16[1,256,640]{2,1,0:T(8,128)(2,1)S(1)}, u32[]{:S(2)}, u32[]{:S(2)}) collective-permute-start(bf16[1,256,640]{2,1,0:T(8,128)(2,1)S(1)} %slice.55), channel_id=1, source_target_pairs={{0,3},{1,0},{2,1},{3,2},{4,7},{5,4},{6,5},{7,6},{8,11},{9,8},{10,9... | collective-permute-start | bytes 983048 | tf_op jit(solution)/shard_map/ppermute | solution.py:309
  26.9 0.1 collective-permute-done.3
  27.2 1.5 pad_maximum_fusion.1.refs_0_
  28.7 2.8 collective-permute-done.6
  31.5 3.9 %collective-permute-done.4 = bf16[1,256,640]{2,1,0:T(8,128)(2,1)S(1)} collective-permute-done((bf16[1,256,640]{2,1,0:T(8,128)(2,1)S(1)}, bf16[1,256,640]{2,1,0:T(8,128)(2,1)S(1)}, u32[]{:S(2)}, u32[]{:S(2)}) %collective-permute-start.4) | collective-permute-done | bytes 327712 | tf_op jit(solution)/shard_map/ppermute | solution.py:309
  35.5 0.3 pad_maximum_fusion.refs_1_
  35.8 0.1 collective-permute-start.18
  35.9 0.7 copy-done.7
  36.6 0.7 copy-done.9
  37.3 0.5 collective-permute-start.2
  37.8 0.5 collective-permute-start.11
  38.3 11.0 %collective-permute-done.2 = f32[1,640]{1,0:T(1,128)S(1)} collective-permute-done((f32[1,640]{1,0:T(1,128)S(1)}, f32[1,640]{1,0:T(1,128)S(1)}, u32[]{:S(2)}, u32[]{:S(2)}) %collective-permute-start.2) | collective-permute-done | bytes 2592 | tf_op jit(solution)/shard_map/ppermute | solution.py:329
  49.4 0.3 select_bitcast_fusion.1
  49.7 0.6 copy-done.11
  50.3 0.3 copy-done.13
  50.5 0.2 pad_maximum_fusion.3.refs_4_
  50.7 0.2 pad_maximum_fusion.2.refs_3_
  50.9 3.1 %collective-permute-start.13 = (bf16[2,64,640]{2,1,0:T(8,128)(2,1)S(1)}, bf16[2,64,640]{2,1,0:T(8,128)(2,1)S(1)}, u32[]{:S(2)}, u32[]{:S(2)}) collective-permute-start(bf16[2,64,640]{2,1,0:T(8,128)(2,1)S(1)} %get-tuple-element.424), channel_id=1, source_target_pairs={{1,0},{2,1},{3,2},{4,3},{5,4},{6,5},{7,6},{8,7},{9,8},{10,9},{11,1... | collective-permute-start | bytes 491528 | tf_op jit(solution)/shard_map/ppermute | solution.py:361
  54.1 2.7 collective-permute-start.12
  56.8 12.1 %stale_6.2 = (bf16[2,5,1536,128]{3,2,1,0:T(8,128)(2,1)}, bf16[2,5,128,1536]{3,2,1,0:T(8,128)(2,1)}) custom-call(bf16[3,2,256,640]{3,2,1,0:T(8,128)(2,1)} %pad_maximum_fusion.1.refs_0_, bf16[3,2,256,640]{3,2,1,0:T(8,128)(2,1)} %copy-done.5, f32[2,640]{1,0:T(2,128)S(1)} %pad_maximum_fusion.7.refs_2_, bf16[2,640,640]{2,1,0:T(8,128)(2,1)S(1)} %pad_maximum_fusion.2.refs_3_, ...), custom_call_target="tpu_custom_call" | custom-call | flops 5033164800 | bytes 11796480 | tf_op jit(solution)/shard_map/stale_6/pallas_call | solution.py:79
  68.9 7.8 %collective-permute-done.12 = bf16[2,64,640]{2,1,0:T(8,128)(2,1)S(1)} collective-permute-done((bf16[2,64,640]{2,1,0:T(8,128)(2,1)S(1)}, bf16[2,64,640]{2,1,0:T(8,128)(2,1)S(1)}, u32[]{:S(2)}, u32[]{:S(2)}) %collective-permute-start.12) | collective-permute-done | bytes 163872 | tf_op jit(solution)/shard_map/ppermute | solution.py:360
  76.8 1.3 copy-done.14
  78.2 0.1 slice.47
  78.3 0.3 copy-done.6
  78.7 0.5 collective-permute-start.20
  79.1 0.1 slice-done
  79.2 0.1 pad_maximum_fusion.4
  79.4 1.5 collective-permute-start.19
  81.0 0.6 collective-permute-start.16
  81.5 0.5 collective-permute-done.9
  82.1 0.2 collective-permute-start.17
  82.3 12.1 %stale_6.3 = (bf16[2,5,1536,128]{3,2,1,0:T(8,128)(2,1)}, bf16[2,5,128,1536]{3,2,1,0:T(8,128)(2,1)}) custom-call(bf16[3,2,256,640]{3,2,1,0:T(8,128)(2,1)} %copy-done.14, bf16[3,2,256,640]{3,2,1,0:T(8,128)(2,1)} %copy-done.6, f32[2,640]{1,0:T(2,128)S(1)} %pad_maximum_fusion.7.refs_2_, bf16[2,640,640]{2,1,0:T(8,128)(2,1)S(1)} %pad_maximum_fusion.2.refs_3_, ...), custom_call_target="tpu_custom_call" | custom-call | flops 5033164800 | bytes 11796480 | tf_op jit(solution)/shard_map/stale_6/pallas_call | solution.py:79
  94.5 1.8 collective-permute-done.20.refs_1_
  96.3 0.8 collective-permute-done.19.refs_0_
  97.1 9.2 %stale_4.1 = (bf16[2,5,1024,128]{3,2,1,0:T(8,128)(2,1)}, bf16[2,5,128,1024]{3,2,1,0:T(8,128)(2,1)}) custom-call(bf16[2,2,256,640]{3,2,1,0:T(8,128)(2,1)S(1)} %collective-permute-done.19.refs_0_, bf16[2,2,256,640]{3,2,1,0:T(8,128)(2,1)S(1)} %collective-permute-done.20.refs_1_, f32[2,640]{1,0:T(2,128)S(1)} %pad_maximum_fusion.7.refs_2_, ...), custom_call_target="tpu_custom_call" | custom-call | flops 3355443200 | bytes 7864320 | tf_op jit(solution)/shard_map/stale_4/pallas_call | solution.py:79
  106.3 0.9 copy-done.17
  107.2 0.3 copy-done.18
  107.5 169.5 %while.13 = (s32[]{:T(128)}, bf16[256,640]{1,0:T(8,128)(2,1)S(1)}, f32[2,640]{1,0:T(2,128)S(1)}, f32[2,640]{1,0:T(2,128)S(1)}, bf16[2,64,640]{2,1,0:T(8,128)(2,1...) while((s32[]{:T(128)}, bf16[256,640]{1,0:T(8,128)(2,1)S(1)}, ...), condition=%wide.region_3.4_spmd, body=%wide.region_0.3_spmd.sunk | while | flops 25999998976 | bytes 46621712 | solution.py:386
  107.5 33.4 %blocks.5 = bf16[256,640]{1,0:T(8,128)(2,1)S(1)} custom-call(bf16[256,640]{1,0:T(8,128)(2,1)S(1)} %get-tuple-element.590.refs_0_, f32[2,640]{1,0:T(2,128)S(1)} %get-tuple-element.615.refs_1_, f32[2,640]{1,0:T(2,128)S(1)} %get-tuple-element.616.refs_2_, bf16[2,64,640]{2,1,0:T(8,128)(2,1)S(1)} %get-tuple-element.617.refs_3_, ...), custom_call_target="tpu_custom_call" | custom-call | flops 25999998976 | bytes 44000000 | tf_op jit(solution)/shard_map/while/body/eval_jaxpr/blocks/pallas_call | solution.py:258
  140.9 12.3 %conditional.2 = (bf16[256,640]{1,0:T(8,128)(2,1)S(1)}) conditional(s32[]{:T(128)} %convert_element_type.13, bf16[256,640]{1,0:T(8,128)(2,1)S(1)} %blocks.5, bf16[256,640]{1,0:T(8,128)(2,1)S(1)} %blocks.5), branch_computations={%region_1.1_spmd, %region_2.2_spmd} | conditional | bytes 1966128 | solution.py:384
  141.0 3.4 %collective-permute-start = (bf16[256,640]{1,0:T(8,128)(2,1)S(1)}, bf16[256,640]{1,0:T(8,128)(2,1)S(1)}, u32[]{:S(2)}, u32[]{:S(2)}) collective-permute-start(bf16[256,640]{1,0:T(8,128)(2,1)S(1)} %param.1), channel_id=1, source_target_pairs={{0,32},{16,48},{32,64},{48,80},{64,96},{80,112},{1,33},{17,49},{33... | collective-permute-start | bytes 983048 | tf_op jit(solution)/shard_map/while/body/eval_jaxpr/cond/branch_1_fun/ppermute | solution.py:381
  144.4 8.9 %collective-permute-done = bf16[256,640]{1,0:T(8,128)(2,1)S(1)} collective-permute-done((bf16[256,640]{1,0:T(8,128)(2,1)S(1)}, bf16[256,640]{1,0:T(8,128)(2,1)S(1)}, u32[]{:S(2)}, u32[]{:S(2)}) %collective-permute-start) | collective-permute-done | bytes 327712 | tf_op jit(solution)/shard_map/while/body/eval_jaxpr/cond/branch_1_fun/ppermute | solution.py:381
  153.3 33.4 %blocks.5 = bf16[256,640]{1,0:T(8,128)(2,1)S(1)} custom-call(bf16[256,640]{1,0:T(8,128)(2,1)S(1)} %get-tuple-element.590.refs_0_, f32[2,640]{1,0:T(2,128)S(1)} %get-tuple-element.615.refs_1_, f32[2,640]{1,0:T(2,128)S(1)} %get-tuple-element.616.refs_2_, bf16[2,64,640]{2,1,0:T(8,128)(2,1)S(1)} %get-tuple-element.617.refs_3_, ...), custom_call_target="tpu_custom_call" | custom-call | flops 25999998976 | bytes 44000000 | tf_op jit(solution)/shard_map/while/body/eval_jaxpr/blocks/pallas_call | solution.py:258
  186.7 11.9 %conditional.2 = (bf16[256,640]{1,0:T(8,128)(2,1)S(1)}) conditional(s32[]{:T(128)} %convert_element_type.13, bf16[256,640]{1,0:T(8,128)(2,1)S(1)} %blocks.5, bf16[256,640]{1,0:T(8,128)(2,1)S(1)} %blocks.5), branch_computations={%region_1.1_spmd, %region_2.2_spmd} | conditional | bytes 1966128 | solution.py:384
  186.7 3.4 %collective-permute-start = (bf16[256,640]{1,0:T(8,128)(2,1)S(1)}, bf16[256,640]{1,0:T(8,128)(2,1)S(1)}, u32[]{:S(2)}, u32[]{:S(2)}) collective-permute-start(bf16[256,640]{1,0:T(8,128)(2,1)S(1)} %param.1), channel_id=1, source_target_pairs={{0,32},{16,48},{32,64},{48,80},{64,96},{80,112},{1,33},{17,49},{33... | collective-permute-start | bytes 983048 | tf_op jit(solution)/shard_map/while/body/eval_jaxpr/cond/branch_1_fun/ppermute | solution.py:381
  190.2 8.5 %collective-permute-done = bf16[256,640]{1,0:T(8,128)(2,1)S(1)} collective-permute-done((bf16[256,640]{1,0:T(8,128)(2,1)S(1)}, bf16[256,640]{1,0:T(8,128)(2,1)S(1)}, u32[]{:S(2)}, u32[]{:S(2)}) %collective-permute-start) | collective-permute-done | bytes 327712 | tf_op jit(solution)/shard_map/while/body/eval_jaxpr/cond/branch_1_fun/ppermute | solution.py:381
  198.7 33.4 %blocks.5 = bf16[256,640]{1,0:T(8,128)(2,1)S(1)} custom-call(bf16[256,640]{1,0:T(8,128)(2,1)S(1)} %get-tuple-element.590.refs_0_, f32[2,640]{1,0:T(2,128)S(1)} %get-tuple-element.615.refs_1_, f32[2,640]{1,0:T(2,128)S(1)} %get-tuple-element.616.refs_2_, bf16[2,64,640]{2,1,0:T(8,128)(2,1)S(1)} %get-tuple-element.617.refs_3_, ...), custom_call_target="tpu_custom_call" | custom-call | flops 25999998976 | bytes 44000000 | tf_op jit(solution)/shard_map/while/body/eval_jaxpr/blocks/pallas_call | solution.py:258
  232.1 11.4 %conditional.2 = (bf16[256,640]{1,0:T(8,128)(2,1)S(1)}) conditional(s32[]{:T(128)} %convert_element_type.13, bf16[256,640]{1,0:T(8,128)(2,1)S(1)} %blocks.5, bf16[256,640]{1,0:T(8,128)(2,1)S(1)} %blocks.5), branch_computations={%region_1.1_spmd, %region_2.2_spmd} | conditional | bytes 1966128 | solution.py:384
  232.1 3.4 %collective-permute-start = (bf16[256,640]{1,0:T(8,128)(2,1)S(1)}, bf16[256,640]{1,0:T(8,128)(2,1)S(1)}, u32[]{:S(2)}, u32[]{:S(2)}) collective-permute-start(bf16[256,640]{1,0:T(8,128)(2,1)S(1)} %param.1), channel_id=1, source_target_pairs={{0,32},{16,48},{32,64},{48,80},{64,96},{80,112},{1,33},{17,49},{33... | collective-permute-start | bytes 983048 | tf_op jit(solution)/shard_map/while/body/eval_jaxpr/cond/branch_1_fun/ppermute | solution.py:381
  235.5 7.9 %collective-permute-done = bf16[256,640]{1,0:T(8,128)(2,1)S(1)} collective-permute-done((bf16[256,640]{1,0:T(8,128)(2,1)S(1)}, bf16[256,640]{1,0:T(8,128)(2,1)S(1)}, u32[]{:S(2)}, u32[]{:S(2)}) %collective-permute-start) | collective-permute-done | bytes 327712 | tf_op jit(solution)/shard_map/while/body/eval_jaxpr/cond/branch_1_fun/ppermute | solution.py:381
  243.5 33.4 %blocks.5 = bf16[256,640]{1,0:T(8,128)(2,1)S(1)} custom-call(bf16[256,640]{1,0:T(8,128)(2,1)S(1)} %get-tuple-element.590.refs_0_, f32[2,640]{1,0:T(2,128)S(1)} %get-tuple-element.615.refs_1_, f32[2,640]{1,0:T(2,128)S(1)} %get-tuple-element.616.refs_2_, bf16[2,64,640]{2,1,0:T(8,128)(2,1)S(1)} %get-tuple-element.617.refs_3_, ...), custom_call_target="tpu_custom_call" | custom-call | flops 25999998976 | bytes 44000000 | tf_op jit(solution)/shard_map/while/body/eval_jaxpr/blocks/pallas_call | solution.py:258
  277.2 1.4 collective-permute-done.21
  278.6 0.7 collective-permute-start.22
  279.3 0.7 collective-permute-start.24
  280.0 1.3 collective-permute-start.23
  281.3 7.1 %collective-permute-done.23 = bf16[2,4,8,640]{3,2,1,0:T(8,128)(2,1)S(1)} collective-permute-done((bf16[2,4,8,640]{3,2,1,0:T(8,128)(2,1)S(1)}, bf16[2,4,8,640]{3,2,1,0:T(8,128)(2,1)S(1)}, u32[]{:S(2)}, u32[]{:S(2)}) %collective-permute-start.23) | collective-permute-done | bytes 81952 | tf_op jit(solution)/shard_map/ppermute | solution.py:394
  288.4 0.7 fusion.13
  (83 shorter events, 1.1 us)
Async XLA Ops:
  0.0 80.9 %copy-start = (bf16[2,4,64,640]{3,2,1,0:T(8,128)(2,1)S(1)}, bf16[2,4,64,640]{3,2,1,0:T(8,128)(2,1)}, u32[]{:S(2)}) copy-start(bf16[2,4,64,640]{3,2,1,0:T(8,128)(2,1)} %param.14) | copy-start | bytes 1966084
  0.0 3.1 %copy-start.4 = (bf16[1,2,4,64,640]{4,3,2,1,0:T(8,128)(2,1)S(1)}, bf16[1,2,4,64,640]{4,3,2,1,0:T(8,128)(2,1)}, u32[]{:S(2)}) copy-start(bf16[1,2,4,64,640]{4,3,2,1,0:T(8,128)(2,1)} %param.15) | copy-start | bytes 1966084
  1.2 1.9 collective-permute-start.1
  4.4 18.7 %collective-permute-start.5 = (bf16[2,256,640]{2,1,0:T(8,128)(2,1)S(1)}, bf16[2,256,640]{2,1,0:T(8,128)(2,1)S(1)}, u32[]{:S(2)}, u32[]{:S(2)}) collective-permute-start(bf16[2,256,640]{2,1,0:T(8,128)(2,1)S(1)} %fusion), channel_id=1, source_target_pairs={{0,3},{1,0},{2,1},{3,2},{4,7},{5,4},{6,5},{7,6},{8,11},{9,8},{10,9... | collective-permute-start | bytes 1966088 | tf_op jit(solution)/shard_map/ppermute | solution.py:309
  8.5 18.5 %collective-permute-start.3 = (bf16[2,256,640]{2,1,0:T(8,128)(2,1)S(1)}, bf16[2,256,640]{2,1,0:T(8,128)(2,1)S(1)}, u32[]{:S(2)}, u32[]{:S(2)}) collective-permute-start(bf16[2,256,640]{2,1,0:T(8,128)(2,1)S(1)} %fusion), channel_id=1, source_target_pairs={{0,1},{1,2},{2,3},{3,0},{4,5},{5,6},{6,7},{7,4},{8,9},{9,10},{10,1... | collective-permute-start | bytes 1966088 | tf_op jit(solution)/shard_map/ppermute | solution.py:309
  8.5 18.6 %collective-permute-start.8 = (bf16[2,256,640]{2,1,0:T(8,128)(2,1)S(1)}, bf16[2,256,640]{2,1,0:T(8,128)(2,1)S(1)}, u32[]{:S(2)}, u32[]{:S(2)}) collective-permute-start(bf16[2,256,640]{2,1,0:T(8,128)(2,1)S(1)} %fusion), channel_id=1, source_target_pairs={{0,12},{1,13},{2,14},{3,15},{4,0},{5,1},{6,2},{7,3},{8,4},{9,5},{1... | collective-permute-start | bytes 1966088 | tf_op jit(solution)/shard_map/ppermute | solution.py:309
  9.0 18.2 %collective-permute-start.7 = (bf16[2,256,640]{2,1,0:T(8,128)(2,1)S(1)}, bf16[2,256,640]{2,1,0:T(8,128)(2,1)S(1)}, u32[]{:S(2)}, u32[]{:S(2)}) collective-permute-start(bf16[2,256,640]{2,1,0:T(8,128)(2,1)S(1)} %fusion), channel_id=1, source_target_pairs={{0,4},{1,5},{2,6},{3,7},{4,8},{5,9},{6,10},{7,11},{8,12},{9,13},{1... | collective-permute-start | bytes 1966088 | tf_op jit(solution)/shard_map/ppermute | solution.py:309
  23.1 8.4 %collective-permute-start.6 = (bf16[1,256,640]{2,1,0:T(8,128)(2,1)S(1)}, bf16[1,256,640]{2,1,0:T(8,128)(2,1)S(1)}, u32[]{:S(2)}, u32[]{:S(2)}) collective-permute-start(bf16[1,256,640]{2,1,0:T(8,128)(2,1)S(1)} %slice.55), channel_id=1, source_target_pairs={{0,3},{1,0},{2,1},{3,2},{4,7},{5,4},{6,5},{7,6},{8,11},{9,8},{10,9... | collective-permute-start | bytes 983048 | tf_op jit(solution)/shard_map/ppermute | solution.py:309
  27.0 8.4 %collective-permute-start.4 = (bf16[1,256,640]{2,1,0:T(8,128)(2,1)S(1)}, bf16[1,256,640]{2,1,0:T(8,128)(2,1)S(1)}, u32[]{:S(2)}, u32[]{:S(2)}) collective-permute-start(bf16[1,256,640]{2,1,0:T(8,128)(2,1)S(1)} %slice.54), channel_id=1, source_target_pairs={{0,1},{1,2},{2,3},{3,0},{4,5},{5,6},{6,7},{7,4},{8,9},{9,10},{10,1... | collective-permute-start | bytes 983048 | tf_op jit(solution)/shard_map/ppermute | solution.py:309
  35.4 1.1 copy-start.7
  35.5 1.8 copy-start.9
  35.5 1.8 copy-start.15
  35.7 13.9 %copy-start.5 = (bf16[3,2,256,640]{3,2,1,0:T(8,128)(2,1)}, bf16[3,2,256,640]{3,2,1,0:T(8,128)(2,1)S(1)}, u32[]{:S(2)}) copy-start(bf16[3,2,256,640]{3,2,1,0:T(8,128)(2,1)S(1)} %pad_maximum_fusion.refs_1_) | copy-start | bytes 5898244
  35.8 70.6 %collective-permute-start.18 = (bf16[9,640,640]{2,1,0:T(8,128)(2,1)}, bf16[9,640,640]{2,1,0:T(8,128)(2,1)}, u32[]{:S(2)}, u32[]{:S(2)}) collective-permute-start(bf16[9,640,640]{2,1,0:T(8,128)(2,1)} %bitcast.15), channel_id=1, source_target_pairs={{0,16},{16,0},{32,48},{48,32},{64,80},{80,64},{96,112},{112,96},{1... | collective-permute-start | bytes 22118408 | tf_op jit(solution)/shard_map/ppermute | solution.py:329
  36.6 12.7 %collective-permute-start.14 = (bf16[640,640]{1,0:T(8,128)(2,1)S(1)}, bf16[640,640]{1,0:T(8,128)(2,1)S(1)}, u32[]{:S(2)}, u32[]{:S(2)}) collective-permute-start(bf16[640,640]{1,0:T(8,128)(2,1)S(1)} %bitcast.86), channel_id=1, source_target_pairs={{0,16},{16,0},{32,48},{48,32},{64,80},{80,64},{96,112},{112,96},{1... | collective-permute-start | bytes 2457608 | tf_op jit(solution)/shard_map/ppermute | solution.py:329
  37.3 12.1 %collective-permute-start.15 = (bf16[640,640]{1,0:T(8,128)(2,1)S(1)}, bf16[640,640]{1,0:T(8,128)(2,1)S(1)}, u32[]{:S(2)}, u32[]{:S(2)}) collective-permute-start(bf16[640,640]{1,0:T(8,128)(2,1)S(1)} %bitcast.88), channel_id=1, source_target_pairs={{0,16},{16,0},{32,48},{48,32},{64,80},{80,64},{96,112},{112,96},{1... | collective-permute-start | bytes 2457608 | tf_op jit(solution)/shard_map/ppermute | solution.py:329
  37.3 12.0 %collective-permute-start.2 = (f32[1,640]{1,0:T(1,128)S(1)}, f32[1,640]{1,0:T(1,128)S(1)}, u32[]{:S(2)}, u32[]{:S(2)}) collective-permute-start(f32[1,640]{1,0:T(1,128)S(1)} %copy-done.15), channel_id=1, source_target_pairs={{0,16},{16,0},{32,48},{48,32},{64,80},{80,64},{96,112},{112,96},{1... | collective-permute-start | bytes 7688 | tf_op jit(solution)/shard_map/ppermute | solution.py:329
  37.8 39.0 %collective-permute-start.11 = (bf16[3,2,256,640]{3,2,1,0:T(8,128)(2,1)S(1)}, bf16[3,2,256,640]{3,2,1,0:T(8,128)(2,1)S(1)}, u32[]{:S(2)}, u32[]{:S(2)}) collective-permute-start(bf16[3,2,256,640]{3,2,1,0:T(8,128)(2,1)S(1)} %pad_maximum_fusion.refs_1_), channel_id=1, source_target_pairs={{0,12},{1,13},{2,14},{3,15},{4,0},{5,1},{6,2},{7,3},{8,4},{9,5},{1... | collective-permute-start | bytes 5898248 | tf_op jit(solution)/shard_map/ppermute | solution.py:309
  49.3 27.5 %collective-permute-start.10 = (bf16[3,2,256,640]{3,2,1,0:T(8,128)(2,1)S(1)}, bf16[3,2,256,640]{3,2,1,0:T(8,128)(2,1)S(1)}, u32[]{:S(2)}, u32[]{:S(2)}) collective-permute-start(bf16[3,2,256,640]{3,2,1,0:T(8,128)(2,1)S(1)} %pad_maximum_fusion.refs_1_), channel_id=1, source_target_pairs={{0,4},{1,5},{2,6},{3,7},{4,8},{5,9},{6,10},{7,11},{8,12},{9,13},{1... | collective-permute-start | bytes 5898248 | tf_op jit(solution)/shard_map/ppermute | solution.py:309
  49.3 0.9 copy-start.11
  49.4 1.2 copy-start.13
  50.7 31.6 %copy-start.2 = (bf16[2,640,640]{2,1,0:T(8,128)(2,1)}, bf16[2,640,640]{2,1,0:T(8,128)(2,1)S(1)}, u32[]{:S(2)}) copy-start(bf16[2,640,640]{2,1,0:T(8,128)(2,1)S(1)} %pad_maximum_fusion.3.refs_4_) | copy-start | bytes 4915204
  50.9 31.4 %copy-start.3 = (bf16[2,640,640]{2,1,0:T(8,128)(2,1)}, bf16[2,640,640]{2,1,0:T(8,128)(2,1)S(1)}, u32[]{:S(2)}) copy-start(bf16[2,640,640]{2,1,0:T(8,128)(2,1)S(1)} %pad_maximum_fusion.2.refs_3_) | copy-start | bytes 4915204
  50.9 18.0 %collective-permute-start.13 = (bf16[2,64,640]{2,1,0:T(8,128)(2,1)S(1)}, bf16[2,64,640]{2,1,0:T(8,128)(2,1)S(1)}, u32[]{:S(2)}, u32[]{:S(2)}) collective-permute-start(bf16[2,64,640]{2,1,0:T(8,128)(2,1)S(1)} %get-tuple-element.424), channel_id=1, source_target_pairs={{1,0},{2,1},{3,2},{4,3},{5,4},{6,5},{7,6},{8,7},{9,8},{10,9},{11,1... | collective-permute-start | bytes 491528 | tf_op jit(solution)/shard_map/ppermute | solution.py:361
  54.1 22.7 %collective-permute-start.12 = (bf16[2,64,640]{2,1,0:T(8,128)(2,1)S(1)}, bf16[2,64,640]{2,1,0:T(8,128)(2,1)S(1)}, u32[]{:S(2)}, u32[]{:S(2)}) collective-permute-start(bf16[2,64,640]{2,1,0:T(8,128)(2,1)S(1)} %get-tuple-element.425), channel_id=1, source_target_pairs={{0,1},{1,2},{2,3},{3,4},{4,5},{5,6},{6,7},{7,8},{8,9},{9,10},{10,1... | collective-permute-start | bytes 491528 | tf_op jit(solution)/shard_map/ppermute | solution.py:360
  68.9 7.9 %copy-start.19 = (bf16[2,64,640]{2,1,0:T(8,128)(2,1)}, bf16[2,64,640]{2,1,0:T(8,128)(2,1)S(1)}, u32[]{:S(2)}) copy-start(bf16[2,64,640]{2,1,0:T(8,128)(2,1)S(1)} %collective-permute-done.13) | copy-start | bytes 491524
  76.8 5.5 %copy-start.21 = (bf16[2,64,640]{2,1,0:T(8,128)(2,1)}, bf16[2,64,640]{2,1,0:T(8,128)(2,1)S(1)}, u32[]{:S(2)}) copy-start(bf16[2,64,640]{2,1,0:T(8,128)(2,1)S(1)} %collective-permute-done.12) | copy-start | bytes 491524
  76.8 1.9 copy-start.6
  76.8 1.4 copy-start.14
  78.1 1.1 slice-start
  78.2 2.7 copy-start.16
  78.7 17.6 %collective-permute-start.20 = (bf16[2,2,256,640]{3,2,1,0:T(8,128)(2,1)S(1)}, bf16[2,2,256,640]{3,2,1,0:T(8,128)(2,1)S(1)}, u32[]{:S(2)}, u32[]{:S(2)}) collective-permute-start(bf16[2,2,256,640]{3,2,1,0:T(8,128)(2,1)S(1)} %slice.47), channel_id=1, source_target_pairs={{0,12},{1,13},{2,14},{3,15},{4,0},{5,1},{6,2},{7,3},{8,4},{9,5},{1... | collective-permute-start | bytes 3932168 | tf_op jit(solution)/shard_map/ppermute | solution.py:309
  79.4 17.7 %collective-permute-start.19 = (bf16[2,2,256,640]{3,2,1,0:T(8,128)(2,1)S(1)}, bf16[2,2,256,640]{3,2,1,0:T(8,128)(2,1)S(1)}, u32[]{:S(2)}, u32[]{:S(2)}) collective-permute-start(bf16[2,2,256,640]{3,2,1,0:T(8,128)(2,1)S(1)} %pad_maximum_fusion.4), channel_id=1, source_target_pairs={{0,4},{1,5},{2,6},{3,7},{4,8},{5,9},{6,10},{7,11},{8,12},{9,13},{1... | collective-permute-start | bytes 3932168 | tf_op jit(solution)/shard_map/ppermute | solution.py:309
  80.9 1.2 collective-permute-start.9
  81.0 25.3 %collective-permute-start.16 = (bf16[640,640]{1,0:T(8,128)(2,1)}, bf16[640,640]{1,0:T(8,128)(2,1)S(1)}, u32[]{:S(2)}, u32[]{:S(2)}) collective-permute-start(bf16[640,640]{1,0:T(8,128)(2,1)} %bitcast.17), channel_id=1, source_target_pairs={{0,16},{16,0},{32,48},{48,32},{64,80},{80,64},{96,112},{112,96},{1... | collective-permute-start | bytes 2457608 | tf_op jit(solution)/shard_map/ppermute | solution.py:329
  82.1 24.2 %collective-permute-start.17 = (bf16[640,640]{1,0:T(8,128)(2,1)}, bf16[640,640]{1,0:T(8,128)(2,1)S(1)}, u32[]{:S(2)}, u32[]{:S(2)}) collective-permute-start(bf16[640,640]{1,0:T(8,128)(2,1)} %bitcast.16), channel_id=1, source_target_pairs={{0,16},{16,0},{32,48},{48,32},{64,80},{80,64},{96,112},{112,96},{1... | collective-permute-start | bytes 2457608 | tf_op jit(solution)/shard_map/ppermute | solution.py:329
  94.4 13.1 %copy-start.8 = (bf16[1,640,640]{2,1,0:T(8,128)(2,1)S(1)}, bf16[1,640,640]{2,1,0:T(8,128)(2,1)}, u32[]{:S(2)}) copy-start(bf16[1,640,640]{2,1,0:T(8,128)(2,1)} %param.19) | copy-start | bytes 2457604
  94.4 13.1 %copy-start.10 = (bf16[1,640,640]{2,1,0:T(8,128)(2,1)S(1)}, bf16[1,640,640]{2,1,0:T(8,128)(2,1)}, u32[]{:S(2)}) copy-start(bf16[1,640,640]{2,1,0:T(8,128)(2,1)} %param.20) | copy-start | bytes 2457604
  94.4 13.1 %copy-start.12 = (bf16[640,640]{1,0:T(8,128)(2,1)S(1)}, bf16[640,640]{1,0:T(8,128)(2,1)}, u32[]{:S(2)}) copy-start(bf16[640,640]{1,0:T(8,128)(2,1)} %copy-done.11) | copy-start | bytes 2457604
  94.5 13.1 %copy-start.20 = (bf16[2,64,640]{2,1,0:T(8,128)(2,1)S(1)}, bf16[2,64,640]{2,1,0:T(8,128)(2,1)}, u32[]{:S(2)}) copy-start(bf16[2,64,640]{2,1,0:T(8,128)(2,1)} %copy-done.19) | copy-start | bytes 491524
  94.5 13.1 %copy-start.22 = (bf16[2,64,640]{2,1,0:T(8,128)(2,1)S(1)}, bf16[2,64,640]{2,1,0:T(8,128)(2,1)}, u32[]{:S(2)}) copy-start(bf16[2,64,640]{2,1,0:T(8,128)(2,1)} %copy-done.21) | copy-start | bytes 491524
  106.3 0.9 copy-start.17
  106.3 1.2 copy-start.18
  141.0 12.3 %collective-permute-start = (bf16[256,640]{1,0:T(8,128)(2,1)S(1)}, bf16[256,640]{1,0:T(8,128)(2,1)S(1)}, u32[]{:S(2)}, u32[]{:S(2)}) collective-permute-start(bf16[256,640]{1,0:T(8,128)(2,1)S(1)} %param.1), channel_id=1, source_target_pairs={{0,32},{16,48},{32,64},{48,80},{64,96},{80,112},{1,33},{17,49},{33... | collective-permute-start | bytes 983048 | tf_op jit(solution)/shard_map/while/body/eval_jaxpr/cond/branch_1_fun/ppermute | solution.py:381
  186.7 11.9 %collective-permute-start = (bf16[256,640]{1,0:T(8,128)(2,1)S(1)}, bf16[256,640]{1,0:T(8,128)(2,1)S(1)}, u32[]{:S(2)}, u32[]{:S(2)}) collective-permute-start(bf16[256,640]{1,0:T(8,128)(2,1)S(1)} %param.1), channel_id=1, source_target_pairs={{0,32},{16,48},{32,64},{48,80},{64,96},{80,112},{1,33},{17,49},{33... | collective-permute-start | bytes 983048 | tf_op jit(solution)/shard_map/while/body/eval_jaxpr/cond/branch_1_fun/ppermute | solution.py:381
  232.1 11.3 %collective-permute-start = (bf16[256,640]{1,0:T(8,128)(2,1)S(1)}, bf16[256,640]{1,0:T(8,128)(2,1)S(1)}, u32[]{:S(2)}, u32[]{:S(2)}) collective-permute-start(bf16[256,640]{1,0:T(8,128)(2,1)S(1)} %param.1), channel_id=1, source_target_pairs={{0,32},{16,48},{32,64},{48,80},{64,96},{80,112},{1,33},{17,49},{33... | collective-permute-start | bytes 983048 | tf_op jit(solution)/shard_map/while/body/eval_jaxpr/cond/branch_1_fun/ppermute | solution.py:381
  277.0 12.1 %copy-start.1 = (bf16[2,4,64,640]{3,2,1,0:T(8,128)(2,1)S(1)}, bf16[2,4,64,640]{3,2,1,0:T(8,128)(2,1)}, u32[]{:S(2)}) copy-start(bf16[2,4,64,640]{3,2,1,0:T(8,128)(2,1)} %param.14) | copy-start | bytes 1966084
  277.1 1.5 collective-permute-start.21
  278.6 2.7 collective-permute-start.22
  279.3 2.0 collective-permute-start.24
  280.0 8.4 %collective-permute-start.23 = (bf16[2,4,8,640]{3,2,1,0:T(8,128)(2,1)S(1)}, bf16[2,4,8,640]{3,2,1,0:T(8,128)(2,1)S(1)}, u32[]{:S(2)}, u32[]{:S(2)}) collective-permute-start(bf16[2,4,8,640]{3,2,1,0:T(8,128)(2,1)S(1)} %get-tuple-element.419), channel_id=1, source_target_pairs={{96,32},{112,48},{97,33},{113,49},{98,34},{114,50},{99,35},{115,51... | collective-permute-start | bytes 245768 | tf_op jit(solution)/shard_map/ppermute | solution.py:394

commit v3 on v2

--- a/solution.py
+++ b/solution.py
@@ -103,11 +103,11 @@
         cost_estimate=pl.CostEstimate(
             flops=8 * cells * C * C, transcendentals=0, bytes_accessed=12 * cells * C
         ),
-        name="stale_%d" % (count * size),
+        name="stale",
     )(*pieces, gains, wk, wv)
 
 
-STORES = 3
+STORES = 4
 NAMES = ("query", "key", "value", "out", "conv")
 
 
@@ -342,38 +342,35 @@
     )
     mine = jnp.stack(exchanged(mine))
     raw, edges = mine[:, :CELLS], mine[:, CELLS:].reshape(2, 2, W, C)
-    raw, first_sent, norm_attn = lax.optimization_barrier(
-        (raw, {name: own[name] for name in ("key", "value")}, norm_attn)
-    )
-    other = {name: swap(value) for name, value in first_sent.items()}
     gains = jnp.concatenate(ordered(norm_attn, swap(norm_attn)), 0)
+    conv_gains = jnp.concatenate(ordered(norm_conv, swap(norm_conv)), 0)
+    raw, sent = lax.optimization_barrier(
+        (raw, {name: own[name] for name in ("key", "value")})
+    )
+    other = {name: swap(value) for name, value in sent.items()}
     wk, wv = [jnp.stack(ordered(own[name], other[name])) for name in ("key", "value")]
     back, ahead = ring_near(raw, 0)
-    own_back, own_ahead = ring_near(raw, 1)
     far = ring_far(back, ahead, 0)
-    rest = jnp.stack([back, jnp.concatenate(far, 0), ahead])
-    first = jnp.stack([raw, own_back, own_ahead])
-    rest, first, sent, edges, norm_conv = lax.optimization_barrier(
-        (rest, first, {name: own[name] for name in ("query", "out", "conv")}, edges, norm_conv)
-    )
-    back, ahead = ring_near(rest, 1)
+    back, ahead, far, wk, wv, gains, edges, conv_sent = lax.optimization_barrier(
+        (back, ahead, far, wk, wv, gains, edges, own["conv"])
+    )
+    other["conv"] = swap(conv_sent)
+    row = jnp.stack([raw, back]), jnp.stack([jnp.concatenate(far, 0), ahead])
+    first = turned(row[0], 1, 1), turned(row[1], 1, -1)
+    second = turned(row[1], 1, 1), turned(row[0], 1, -1)
     upper = lax.ppermute(edges[:, 1], "patch", [(i, i + 1) for i in range(15)])
     lower = lax.ppermute(edges[:, 0], "patch", [(i + 1, i) for i in range(15)])
-    stored = stale_call([first, rest], gains, wk, wv)
-    back, ahead, upper, lower, stored = lax.optimization_barrier(
-        (back, ahead, upper, lower, stored)
-    )
-    far = (
-        turned(jnp.concatenate([first[1:2], back[:1]], 0), 1, 1),
-        turned(ahead[1:], 1, -1),
-    )
-
+    stored = [stale_call(row, gains, wk, wv)]
+    first, upper, lower, stored = lax.optimization_barrier((first, upper, lower, stored))
+    far = turned(first[0], 1, 1), turned(first[1], 1, -1)
+    stored.append(stale_call(first, gains, wk, wv))
+    second, stored, sent = lax.optimization_barrier(
+        (second, stored, {name: own[name] for name in ("query", "out")})
+    )
     other |= {name: swap(value) for name, value in sent.items()}
-    conv_gains = jnp.concatenate(ordered(norm_conv, swap(norm_conv)), 0)
+    stored += [stale_call(pieces, gains, wk, wv) for pieces in (second, far)]
 
     x = lax.dynamic_index_in_dim(latent, core, 0, keepdims=False).reshape(CELLS, C)
-    stored = [stored] + [stale_call(pieces, gains, wk, wv) for pieces in ([back, ahead], far)]
-
     def two_blocks(x):
         return block_call(x, gains, conv_gains, upper, lower, own, other, stored)
 

time: 290 us -> 283 us (0.976)
  waiting for transfers between devices: 76.9 us -> 59.4 us
  Pallas kernels: 167 us -> 175 us
  local copies, waits for them, and re-layouts: 5.89 us -> 1.33 us
  starting transfers between devices: 32.6 us -> 36.5 us
    ppermute x10, waiting for transfers between devices: 21.9 us -> 10.9 us  [turned(): return lax.ppermute(value, ('segment', 'patch'), pairs)]
    ppermute x1, waiting for transfers between devices: 0.01 us -> 11 us  [shards(): lower = lax.ppermute(edges[:, 0], 'patch', [(i + 1, i) for i in range(15)])]
    ppermute x9, waiting for transfers between devices: 14.8 us -> 5.71 us  [swap(): return lax.ppermute(value, 'segment', sibling)]
    ppermute x1, waiting for transfers between devices: 7.82 us -> 0.66 us  [shards(): upper = lax.ppermute(edges[:, 1], 'patch', [(i, i + 1) for i in range(15)])]
    pallas_call x4, Pallas kernels: 134 us -> 138 us  [block_call(): pl.pallas_call(block_kernel, out_shape=jax.ShapeDtypeStruct((CELLS, C), B...]
    unnamed x47 -> x21, local copies, waits for them, and re-layouts: 5.24 us -> 0.96 us
    pallas_call x3 -> x4, Pallas kernels: 33.5 us -> 37.1 us  [stale_call(): pl.pallas_call(functools.partial(stale_kernel, count), grid=(2, count, st...]
  transfers between devices with their start and end apart: 27 -> 27, of which waited for: 15 -> 13; matrix products, arithmetic and copies ran while one was open for 1% -> 1% of each run, Pallas kernels for 12% -> 13%
where the time goes in v3:
time: 283 us; the launch traced here: 280 us
  Pallas kernels  175 us (62%)
  waiting for transfers between devices  59.4 us (21%)
  starting transfers between devices  36.5 us (13%)
  other arithmetic  7.52 us (3%)
    pallas_call x4, Pallas kernels, block_call(): pl.pallas_call(block_kernel, out_shape=jax.ShapeDtypeStruct((CELLS, C), B...  138 us
    pallas_call x4, Pallas kernels, stale_call(): pl.pallas_call(functools.partial(stale_kernel, count), grid=(2, count, st...  37.1 us
    ppermute x3, waiting for transfers between devices, hop(): return lax.ppermute(x, 'segment', [(i, i + 2) for i in range(6)])  24.1 us
    ppermute x10, starting transfers between devices, turned(): return lax.ppermute(value, ('segment', 'patch'), pairs)  15 us
    ppermute x1, waiting for transfers between devices, shards(): lower = lax.ppermute(edges[:, 0], 'patch', [(i + 1, i) for i in range(15)])  11 us
    ppermute x10, waiting for transfers between devices, turned(): return lax.ppermute(value, ('segment', 'patch'), pairs)  10.9 us
    ppermute x3, starting transfers between devices, hop(): return lax.ppermute(x, 'segment', [(i, i + 2) for i in range(6)])  10.2 us
    ppermute x3, waiting for transfers between devices, shards(): lax.ppermute(both[:, :, (3 + d) % 4], 'segment', [(6, (6 + 2 * d) % 8), (...  7.11 us
  transfers between devices with their start and end apart: 27, of which 13 were waited for; matrix products, arithmetic and copies ran while one was open for 1% of the time, Pallas kernels for 13%

profile of v3, /device:TPU:18, one launch (start us, length us, event | category | flops | bytes accessed | tf_op | source)
XLA Modules:
  0.0 280.3 jit_solution(6479799947345330953)
XLA Ops:
  0.0 2.0 fusion.2
  2.0 0.0 copy-start.8
  2.0 0.0 copy-start.7
  2.0 2.2 collective-permute-done.1
  4.2 1.2 select_bitcast_fusion.4
  5.4 0.1 fusion
  5.5 0.2 collective-permute-start.6
  5.7 0.4 collective-permute-start.7
  6.1 4.0 %collective-permute-start.3 = (bf16[2,256,640]{2,1,0:T(8,128)(2,1)S(1)}, bf16[2,256,640]{2,1,0:T(8,128)(2,1)S(1)}, u32[]{:S(2)}, u32[]{:S(2)}) collective-permute-start(bf16[2,256,640]{2,1,0:T(8,128)(2,1)S(1)} %fusion), channel_id=1, source_target_pairs={{0,3},{1,0},{2,1},{3,2},{4,7},{5,4},{6,5},{7,6},{8,11},{9,8},{10,9... | collective-permute-start | bytes 1966088 | tf_op jit(solution)/shard_map/ppermute | solution.py:309
  10.1 0.0 collective-permute-start.8
  10.1 1.2 collective-permute-done.8
  11.3 0.2 collective-permute-start.9
  11.5 1.0 collective-permute-done.9
  12.5 5.7 %collective-permute-done.3 = bf16[2,256,640]{2,1,0:T(8,128)(2,1)S(1)} collective-permute-done((bf16[2,256,640]{2,1,0:T(8,128)(2,1)S(1)}, bf16[2,256,640]{2,1,0:T(8,128)(2,1)S(1)}, u32[]{:S(2)}, u32[]{:S(2)}) %collective-permute-start.3) | collective-permute-done | bytes 655392 | tf_op jit(solution)/shard_map/ppermute | solution.py:309
  18.3 3.8 %collective-permute-start.5 = (bf16[1,256,640]{2,1,0:T(8,128)(2,1)S(1)}, bf16[1,256,640]{2,1,0:T(8,128)(2,1)S(1)}, u32[]{:S(2)}, u32[]{:S(2)}) collective-permute-start(bf16[1,256,640]{2,1,0:T(8,128)(2,1)S(1)} %slice.43), channel_id=1, source_target_pairs={{0,3},{1,0},{2,1},{3,2},{4,7},{5,4},{6,5},{7,6},{8,11},{9,8},{10,9... | collective-permute-start | bytes 983048 | tf_op jit(solution)/shard_map/ppermute | solution.py:309
  22.1 0.1 collective-permute-start.4
  22.2 0.0 collective-permute-done.7
  22.2 0.3 select_bitcast_fusion.1
  22.5 1.3 pad_maximum_fusion.1.refs_4_
  23.9 1.4 pad_maximum_fusion.refs_3_
  25.3 1.3 collective-permute-done.5
  26.6 3.8 %collective-permute-done.4 = bf16[1,256,640]{2,1,0:T(8,128)(2,1)S(1)} collective-permute-done((bf16[1,256,640]{2,1,0:T(8,128)(2,1)S(1)}, bf16[1,256,640]{2,1,0:T(8,128)(2,1)S(1)}, u32[]{:S(2)}, u32[]{:S(2)}) %collective-permute-start.4) | collective-permute-done | bytes 327712 | tf_op jit(solution)/shard_map/ppermute | solution.py:309
  30.4 0.1 maximum_bitcast_fusion
  30.5 0.1 pad_maximum_fusion.3.refs_1_
  30.6 0.5 collective-permute-start.11
  31.2 0.1 pad_maximum_fusion.2.refs_0_
  31.3 1.6 collective-permute-start.10
  33.0 1.9 collective-permute-start.13
  34.9 3.9 %collective-permute-start.12 = (bf16[2,64,640]{2,1,0:T(8,128)(2,1)S(1)}, bf16[2,64,640]{2,1,0:T(8,128)(2,1)}, u32[]{:S(2)}, u32[]{:S(2)}) collective-permute-start(bf16[2,64,640]{2,1,0:T(8,128)(2,1)S(1)} %get-tuple-element.477), channel_id=1, source_target_pairs={{0,1},{1,2},{2,3},{3,4},{4,5},{5,6},{6,7},{7,8},{8,9},{9,10},{10,1... | collective-permute-start | bytes 491528 | tf_op jit(solution)/shard_map/ppermute | solution.py:361
  38.8 11.0 %collective-permute-done.13 = bf16[2,64,640]{2,1,0:T(8,128)(2,1)} collective-permute-done((bf16[2,64,640]{2,1,0:T(8,128)(2,1)S(1)}, bf16[2,64,640]{2,1,0:T(8,128)(2,1)}, u32[]{:S(2)}, u32[]{:S(2)}) %collective-permute-start.13) | collective-permute-done | bytes 163872 | tf_op jit(solution)/shard_map/ppermute | solution.py:362
  49.8 1.6 collective-permute-start.14
  51.4 0.7 collective-permute-done.12
  52.0 1.3 collective-permute-start.15
  53.4 9.2 %stale.4 = (bf16[2,5,1024,128]{3,2,1,0:T(8,128)(2,1)}, bf16[2,5,128,1024]{3,2,1,0:T(8,128)(2,1)}) custom-call(bf16[2,2,256,640]{3,2,1,0:T(8,128)(2,1)S(1)} %pad_maximum_fusion.2.refs_0_, bf16[2,2,256,640]{3,2,1,0:T(8,128)(2,1)S(1)} %pad_maximum_fusion.3.refs_1_, f32[2,640]{1,0:T(2,128)S(1)} %pad_maximum_fusion.6.refs_2_, ...), custom_call_target="tpu_custom_call" | custom-call | flops 3355443200 | bytes 7864320 | tf_op jit(solution)/shard_map/stale/pallas_call | solution.py:79
  62.6 0.8 collective-permute-start.19
  63.4 1.3 collective-permute-start.20
  64.7 9.3 %stale.5 = (bf16[2,5,1024,128]{3,2,1,0:T(8,128)(2,1)}, bf16[2,5,128,1024]{3,2,1,0:T(8,128)(2,1)}) custom-call(bf16[2,2,256,640]{3,2,1,0:T(8,128)(2,1)S(1)} %collective-permute-done.10.refs_0_, bf16[2,2,256,640]{3,2,1,0:T(8,128)(2,1)S(1)} %collective-permute-done.11.refs_1_, f32[2,640]{1,0:T(2,128)S(1)} %pad_maximum_fusion.6.refs_2_, ...), custom_call_target="tpu_custom_call" | custom-call | flops 3355443200 | bytes 7864320 | tf_op jit(solution)/shard_map/stale/pallas_call | solution.py:79
  74.0 1.6 collective-permute-start.16
  75.6 0.3 collective-permute-start.17
  75.9 9.3 %stale.6 = (bf16[2,5,1024,128]{3,2,1,0:T(8,128)(2,1)}, bf16[2,5,128,1024]{3,2,1,0:T(8,128)(2,1)}) custom-call(bf16[2,2,256,640]{3,2,1,0:T(8,128)(2,1)S(1)} %collective-permute-done.14.refs_0_, bf16[2,2,256,640]{3,2,1,0:T(8,128)(2,1)S(1)} %collective-permute-done.15.refs_1_, f32[2,640]{1,0:T(2,128)S(1)} %pad_maximum_fusion.6.refs_2_, ...), custom_call_target="tpu_custom_call" | custom-call | flops 3355443200 | bytes 7864320 | tf_op jit(solution)/shard_map/stale/pallas_call | solution.py:79
  85.2 9.3 %stale.7 = (bf16[2,5,1024,128]{3,2,1,0:T(8,128)(2,1)}, bf16[2,5,128,1024]{3,2,1,0:T(8,128)(2,1)}) custom-call(bf16[2,2,256,640]{3,2,1,0:T(8,128)(2,1)S(1)} %collective-permute-done.19.refs_0_, bf16[2,2,256,640]{3,2,1,0:T(8,128)(2,1)S(1)} %collective-permute-done.20.refs_1_, f32[2,640]{1,0:T(2,128)S(1)} %pad_maximum_fusion.6.refs_2_, ...), custom_call_target="tpu_custom_call" | custom-call | flops 3355443200 | bytes 7864320 | tf_op jit(solution)/shard_map/stale/pallas_call | solution.py:79
  94.5 0.9 copy-done.9
  95.5 172.7 %while.13 = (s32[]{:T(128)}, bf16[256,640]{1,0:T(8,128)(2,1)S(1)}, f32[2,640]{1,0:T(2,128)S(1)}, f32[2,640]{1,0:T(2,128)S(1)}, bf16[2,64,640]{2,1,0:T(8,128)(2,1...) while((s32[]{:T(128)}, bf16[256,640]{1,0:T(8,128)(2,1)S(1)}, ...), condition=%wide.region_3.4_spmd, body=%wide.region_0.3_spmd.sunk | while | flops 25999998976 | bytes 46621728 | solution.py:383
  95.5 34.5 %blocks.5 = bf16[256,640]{1,0:T(8,128)(2,1)S(1)} custom-call(bf16[256,640]{1,0:T(8,128)(2,1)S(1)} %get-tuple-element.658.refs_0_, f32[2,640]{1,0:T(2,128)S(1)} %get-tuple-element.685.refs_1_, f32[2,640]{1,0:T(2,128)S(1)} %get-tuple-element.686.refs_2_, bf16[2,64,640]{2,1,0:T(8,128)(2,1)} %get-tuple-element.687.refs_3_, ...), custom_call_target="tpu_custom_call" | custom-call | flops 25999998976 | bytes 44000000 | tf_op jit(solution)/shard_map/while/body/eval_jaxpr/blocks/pallas_call | solution.py:258
  129.9 12.1 %conditional.2 = (bf16[256,640]{1,0:T(8,128)(2,1)S(1)}) conditional(s32[]{:T(128)} %convert_element_type.13, bf16[256,640]{1,0:T(8,128)(2,1)S(1)} %blocks.5, bf16[256,640]{1,0:T(8,128)(2,1)S(1)} %blocks.5), branch_computations={%region_1.1_spmd, %region_2.2_spmd} | conditional | bytes 1966128 | solution.py:381
  130.0 3.4 %collective-permute-start = (bf16[256,640]{1,0:T(8,128)(2,1)S(1)}, bf16[256,640]{1,0:T(8,128)(2,1)S(1)}, u32[]{:S(2)}, u32[]{:S(2)}) collective-permute-start(bf16[256,640]{1,0:T(8,128)(2,1)S(1)} %param.1), channel_id=1, source_target_pairs={{0,32},{16,48},{32,64},{48,80},{64,96},{80,112},{1,33},{17,49},{33... | collective-permute-start | bytes 983048 | tf_op jit(solution)/shard_map/while/body/eval_jaxpr/cond/branch_1_fun/ppermute | solution.py:378
  133.4 8.6 %collective-permute-done = bf16[256,640]{1,0:T(8,128)(2,1)S(1)} collective-permute-done((bf16[256,640]{1,0:T(8,128)(2,1)S(1)}, bf16[256,640]{1,0:T(8,128)(2,1)S(1)}, u32[]{:S(2)}, u32[]{:S(2)}) %collective-permute-start) | collective-permute-done | bytes 327712 | tf_op jit(solution)/shard_map/while/body/eval_jaxpr/cond/branch_1_fun/ppermute | solution.py:378
  142.0 34.5 %blocks.5 = bf16[256,640]{1,0:T(8,128)(2,1)S(1)} custom-call(bf16[256,640]{1,0:T(8,128)(2,1)S(1)} %get-tuple-element.658.refs_0_, f32[2,640]{1,0:T(2,128)S(1)} %get-tuple-element.685.refs_1_, f32[2,640]{1,0:T(2,128)S(1)} %get-tuple-element.686.refs_2_, bf16[2,64,640]{2,1,0:T(8,128)(2,1)} %get-tuple-element.687.refs_3_, ...), custom_call_target="tpu_custom_call" | custom-call | flops 25999998976 | bytes 44000000 | tf_op jit(solution)/shard_map/while/body/eval_jaxpr/blocks/pallas_call | solution.py:258
  176.5 11.5 %conditional.2 = (bf16[256,640]{1,0:T(8,128)(2,1)S(1)}) conditional(s32[]{:T(128)} %convert_element_type.13, bf16[256,640]{1,0:T(8,128)(2,1)S(1)} %blocks.5, bf16[256,640]{1,0:T(8,128)(2,1)S(1)} %blocks.5), branch_computations={%region_1.1_spmd, %region_2.2_spmd} | conditional | bytes 1966128 | solution.py:381
  176.6 3.4 %collective-permute-start = (bf16[256,640]{1,0:T(8,128)(2,1)S(1)}, bf16[256,640]{1,0:T(8,128)(2,1)S(1)}, u32[]{:S(2)}, u32[]{:S(2)}) collective-permute-start(bf16[256,640]{1,0:T(8,128)(2,1)S(1)} %param.1), channel_id=1, source_target_pairs={{0,32},{16,48},{32,64},{48,80},{64,96},{80,112},{1,33},{17,49},{33... | collective-permute-start | bytes 983048 | tf_op jit(solution)/shard_map/while/body/eval_jaxpr/cond/branch_1_fun/ppermute | solution.py:378
  180.0 8.1 %collective-permute-done = bf16[256,640]{1,0:T(8,128)(2,1)S(1)} collective-permute-done((bf16[256,640]{1,0:T(8,128)(2,1)S(1)}, bf16[256,640]{1,0:T(8,128)(2,1)S(1)}, u32[]{:S(2)}, u32[]{:S(2)}) %collective-permute-start) | collective-permute-done | bytes 327712 | tf_op jit(solution)/shard_map/while/body/eval_jaxpr/cond/branch_1_fun/ppermute | solution.py:378
  188.1 34.5 %blocks.5 = bf16[256,640]{1,0:T(8,128)(2,1)S(1)} custom-call(bf16[256,640]{1,0:T(8,128)(2,1)S(1)} %get-tuple-element.658.refs_0_, f32[2,640]{1,0:T(2,128)S(1)} %get-tuple-element.685.refs_1_, f32[2,640]{1,0:T(2,128)S(1)} %get-tuple-element.686.refs_2_, bf16[2,64,640]{2,1,0:T(8,128)(2,1)} %get-tuple-element.687.refs_3_, ...), custom_call_target="tpu_custom_call" | custom-call | flops 25999998976 | bytes 44000000 | tf_op jit(solution)/shard_map/while/body/eval_jaxpr/blocks/pallas_call | solution.py:258
  222.6 10.9 %conditional.2 = (bf16[256,640]{1,0:T(8,128)(2,1)S(1)}) conditional(s32[]{:T(128)} %convert_element_type.13, bf16[256,640]{1,0:T(8,128)(2,1)S(1)} %blocks.5, bf16[256,640]{1,0:T(8,128)(2,1)S(1)} %blocks.5), branch_computations={%region_1.1_spmd, %region_2.2_spmd} | conditional | bytes 1966128 | solution.py:381
  222.7 3.4 %collective-permute-start = (bf16[256,640]{1,0:T(8,128)(2,1)S(1)}, bf16[256,640]{1,0:T(8,128)(2,1)S(1)}, u32[]{:S(2)}, u32[]{:S(2)}) collective-permute-start(bf16[256,640]{1,0:T(8,128)(2,1)S(1)} %param.1), channel_id=1, source_target_pairs={{0,32},{16,48},{32,64},{48,80},{64,96},{80,112},{1,33},{17,49},{33... | collective-permute-start | bytes 983048 | tf_op jit(solution)/shard_map/while/body/eval_jaxpr/cond/branch_1_fun/ppermute | solution.py:378
  226.1 7.5 %collective-permute-done = bf16[256,640]{1,0:T(8,128)(2,1)S(1)} collective-permute-done((bf16[256,640]{1,0:T(8,128)(2,1)S(1)}, bf16[256,640]{1,0:T(8,128)(2,1)S(1)}, u32[]{:S(2)}, u32[]{:S(2)}) %collective-permute-start) | collective-permute-done | bytes 327712 | tf_op jit(solution)/shard_map/while/body/eval_jaxpr/cond/branch_1_fun/ppermute | solution.py:378
  233.6 34.5 %blocks.5 = bf16[256,640]{1,0:T(8,128)(2,1)S(1)} custom-call(bf16[256,640]{1,0:T(8,128)(2,1)S(1)} %get-tuple-element.658.refs_0_, f32[2,640]{1,0:T(2,128)S(1)} %get-tuple-element.685.refs_1_, f32[2,640]{1,0:T(2,128)S(1)} %get-tuple-element.686.refs_2_, bf16[2,64,640]{2,1,0:T(8,128)(2,1)} %get-tuple-element.687.refs_3_, ...), custom_call_target="tpu_custom_call" | custom-call | flops 25999998976 | bytes 44000000 | tf_op jit(solution)/shard_map/while/body/eval_jaxpr/blocks/pallas_call | solution.py:258
  268.2 0.0 copy-start.1
  268.3 0.1 collective-permute-start.21
  268.4 1.4 collective-permute-done.21
  269.8 0.7 collective-permute-start.22
  270.5 0.7 collective-permute-start.24
  271.2 1.3 collective-permute-start.23
  272.5 7.1 %collective-permute-done.23 = bf16[2,4,8,640]{3,2,1,0:T(8,128)(2,1)S(1)} collective-permute-done((bf16[2,4,8,640]{3,2,1,0:T(8,128)(2,1)S(1)}, bf16[2,4,8,640]{3,2,1,0:T(8,128)(2,1)S(1)}, u32[]{:S(2)}, u32[]{:S(2)}) %collective-permute-start.23) | collective-permute-done | bytes 81952 | tf_op jit(solution)/shard_map/ppermute | solution.py:391
  279.6 0.7 fusion.13
  (52 shorter events, 0.6 us)
Async XLA Ops:
  0.0 75.9 %copy-start = (bf16[2,4,64,640]{3,2,1,0:T(8,128)(2,1)S(1)}, bf16[2,4,64,640]{3,2,1,0:T(8,128)(2,1)}, u32[]{:S(2)}) copy-start(bf16[2,4,64,640]{3,2,1,0:T(8,128)(2,1)} %param.14) | copy-start | bytes 1966084
  0.0 4.2 %copy-start.3 = (bf16[1,2,2,64,640]{4,3,2,1,0:T(8,128)(2,1)S(1)}, bf16[1,2,2,64,640]{4,3,2,1,0:T(8,128)(2,1)}, u32[]{:S(2)}) copy-start(bf16[1,2,2,64,640]{4,3,2,1,0:T(8,128)(2,1)} %param.16) | copy-start | bytes 983044
  0.0 4.2 %copy-start.2 = (bf16[1,2,4,64,640]{4,3,2,1,0:T(8,128)(2,1)S(1)}, bf16[1,2,4,64,640]{4,3,2,1,0:T(8,128)(2,1)}, u32[]{:S(2)}) copy-start(bf16[1,2,4,64,640]{4,3,2,1,0:T(8,128)(2,1)} %param.15) | copy-start | bytes 1966084
  2.0 2.2 collective-permute-start.1
  2.0 3.5 %copy-start.4 = (bf16[1,640,640]{2,1,0:T(8,128)(2,1)S(1)}, bf16[1,640,640]{2,1,0:T(8,128)(2,1)}, u32[]{:S(2)}) copy-start(bf16[1,640,640]{2,1,0:T(8,128)(2,1)} %param.19) | copy-start | bytes 2457604
  2.0 3.7 %copy-start.5 = (bf16[1,640,640]{2,1,0:T(8,128)(2,1)S(1)}, bf16[1,640,640]{2,1,0:T(8,128)(2,1)}, u32[]{:S(2)}) copy-start(bf16[1,640,640]{2,1,0:T(8,128)(2,1)} %param.20) | copy-start | bytes 2457604
  2.0 8.1 %copy-start.8 = (f32[1,640]{1,0:T(1,128)S(1)}, f32[1,640]{1,0:T(1,128)}, u32[]{:S(2)}) copy-start(f32[1,640]{1,0:T(1,128)} %param.17) | copy-start | bytes 7684
  2.0 9.3 %copy-start.7 = (f32[1,640]{1,0:T(1,128)S(1)}, f32[1,640]{1,0:T(1,128)}, u32[]{:S(2)}) copy-start(f32[1,640]{1,0:T(1,128)} %param.22) | copy-start | bytes 7684
  5.5 16.7 %collective-permute-start.6 = (bf16[640,640]{1,0:T(8,128)(2,1)S(1)}, bf16[640,640]{1,0:T(8,128)(2,1)S(1)}, u32[]{:S(2)}, u32[]{:S(2)}) collective-permute-start(bf16[640,640]{1,0:T(8,128)(2,1)S(1)} %bitcast.84), channel_id=1, source_target_pairs={{0,16},{16,0},{32,48},{48,32},{64,80},{80,64},{96,112},{112,96},{1... | collective-permute-start | bytes 2457608 | tf_op jit(solution)/shard_map/ppermute | solution.py:329
  5.7 16.4 %collective-permute-start.7 = (bf16[640,640]{1,0:T(8,128)(2,1)S(1)}, bf16[640,640]{1,0:T(8,128)(2,1)S(1)}, u32[]{:S(2)}, u32[]{:S(2)}) collective-permute-start(bf16[640,640]{1,0:T(8,128)(2,1)S(1)} %bitcast.86), channel_id=1, source_target_pairs={{0,16},{16,0},{32,48},{48,32},{64,80},{80,64},{96,112},{112,96},{1... | collective-permute-start | bytes 2457608 | tf_op jit(solution)/shard_map/ppermute | solution.py:329
  6.1 12.1 %collective-permute-start.3 = (bf16[2,256,640]{2,1,0:T(8,128)(2,1)S(1)}, bf16[2,256,640]{2,1,0:T(8,128)(2,1)S(1)}, u32[]{:S(2)}, u32[]{:S(2)}) collective-permute-start(bf16[2,256,640]{2,1,0:T(8,128)(2,1)S(1)} %fusion), channel_id=1, source_target_pairs={{0,3},{1,0},{2,1},{3,2},{4,7},{5,4},{6,5},{7,6},{8,11},{9,8},{10,9... | collective-permute-start | bytes 1966088 | tf_op jit(solution)/shard_map/ppermute | solution.py:309
  10.1 11.9 %collective-permute-start.2 = (bf16[2,256,640]{2,1,0:T(8,128)(2,1)S(1)}, bf16[2,256,640]{2,1,0:T(8,128)(2,1)S(1)}, u32[]{:S(2)}, u32[]{:S(2)}) collective-permute-start(bf16[2,256,640]{2,1,0:T(8,128)(2,1)S(1)} %fusion), channel_id=1, source_target_pairs={{0,1},{1,2},{2,3},{3,0},{4,5},{5,6},{6,7},{7,4},{8,9},{9,10},{10,1... | collective-permute-start | bytes 1966088 | tf_op jit(solution)/shard_map/ppermute | solution.py:309
  10.1 1.2 collective-permute-start.8
  11.3 1.2 collective-permute-start.9
  18.3 8.4 %collective-permute-start.5 = (bf16[1,256,640]{2,1,0:T(8,128)(2,1)S(1)}, bf16[1,256,640]{2,1,0:T(8,128)(2,1)S(1)}, u32[]{:S(2)}, u32[]{:S(2)}) collective-permute-start(bf16[1,256,640]{2,1,0:T(8,128)(2,1)S(1)} %slice.43), channel_id=1, source_target_pairs={{0,3},{1,0},{2,1},{3,2},{4,7},{5,4},{6,5},{7,6},{8,11},{9,8},{10,9... | collective-permute-start | bytes 983048 | tf_op jit(solution)/shard_map/ppermute | solution.py:309
  22.1 8.4 %collective-permute-start.4 = (bf16[1,256,640]{2,1,0:T(8,128)(2,1)S(1)}, bf16[1,256,640]{2,1,0:T(8,128)(2,1)S(1)}, u32[]{:S(2)}, u32[]{:S(2)}) collective-permute-start(bf16[1,256,640]{2,1,0:T(8,128)(2,1)S(1)} %slice.42), channel_id=1, source_target_pairs={{0,1},{1,2},{2,3},{3,0},{4,5},{5,6},{6,7},{7,4},{8,9},{9,10},{10,1... | collective-permute-start | bytes 983048 | tf_op jit(solution)/shard_map/ppermute | solution.py:309
  22.2 1.7 copy-start.6
  30.4 64.1 %collective-permute-start.18 = (bf16[9,640,640]{2,1,0:T(8,128)(2,1)}, bf16[9,640,640]{2,1,0:T(8,128)(2,1)}, u32[]{:S(2)}, u32[]{:S(2)}) collective-permute-start(bf16[9,640,640]{2,1,0:T(8,128)(2,1)} %bitcast.14), channel_id=1, source_target_pairs={{0,16},{16,0},{32,48},{48,32},{64,80},{80,64},{96,112},{112,96},{1... | collective-permute-start | bytes 22118408 | tf_op jit(solution)/shard_map/ppermute | solution.py:329
  30.6 32.0 %collective-permute-start.11 = (bf16[2,2,256,640]{3,2,1,0:T(8,128)(2,1)S(1)}, bf16[2,2,256,640]{3,2,1,0:T(8,128)(2,1)S(1)}, u32[]{:S(2)}, u32[]{:S(2)}) collective-permute-start(bf16[2,2,256,640]{3,2,1,0:T(8,128)(2,1)S(1)} %pad_maximum_fusion.3.refs_1_), channel_id=1, source_target_pairs={{0,12},{1,13},{2,14},{3,15},{4,0},{5,1},{6,2},{7,3},{8,4},{9,5},{1... | collective-permute-start | bytes 3932168 | tf_op jit(solution)/shard_map/ppermute | solution.py:309
  31.3 31.3 %collective-permute-start.10 = (bf16[2,2,256,640]{3,2,1,0:T(8,128)(2,1)S(1)}, bf16[2,2,256,640]{3,2,1,0:T(8,128)(2,1)S(1)}, u32[]{:S(2)}, u32[]{:S(2)}) collective-permute-start(bf16[2,2,256,640]{3,2,1,0:T(8,128)(2,1)S(1)} %pad_maximum_fusion.2.refs_0_), channel_id=1, source_target_pairs={{0,4},{1,5},{2,6},{3,7},{4,8},{5,9},{6,10},{7,11},{8,12},{9,13},{1... | collective-permute-start | bytes 3932168 | tf_op jit(solution)/shard_map/ppermute | solution.py:309
  33.0 16.8 %collective-permute-start.13 = (bf16[2,64,640]{2,1,0:T(8,128)(2,1)S(1)}, bf16[2,64,640]{2,1,0:T(8,128)(2,1)}, u32[]{:S(2)}, u32[]{:S(2)}) collective-permute-start(bf16[2,64,640]{2,1,0:T(8,128)(2,1)S(1)} %get-tuple-element.476), channel_id=1, source_target_pairs={{1,0},{2,1},{3,2},{4,3},{5,4},{6,5},{7,6},{8,7},{9,8},{10,9},{11,1... | collective-permute-start | bytes 491528 | tf_op jit(solution)/shard_map/ppermute | solution.py:362
  34.9 17.1 %collective-permute-start.12 = (bf16[2,64,640]{2,1,0:T(8,128)(2,1)S(1)}, bf16[2,64,640]{2,1,0:T(8,128)(2,1)}, u32[]{:S(2)}, u32[]{:S(2)}) collective-permute-start(bf16[2,64,640]{2,1,0:T(8,128)(2,1)S(1)} %get-tuple-element.477), channel_id=1, source_target_pairs={{0,1},{1,2},{2,3},{3,4},{4,5},{5,6},{6,7},{7,8},{8,9},{9,10},{10,1... | collective-permute-start | bytes 491528 | tf_op jit(solution)/shard_map/ppermute | solution.py:361
  49.8 24.2 %collective-permute-start.14 = (bf16[2,2,256,640]{3,2,1,0:T(8,128)(2,1)S(1)}, bf16[2,2,256,640]{3,2,1,0:T(8,128)(2,1)S(1)}, u32[]{:S(2)}, u32[]{:S(2)}) collective-permute-start(bf16[2,2,256,640]{3,2,1,0:T(8,128)(2,1)S(1)} %pad_maximum_fusion.3.refs_1_), channel_id=1, source_target_pairs={{0,4},{1,5},{2,6},{3,7},{4,8},{5,9},{6,10},{7,11},{8,12},{9,13},{1... | collective-permute-start | bytes 3932168 | tf_op jit(solution)/shard_map/ppermute | solution.py:309
  52.0 21.9 %collective-permute-start.15 = (bf16[2,2,256,640]{3,2,1,0:T(8,128)(2,1)S(1)}, bf16[2,2,256,640]{3,2,1,0:T(8,128)(2,1)S(1)}, u32[]{:S(2)}, u32[]{:S(2)}) collective-permute-start(bf16[2,2,256,640]{3,2,1,0:T(8,128)(2,1)S(1)} %pad_maximum_fusion.2.refs_0_), channel_id=1, source_target_pairs={{0,12},{1,13},{2,14},{3,15},{4,0},{5,1},{6,2},{7,3},{8,4},{9,5},{1... | collective-permute-start | bytes 3932168 | tf_op jit(solution)/shard_map/ppermute | solution.py:309
  62.6 22.6 %collective-permute-start.19 = (bf16[2,2,256,640]{3,2,1,0:T(8,128)(2,1)S(1)}, bf16[2,2,256,640]{3,2,1,0:T(8,128)(2,1)S(1)}, u32[]{:S(2)}, u32[]{:S(2)}) collective-permute-start(bf16[2,2,256,640]{3,2,1,0:T(8,128)(2,1)S(1)} %collective-permute-done.10.refs_0_), channel_id=1, source_target_pairs={{0,4},{1,5},{2,6},{3,7},{4,8},{5,9},{6,10},{7,11},{8,12},{9,13},{1... | collective-permute-start | bytes 3932168 | tf_op jit(solution)/shard_map/ppermute | solution.py:309
  63.4 21.9 %collective-permute-start.20 = (bf16[2,2,256,640]{3,2,1,0:T(8,128)(2,1)S(1)}, bf16[2,2,256,640]{3,2,1,0:T(8,128)(2,1)S(1)}, u32[]{:S(2)}, u32[]{:S(2)}) collective-permute-start(bf16[2,2,256,640]{3,2,1,0:T(8,128)(2,1)S(1)} %collective-permute-done.11.refs_1_), channel_id=1, source_target_pairs={{0,12},{1,13},{2,14},{3,15},{4,0},{5,1},{6,2},{7,3},{8,4},{9,5},{1... | collective-permute-start | bytes 3932168 | tf_op jit(solution)/shard_map/ppermute | solution.py:309
  74.0 20.5 %collective-permute-start.16 = (bf16[640,640]{1,0:T(8,128)(2,1)}, bf16[640,640]{1,0:T(8,128)(2,1)}, u32[]{:S(2)}, u32[]{:S(2)}) collective-permute-start(bf16[640,640]{1,0:T(8,128)(2,1)} %bitcast.21), channel_id=1, source_target_pairs={{0,16},{16,0},{32,48},{48,32},{64,80},{80,64},{96,112},{112,96},{1... | collective-permute-start | bytes 2457608 | tf_op jit(solution)/shard_map/ppermute | solution.py:329
  75.6 18.9 %collective-permute-start.17 = (bf16[640,640]{1,0:T(8,128)(2,1)}, bf16[640,640]{1,0:T(8,128)(2,1)S(1)}, u32[]{:S(2)}, u32[]{:S(2)}) collective-permute-start(bf16[640,640]{1,0:T(8,128)(2,1)} %bitcast.22), channel_id=1, source_target_pairs={{0,16},{16,0},{32,48},{48,32},{64,80},{80,64},{96,112},{112,96},{1... | collective-permute-start | bytes 2457608 | tf_op jit(solution)/shard_map/ppermute | solution.py:329
  94.5 0.9 copy-start.9
  130.0 12.0 %collective-permute-start = (bf16[256,640]{1,0:T(8,128)(2,1)S(1)}, bf16[256,640]{1,0:T(8,128)(2,1)S(1)}, u32[]{:S(2)}, u32[]{:S(2)}) collective-permute-start(bf16[256,640]{1,0:T(8,128)(2,1)S(1)} %param.1), channel_id=1, source_target_pairs={{0,32},{16,48},{32,64},{48,80},{64,96},{80,112},{1,33},{17,49},{33... | collective-permute-start | bytes 983048 | tf_op jit(solution)/shard_map/while/body/eval_jaxpr/cond/branch_1_fun/ppermute | solution.py:378
  176.6 11.5 %collective-permute-start = (bf16[256,640]{1,0:T(8,128)(2,1)S(1)}, bf16[256,640]{1,0:T(8,128)(2,1)S(1)}, u32[]{:S(2)}, u32[]{:S(2)}) collective-permute-start(bf16[256,640]{1,0:T(8,128)(2,1)S(1)} %param.1), channel_id=1, source_target_pairs={{0,32},{16,48},{32,64},{48,80},{64,96},{80,112},{1,33},{17,49},{33... | collective-permute-start | bytes 983048 | tf_op jit(solution)/shard_map/while/body/eval_jaxpr/cond/branch_1_fun/ppermute | solution.py:378
  222.7 10.9 %collective-permute-start = (bf16[256,640]{1,0:T(8,128)(2,1)S(1)}, bf16[256,640]{1,0:T(8,128)(2,1)S(1)}, u32[]{:S(2)}, u32[]{:S(2)}) collective-permute-start(bf16[256,640]{1,0:T(8,128)(2,1)S(1)} %param.1), channel_id=1, source_target_pairs={{0,32},{16,48},{32,64},{48,80},{64,96},{80,112},{1,33},{17,49},{33... | collective-permute-start | bytes 983048 | tf_op jit(solution)/shard_map/while/body/eval_jaxpr/cond/branch_1_fun/ppermute | solution.py:378
  268.2 12.1 %copy-start.1 = (bf16[2,4,64,640]{3,2,1,0:T(8,128)(2,1)S(1)}, bf16[2,4,64,640]{3,2,1,0:T(8,128)(2,1)}, u32[]{:S(2)}) copy-start(bf16[2,4,64,640]{3,2,1,0:T(8,128)(2,1)} %param.14) | copy-start | bytes 1966084
  268.3 1.5 collective-permute-start.21
  269.8 2.7 collective-permute-start.22
  270.5 2.0 collective-permute-start.24
  271.2 8.4 %collective-permute-start.23 = (bf16[2,4,8,640]{3,2,1,0:T(8,128)(2,1)S(1)}, bf16[2,4,8,640]{3,2,1,0:T(8,128)(2,1)S(1)}, u32[]{:S(2)}, u32[]{:S(2)}) collective-permute-start(bf16[2,4,8,640]{3,2,1,0:T(8,128)(2,1)S(1)} %get-tuple-element.471), channel_id=1, source_target_pairs={{96,32},{112,48},{97,33},{113,49},{98,34},{114,50},{99,35},{115,51... | collective-permute-start | bytes 245768 | tf_op jit(solution)/shard_map/ppermute | solution.py:391

commit v4 on v3

--- a/solution.py
+++ b/solution.py
@@ -50,54 +50,38 @@
     pltpu.make_async_copy(own, target, sem).wait()
 
 
-def stale_kernel(count, *refs):
-    pieces, (ga_ref, wk_ref, wv_ref, k_ref, vt_ref) = refs[:count], refs[count:]
-    block, piece = pl.program_id(0), pl.program_id(1)
-    raw = pieces[0][...]
-    for i in range(1, count):
-        raw = jnp.where(piece == i, pieces[i][...], raw)
-    raw = raw.reshape(-1, C).astype(F32)
+def stale_kernel(near_ref, far_ref, ga_ref, wk_ref, wv_ref, k_ref, vt_ref):
+    block = pl.program_id(0)
+    raw = jnp.concatenate([near_ref[...], far_ref[...]], 0).reshape(-1, C).astype(F32)
     normed = normalize(raw, ga_ref[pl.ds(block, 1), :]).astype(BF)
     keys = dot(normed, wk_ref[...]).astype(BF)
+    for pair in range(PAIRS):
+        k_ref[pair] = keys[:, pair * 128 : (pair + 1) * 128]
     values = dot_turned(wv_ref[...], normed).astype(BF)
     for pair in range(PAIRS):
-        k_ref[pair] = keys[:, pair * 128 : (pair + 1) * 128]
         vt_ref[pair] = values[pair * 128 : (pair + 1) * 128]
 
 
 def stale_call(pieces, gains, wk, wv):
-    count, size = len(pieces), pieces[0].shape[0]
-    patches, steps = size, 1
-    cells = count * size * CELLS
-
-    def piece_spec(i):
-        def place(b, piece, step):
-            return jnp.where(piece == i, step, jnp.where(piece < i, 0, steps - 1)), b, 0, 0
-
-        return pl.BlockSpec((patches, None, CELLS, C), place)
-
+    size = pieces[0].shape[0]
+    cells = 2 * size * CELLS
     return pl.pallas_call(
-        functools.partial(stale_kernel, count),
-        grid=(2, count, steps),
+        stale_kernel,
+        grid=(2,),
         out_shape=[
             jax.ShapeDtypeStruct((2, PAIRS, cells, 128), BF),
             jax.ShapeDtypeStruct((2, PAIRS, 128, cells), BF),
         ],
-        in_specs=[piece_spec(i) for i in range(count)]
-        + [
-            pl.BlockSpec((2, C), lambda b, piece, step: (0, 0)),
-            pl.BlockSpec((None, C, C), lambda b, piece, step: (b, 0, 0)),
-            pl.BlockSpec((None, C, C), lambda b, piece, step: (b, 0, 0)),
+        in_specs=[
+            pl.BlockSpec((size, None, CELLS, C), lambda b: (0, b, 0, 0)),
+            pl.BlockSpec((size, None, CELLS, C), lambda b: (0, b, 0, 0)),
+            pl.BlockSpec((2, C), lambda b: (0, 0)),
+            pl.BlockSpec((None, C, C), lambda b: (b, 0, 0)),
+            pl.BlockSpec((None, C, C), lambda b: (b, 0, 0)),
         ],
         out_specs=[
-            pl.BlockSpec(
-                (None, PAIRS, patches * CELLS, 128),
-                lambda b, piece, step: (b, 0, piece * steps + step, 0),
-            ),
-            pl.BlockSpec(
-                (None, PAIRS, 128, patches * CELLS),
-                lambda b, piece, step: (b, 0, 0, piece * steps + step),
-            ),
+            pl.BlockSpec((None, PAIRS, cells, 128), lambda b: (b, 0, 0, 0)),
+            pl.BlockSpec((None, PAIRS, 128, cells), lambda b: (b, 0, 0, 0)),
         ],
         compiler_params=pltpu.CompilerParams(vmem_limit_bytes=50 << 20),
         cost_estimate=pl.CostEstimate(
@@ -154,6 +138,8 @@
         return copies
 
     start(0, "query", "key", "value")
+    for copy in pair_copies(0, 0):
+        copy.start()
     mid[...] = x_ref[...].astype(F32)
     lane = lax.broadcasted_iota(jnp.int32, (CELLS, 128), 1)
     own_cells = pl.ds(0, CELLS)
@@ -168,7 +154,7 @@
 
         @pl.when(place == 0)
         def _():
-            for pair in range(PAIRS):
+            for pair in range(1, PAIRS):
                 for copy in pair_copies(0, pair):
                     copy.start()
             start(0, "out", "conv")
@@ -351,17 +337,17 @@
     wk, wv = [jnp.stack(ordered(own[name], other[name])) for name in ("key", "value")]
     back, ahead = ring_near(raw, 0)
     far = ring_far(back, ahead, 0)
-    back, ahead, far, wk, wv, gains, edges, conv_sent = lax.optimization_barrier(
-        (back, ahead, far, wk, wv, gains, edges, own["conv"])
+    upper = lax.ppermute(edges[:, 1], "patch", [(i, i + 1) for i in range(15)])
+    lower = lax.ppermute(edges[:, 0], "patch", [(i + 1, i) for i in range(15)])
+    back, ahead, far, wk, wv, gains, upper, lower, conv_sent = lax.optimization_barrier(
+        (back, ahead, far, wk, wv, gains, upper, lower, own["conv"])
     )
     other["conv"] = swap(conv_sent)
     row = jnp.stack([raw, back]), jnp.stack([jnp.concatenate(far, 0), ahead])
     first = turned(row[0], 1, 1), turned(row[1], 1, -1)
+    stored = [stale_call(row, gains, wk, wv)]
+    row, stored = lax.optimization_barrier((row, stored))
     second = turned(row[1], 1, 1), turned(row[0], 1, -1)
-    upper = lax.ppermute(edges[:, 1], "patch", [(i, i + 1) for i in range(15)])
-    lower = lax.ppermute(edges[:, 0], "patch", [(i + 1, i) for i in range(15)])
-    stored = [stale_call(row, gains, wk, wv)]
-    first, upper, lower, stored = lax.optimization_barrier((first, upper, lower, stored))
     far = turned(first[0], 1, 1), turned(first[1], 1, -1)
     stored.append(stale_call(first, gains, wk, wv))
     second, stored, sent = lax.optimization_barrier(

time: 283 us -> 277 us (0.979)
  Pallas kernels: 175 us -> 170 us
    ppermute x10, waiting for transfers between devices: 10.9 us -> 26 us  [turned(): return lax.ppermute(value, ('segment', 'patch'), pairs)]
    ppermute x1, waiting for transfers between devices: 11 us -> 0.01 us  [shards(): lower = lax.ppermute(edges[:, 0], 'patch', [(i + 1, i) for i in range(15)])]
    pallas_call x4, Pallas kernels: 37.1 us -> 33.6 us  [stale_call(): pl.pallas_call(stale_kernel, grid=(2,), out_shape=[jax.ShapeDtypeStruct((...]
  transfers between devices with their start and end apart: 27 -> 27, of which waited for: 13 -> 15; matrix products, arithmetic and copies ran while one was open for 1% -> 1% of each run, Pallas kernels for 13% -> 12%
where the time goes in v4:
time: 277 us
  Pallas kernels  170 us (61%)
  waiting for transfers between devices  61.3 us (22%)
  starting transfers between devices  35.6 us (13%)
  other arithmetic  7.52 us (3%)
    pallas_call x4, Pallas kernels, block_call(): pl.pallas_call(block_kernel, out_shape=jax.ShapeDtypeStruct((CELLS, C), B...  137 us
    pallas_call x4, Pallas kernels, stale_call(): pl.pallas_call(stale_kernel, grid=(2,), out_shape=[jax.ShapeDtypeStruct((...  33.6 us
    ppermute x10, waiting for transfers between devices, turned(): return lax.ppermute(value, ('segment', 'patch'), pairs)  26 us
    ppermute x3, waiting for transfers between devices, hop(): return lax.ppermute(x, 'segment', [(i, i + 2) for i in range(6)])  24.3 us
    ppermute x10, starting transfers between devices, turned(): return lax.ppermute(value, ('segment', 'patch'), pairs)  14.4 us
    ppermute x3, starting transfers between devices, hop(): return lax.ppermute(x, 'segment', [(i, i + 2) for i in range(6)])  10.2 us
    ppermute x3, waiting for transfers between devices, shards(): lax.ppermute(both[:, :, (3 + d) % 4], 'segment', [(6, (6 + 2 * d) % 8), (...  7.1 us
  transfers between devices with their start and end apart: 27, of which 15 were waited for; matrix products, arithmetic and copies ran while one was open for 1% of the time, Pallas kernels for 12%

profile of v4, /device:TPU:18, one launch (start us, length us, event | category | flops | bytes accessed | tf_op | source)
XLA Modules:
  0.0 276.7 jit_solution(17673325804710373476)
XLA Ops:
  0.0 2.0 fusion.2
  2.0 2.2 collective-permute-done.1
  4.2 1.2 select_bitcast_fusion.4
  5.4 0.1 fusion
  5.5 0.2 collective-permute-start.6
  5.7 0.4 collective-permute-start.7
  6.1 0.1 collective-permute-start.8
  6.2 0.4 collective-permute-start.11
  6.6 4.0 %collective-permute-start.3 = (bf16[2,256,640]{2,1,0:T(8,128)(2,1)S(1)}, bf16[2,256,640]{2,1,0:T(8,128)(2,1)S(1)}, u32[]{:S(2)}, u32[]{:S(2)}) collective-permute-start(bf16[2,256,640]{2,1,0:T(8,128)(2,1)S(1)} %fusion), channel_id=1, source_target_pairs={{0,3},{1,0},{2,1},{3,2},{4,7},{5,4},{6,5},{7,6},{8,11},{9,8},{10,9... | collective-permute-start | bytes 1966088 | tf_op jit(solution)/shard_map/ppermute | solution.py:295
  10.7 0.4 collective-permute-start.2
  11.1 4.7 %collective-permute-start.10 = (bf16[2,64,640]{2,1,0:T(8,128)(2,1)S(1)}, bf16[2,64,640]{2,1,0:T(8,128)(2,1)}, u32[]{:S(2)}, u32[]{:S(2)}) collective-permute-start(bf16[2,64,640]{2,1,0:T(8,128)(2,1)S(1)} %get-tuple-element.474), channel_id=1, source_target_pairs={{1,0},{2,1},{3,2},{4,3},{5,4},{6,5},{7,6},{8,7},{9,8},{10,9},{11,1... | collective-permute-start | bytes 491528 | tf_op jit(solution)/shard_map/ppermute | solution.py:341
  15.8 6.5 %collective-permute-done.3 = bf16[2,256,640]{2,1,0:T(8,128)(2,1)S(1)} collective-permute-done((bf16[2,256,640]{2,1,0:T(8,128)(2,1)S(1)}, bf16[2,256,640]{2,1,0:T(8,128)(2,1)S(1)}, u32[]{:S(2)}, u32[]{:S(2)}) %collective-permute-start.3) | collective-permute-done | bytes 655392 | tf_op jit(solution)/shard_map/ppermute | solution.py:295
  22.3 1.9 collective-permute-start.9
  24.2 3.8 %collective-permute-start.5 = (bf16[1,256,640]{2,1,0:T(8,128)(2,1)S(1)}, bf16[1,256,640]{2,1,0:T(8,128)(2,1)S(1)}, u32[]{:S(2)}, u32[]{:S(2)}) collective-permute-start(bf16[1,256,640]{2,1,0:T(8,128)(2,1)S(1)} %slice.43), channel_id=1, source_target_pairs={{0,3},{1,0},{2,1},{3,2},{4,7},{5,4},{6,5},{7,6},{8,11},{9,8},{10,9... | collective-permute-start | bytes 983048 | tf_op jit(solution)/shard_map/ppermute | solution.py:295
  28.0 0.1 collective-permute-start.4
  28.1 0.3 select_bitcast_fusion.1
  28.5 1.3 pad_maximum_fusion.1.wv_ref
  29.8 1.4 pad_maximum_fusion.wk_ref
  31.2 0.4 collective-permute-done.9
  31.7 0.9 collective-permute-done.5
  32.6 3.8 %collective-permute-done.4 = bf16[1,256,640]{2,1,0:T(8,128)(2,1)S(1)} collective-permute-done((bf16[1,256,640]{2,1,0:T(8,128)(2,1)S(1)}, bf16[1,256,640]{2,1,0:T(8,128)(2,1)S(1)}, u32[]{:S(2)}, u32[]{:S(2)}) %collective-permute-start.4) | collective-permute-done | bytes 327712 | tf_op jit(solution)/shard_map/ppermute | solution.py:295
  36.4 0.1 maximum_bitcast_fusion
  36.5 0.1 pad_maximum_fusion.3.far_ref
  36.6 1.1 collective-permute-start.15
  37.7 0.1 pad_maximum_fusion.2.near_ref
  37.8 1.1 collective-permute-start.14
  38.9 8.5 %stale.4 = (bf16[2,5,1024,128]{3,2,1,0:T(8,128)(2,1)}, bf16[2,5,128,1024]{3,2,1,0:T(8,128)(2,1)}) custom-call(bf16[2,2,256,640]{3,2,1,0:T(8,128)(2,1)S(1)} %pad_maximum_fusion.2.near_ref, bf16[2,2,256,640]{3,2,1,0:T(8,128)(2,1)S(1)} %pad_maximum_fusion.3.far_ref, f32[2,640]{1,0:T(2,128)S(1)} %pad_maximum_fusion.6.ga_ref, ...), custom_call_target="tpu_custom_call" | custom-call | flops 3355443200 | bytes 7864320 | tf_op jit(solution)/shard_map/stale/pallas_call | solution.py:68
  47.4 0.1 collective-permute-start.12
  47.5 1.9 collective-permute-start.13
  49.4 4.9 %collective-permute-done.15.far_ref = bf16[2,2,256,640]{3,2,1,0:T(8,128)(2,1)S(1)} collective-permute-done((bf16[2,2,256,640]{3,2,1,0:T(8,128)(2,1)S(1)}, bf16[2,2,256,640]{3,2,1,0:T(8,128)(2,1)S(1)}, u32[]{:S(2)}, u32[]{:S(2)}) %collective-permute-start.15) | collective-permute-done | bytes 1310752 | tf_op jit(solution)/shard_map/ppermute | solution.py:295
  54.3 1.0 collective-permute-start.20
  55.3 0.2 collective-permute-done.14.near_ref
  55.5 1.0 collective-permute-start.19
  56.5 8.4 %stale.5 = (bf16[2,5,1024,128]{3,2,1,0:T(8,128)(2,1)}, bf16[2,5,128,1024]{3,2,1,0:T(8,128)(2,1)}) custom-call(bf16[2,2,256,640]{3,2,1,0:T(8,128)(2,1)S(1)} %collective-permute-done.14.near_ref, bf16[2,2,256,640]{3,2,1,0:T(8,128)(2,1)S(1)} %collective-permute-done.15.far_ref, f32[2,640]{1,0:T(2,128)S(1)} %pad_maximum_fusion.6.ga_ref, ...), custom_call_target="tpu_custom_call" | custom-call | flops 3355443200 | bytes 7864320 | tf_op jit(solution)/shard_map/stale/pallas_call | solution.py:68
  64.9 4.6 %collective-permute-done.12.near_ref = bf16[2,2,256,640]{3,2,1,0:T(8,128)(2,1)S(1)} collective-permute-done((bf16[2,2,256,640]{3,2,1,0:T(8,128)(2,1)S(1)}, bf16[2,2,256,640]{3,2,1,0:T(8,128)(2,1)S(1)}, u32[]{:S(2)}, u32[]{:S(2)}) %collective-permute-start.12) | collective-permute-done | bytes 1310752 | tf_op jit(solution)/shard_map/ppermute | solution.py:295
  69.5 0.1 collective-permute-start.16
  69.6 0.4 collective-permute-start.17
  70.1 8.4 %stale.6 = (bf16[2,5,1024,128]{3,2,1,0:T(8,128)(2,1)}, bf16[2,5,128,1024]{3,2,1,0:T(8,128)(2,1)}) custom-call(bf16[2,2,256,640]{3,2,1,0:T(8,128)(2,1)S(1)} %collective-permute-done.12.near_ref, bf16[2,2,256,640]{3,2,1,0:T(8,128)(2,1)S(1)} %collective-permute-done.13.far_ref, f32[2,640]{1,0:T(2,128)S(1)} %pad_maximum_fusion.6.ga_ref, ...), custom_call_target="tpu_custom_call" | custom-call | flops 3355443200 | bytes 7864320 | tf_op jit(solution)/shard_map/stale/pallas_call | solution.py:68
  78.5 3.9 %collective-permute-done.20.far_ref = bf16[2,2,256,640]{3,2,1,0:T(8,128)(2,1)S(1)} collective-permute-done((bf16[2,2,256,640]{3,2,1,0:T(8,128)(2,1)S(1)}, bf16[2,2,256,640]{3,2,1,0:T(8,128)(2,1)S(1)}, u32[]{:S(2)}, u32[]{:S(2)}) %collective-permute-start.20) | collective-permute-done | bytes 1310752 | tf_op jit(solution)/shard_map/ppermute | solution.py:295
  82.4 1.2 collective-permute-done.19.near_ref
  83.6 8.4 %stale.7 = (bf16[2,5,1024,128]{3,2,1,0:T(8,128)(2,1)}, bf16[2,5,128,1024]{3,2,1,0:T(8,128)(2,1)}) custom-call(bf16[2,2,256,640]{3,2,1,0:T(8,128)(2,1)S(1)} %collective-permute-done.19.near_ref, bf16[2,2,256,640]{3,2,1,0:T(8,128)(2,1)S(1)} %collective-permute-done.20.far_ref, f32[2,640]{1,0:T(2,128)S(1)} %pad_maximum_fusion.6.ga_ref, ...), custom_call_target="tpu_custom_call" | custom-call | flops 3355443200 | bytes 7864320 | tf_op jit(solution)/shard_map/stale/pallas_call | solution.py:68
  92.0 0.9 copy-done.9
  92.9 171.7 %while.13 = (s32[]{:T(128)}, bf16[256,640]{1,0:T(8,128)(2,1)S(1)}, f32[2,640]{1,0:T(2,128)S(1)}, f32[2,640]{1,0:T(2,128)S(1)}, bf16[2,64,640]{2,1,0:T(8,128)(2,1...) while((s32[]{:T(128)}, bf16[256,640]{1,0:T(8,128)(2,1)S(1)}, ...), condition=%wide.region_3.4_spmd, body=%wide.region_0.3_spmd.sunk | while | flops 25999998976 | bytes 46621728 | solution.py:369
  92.9 34.2 %blocks.5 = bf16[256,640]{1,0:T(8,128)(2,1)S(1)} custom-call(bf16[256,640]{1,0:T(8,128)(2,1)S(1)} %get-tuple-element.656.refs_0_, f32[2,640]{1,0:T(2,128)S(1)} %get-tuple-element.683.refs_1_, f32[2,640]{1,0:T(2,128)S(1)} %get-tuple-element.684.refs_2_, bf16[2,64,640]{2,1,0:T(8,128)(2,1)} %get-tuple-element.685.refs_3_, ...), custom_call_target="tpu_custom_call" | custom-call | flops 25999998976 | bytes 44000000 | tf_op jit(solution)/shard_map/while/body/eval_jaxpr/blocks/pallas_call | solution.py:244
  127.1 12.0 %conditional.2 = (bf16[256,640]{1,0:T(8,128)(2,1)S(1)}) conditional(s32[]{:T(128)} %convert_element_type.13, bf16[256,640]{1,0:T(8,128)(2,1)S(1)} %blocks.5, bf16[256,640]{1,0:T(8,128)(2,1)S(1)} %blocks.5), branch_computations={%region_1.1_spmd, %region_2.2_spmd} | conditional | bytes 1966128 | solution.py:367
  127.1 3.4 %collective-permute-start = (bf16[256,640]{1,0:T(8,128)(2,1)S(1)}, bf16[256,640]{1,0:T(8,128)(2,1)S(1)}, u32[]{:S(2)}, u32[]{:S(2)}) collective-permute-start(bf16[256,640]{1,0:T(8,128)(2,1)S(1)} %param.1), channel_id=1, source_target_pairs={{0,32},{16,48},{32,64},{48,80},{64,96},{80,112},{1,33},{17,49},{33... | collective-permute-start | bytes 983048 | tf_op jit(solution)/shard_map/while/body/eval_jaxpr/cond/branch_1_fun/ppermute | solution.py:364
  130.5 8.6 %collective-permute-done = bf16[256,640]{1,0:T(8,128)(2,1)S(1)} collective-permute-done((bf16[256,640]{1,0:T(8,128)(2,1)S(1)}, bf16[256,640]{1,0:T(8,128)(2,1)S(1)}, u32[]{:S(2)}, u32[]{:S(2)}) %collective-permute-start) | collective-permute-done | bytes 327712 | tf_op jit(solution)/shard_map/while/body/eval_jaxpr/cond/branch_1_fun/ppermute | solution.py:364
  139.1 34.2 %blocks.5 = bf16[256,640]{1,0:T(8,128)(2,1)S(1)} custom-call(bf16[256,640]{1,0:T(8,128)(2,1)S(1)} %get-tuple-element.656.refs_0_, f32[2,640]{1,0:T(2,128)S(1)} %get-tuple-element.683.refs_1_, f32[2,640]{1,0:T(2,128)S(1)} %get-tuple-element.684.refs_2_, bf16[2,64,640]{2,1,0:T(8,128)(2,1)} %get-tuple-element.685.refs_3_, ...), custom_call_target="tpu_custom_call" | custom-call | flops 25999998976 | bytes 44000000 | tf_op jit(solution)/shard_map/while/body/eval_jaxpr/blocks/pallas_call | solution.py:244
  173.3 11.6 %conditional.2 = (bf16[256,640]{1,0:T(8,128)(2,1)S(1)}) conditional(s32[]{:T(128)} %convert_element_type.13, bf16[256,640]{1,0:T(8,128)(2,1)S(1)} %blocks.5, bf16[256,640]{1,0:T(8,128)(2,1)S(1)} %blocks.5), branch_computations={%region_1.1_spmd, %region_2.2_spmd} | conditional | bytes 1966128 | solution.py:367
  173.4 3.4 %collective-permute-start = (bf16[256,640]{1,0:T(8,128)(2,1)S(1)}, bf16[256,640]{1,0:T(8,128)(2,1)S(1)}, u32[]{:S(2)}, u32[]{:S(2)}) collective-permute-start(bf16[256,640]{1,0:T(8,128)(2,1)S(1)} %param.1), channel_id=1, source_target_pairs={{0,32},{16,48},{32,64},{48,80},{64,96},{80,112},{1,33},{17,49},{33... | collective-permute-start | bytes 983048 | tf_op jit(solution)/shard_map/while/body/eval_jaxpr/cond/branch_1_fun/ppermute | solution.py:364
  176.8 8.1 %collective-permute-done = bf16[256,640]{1,0:T(8,128)(2,1)S(1)} collective-permute-done((bf16[256,640]{1,0:T(8,128)(2,1)S(1)}, bf16[256,640]{1,0:T(8,128)(2,1)S(1)}, u32[]{:S(2)}, u32[]{:S(2)}) %collective-permute-start) | collective-permute-done | bytes 327712 | tf_op jit(solution)/shard_map/while/body/eval_jaxpr/cond/branch_1_fun/ppermute | solution.py:364
  185.0 34.2 %blocks.5 = bf16[256,640]{1,0:T(8,128)(2,1)S(1)} custom-call(bf16[256,640]{1,0:T(8,128)(2,1)S(1)} %get-tuple-element.656.refs_0_, f32[2,640]{1,0:T(2,128)S(1)} %get-tuple-element.683.refs_1_, f32[2,640]{1,0:T(2,128)S(1)} %get-tuple-element.684.refs_2_, bf16[2,64,640]{2,1,0:T(8,128)(2,1)} %get-tuple-element.685.refs_3_, ...), custom_call_target="tpu_custom_call" | custom-call | flops 25999998976 | bytes 44000000 | tf_op jit(solution)/shard_map/while/body/eval_jaxpr/blocks/pallas_call | solution.py:244
  219.2 11.1 %conditional.2 = (bf16[256,640]{1,0:T(8,128)(2,1)S(1)}) conditional(s32[]{:T(128)} %convert_element_type.13, bf16[256,640]{1,0:T(8,128)(2,1)S(1)} %blocks.5, bf16[256,640]{1,0:T(8,128)(2,1)S(1)} %blocks.5), branch_computations={%region_1.1_spmd, %region_2.2_spmd} | conditional | bytes 1966128 | solution.py:367
  219.2 3.4 %collective-permute-start = (bf16[256,640]{1,0:T(8,128)(2,1)S(1)}, bf16[256,640]{1,0:T(8,128)(2,1)S(1)}, u32[]{:S(2)}, u32[]{:S(2)}) collective-permute-start(bf16[256,640]{1,0:T(8,128)(2,1)S(1)} %param.1), channel_id=1, source_target_pairs={{0,32},{16,48},{32,64},{48,80},{64,96},{80,112},{1,33},{17,49},{33... | collective-permute-start | bytes 983048 | tf_op jit(solution)/shard_map/while/body/eval_jaxpr/cond/branch_1_fun/ppermute | solution.py:364
  222.6 7.6 %collective-permute-done = bf16[256,640]{1,0:T(8,128)(2,1)S(1)} collective-permute-done((bf16[256,640]{1,0:T(8,128)(2,1)S(1)}, bf16[256,640]{1,0:T(8,128)(2,1)S(1)}, u32[]{:S(2)}, u32[]{:S(2)}) %collective-permute-start) | collective-permute-done | bytes 327712 | tf_op jit(solution)/shard_map/while/body/eval_jaxpr/cond/branch_1_fun/ppermute | solution.py:364
  230.3 34.2 %blocks.5 = bf16[256,640]{1,0:T(8,128)(2,1)S(1)} custom-call(bf16[256,640]{1,0:T(8,128)(2,1)S(1)} %get-tuple-element.656.refs_0_, f32[2,640]{1,0:T(2,128)S(1)} %get-tuple-element.683.refs_1_, f32[2,640]{1,0:T(2,128)S(1)} %get-tuple-element.684.refs_2_, bf16[2,64,640]{2,1,0:T(8,128)(2,1)} %get-tuple-element.685.refs_3_, ...), custom_call_target="tpu_custom_call" | custom-call | flops 25999998976 | bytes 44000000 | tf_op jit(solution)/shard_map/while/body/eval_jaxpr/blocks/pallas_call | solution.py:244
  264.6 0.0 copy-start.1
  264.7 0.1 collective-permute-start.21
  264.8 1.4 collective-permute-done.21
  266.2 0.7 collective-permute-start.22
  266.9 0.7 collective-permute-start.24
  267.6 1.3 collective-permute-start.23
  268.9 7.1 %collective-permute-done.23 = bf16[2,4,8,640]{3,2,1,0:T(8,128)(2,1)S(1)} collective-permute-done((bf16[2,4,8,640]{3,2,1,0:T(8,128)(2,1)S(1)}, bf16[2,4,8,640]{3,2,1,0:T(8,128)(2,1)S(1)}, u32[]{:S(2)}, u32[]{:S(2)}) %collective-permute-start.23) | collective-permute-done | bytes 81952 | tf_op jit(solution)/shard_map/ppermute | solution.py:377
  276.0 0.7 fusion.13
  (52 shorter events, 0.6 us)
Async XLA Ops:
  0.0 70.1 %copy-start = (bf16[2,4,64,640]{3,2,1,0:T(8,128)(2,1)S(1)}, bf16[2,4,64,640]{3,2,1,0:T(8,128)(2,1)}, u32[]{:S(2)}) copy-start(bf16[2,4,64,640]{3,2,1,0:T(8,128)(2,1)} %param.14) | copy-start | bytes 1966084
  0.0 4.2 %copy-start.3 = (bf16[1,2,2,64,640]{4,3,2,1,0:T(8,128)(2,1)S(1)}, bf16[1,2,2,64,640]{4,3,2,1,0:T(8,128)(2,1)}, u32[]{:S(2)}) copy-start(bf16[1,2,2,64,640]{4,3,2,1,0:T(8,128)(2,1)} %param.16) | copy-start | bytes 983044
  0.0 4.2 %copy-start.2 = (bf16[1,2,4,64,640]{4,3,2,1,0:T(8,128)(2,1)S(1)}, bf16[1,2,4,64,640]{4,3,2,1,0:T(8,128)(2,1)}, u32[]{:S(2)}) copy-start(bf16[1,2,4,64,640]{4,3,2,1,0:T(8,128)(2,1)} %param.15) | copy-start | bytes 1966084
  2.0 2.2 collective-permute-start.1
  2.0 3.5 %copy-start.4 = (bf16[1,640,640]{2,1,0:T(8,128)(2,1)S(1)}, bf16[1,640,640]{2,1,0:T(8,128)(2,1)}, u32[]{:S(2)}) copy-start(bf16[1,640,640]{2,1,0:T(8,128)(2,1)} %param.19) | copy-start | bytes 2457604
  2.0 3.7 %copy-start.5 = (bf16[1,640,640]{2,1,0:T(8,128)(2,1)S(1)}, bf16[1,640,640]{2,1,0:T(8,128)(2,1)}, u32[]{:S(2)}) copy-start(bf16[1,640,640]{2,1,0:T(8,128)(2,1)} %param.20) | copy-start | bytes 2457604
  2.0 4.1 %copy-start.8 = (f32[1,640]{1,0:T(1,128)S(1)}, f32[1,640]{1,0:T(1,128)}, u32[]{:S(2)}) copy-start(f32[1,640]{1,0:T(1,128)} %param.17) | copy-start | bytes 7684
  2.0 4.2 %copy-start.7 = (f32[1,640]{1,0:T(1,128)S(1)}, f32[1,640]{1,0:T(1,128)}, u32[]{:S(2)}) copy-start(f32[1,640]{1,0:T(1,128)} %param.22) | copy-start | bytes 7684
  5.5 22.5 %collective-permute-start.6 = (bf16[640,640]{1,0:T(8,128)(2,1)S(1)}, bf16[640,640]{1,0:T(8,128)(2,1)S(1)}, u32[]{:S(2)}, u32[]{:S(2)}) collective-permute-start(bf16[640,640]{1,0:T(8,128)(2,1)S(1)} %bitcast.88), channel_id=1, source_target_pairs={{0,16},{16,0},{32,48},{48,32},{64,80},{80,64},{96,112},{112,96},{1... | collective-permute-start | bytes 2457608 | tf_op jit(solution)/shard_map/ppermute | solution.py:315
  5.7 22.4 %collective-permute-start.7 = (bf16[640,640]{1,0:T(8,128)(2,1)S(1)}, bf16[640,640]{1,0:T(8,128)(2,1)S(1)}, u32[]{:S(2)}, u32[]{:S(2)}) collective-permute-start(bf16[640,640]{1,0:T(8,128)(2,1)S(1)} %bitcast.90), channel_id=1, source_target_pairs={{0,16},{16,0},{32,48},{48,32},{64,80},{80,64},{96,112},{112,96},{1... | collective-permute-start | bytes 2457608 | tf_op jit(solution)/shard_map/ppermute | solution.py:315
  6.1 4.6 %collective-permute-start.8 = (f32[1,640]{1,0:T(1,128)S(1)}, f32[1,640]{1,0:T(1,128)S(1)}, u32[]{:S(2)}, u32[]{:S(2)}) collective-permute-start(f32[1,640]{1,0:T(1,128)S(1)} %copy-done.8), channel_id=1, source_target_pairs={{0,16},{16,0},{32,48},{48,32},{64,80},{80,64},{96,112},{112,96},{1... | collective-permute-start | bytes 7688 | tf_op jit(solution)/shard_map/ppermute | solution.py:315
  6.2 4.8 %collective-permute-start.11 = (f32[1,640]{1,0:T(1,128)S(1)}, f32[1,640]{1,0:T(1,128)S(1)}, u32[]{:S(2)}, u32[]{:S(2)}) collective-permute-start(f32[1,640]{1,0:T(1,128)S(1)} %copy-done.7), channel_id=1, source_target_pairs={{0,16},{16,0},{32,48},{48,32},{64,80},{80,64},{96,112},{112,96},{1... | collective-permute-start | bytes 7688 | tf_op jit(solution)/shard_map/ppermute | solution.py:315
  6.6 15.7 %collective-permute-start.3 = (bf16[2,256,640]{2,1,0:T(8,128)(2,1)S(1)}, bf16[2,256,640]{2,1,0:T(8,128)(2,1)S(1)}, u32[]{:S(2)}, u32[]{:S(2)}) collective-permute-start(bf16[2,256,640]{2,1,0:T(8,128)(2,1)S(1)} %fusion), channel_id=1, source_target_pairs={{0,3},{1,0},{2,1},{3,2},{4,7},{5,4},{6,5},{7,6},{8,11},{9,8},{10,9... | collective-permute-start | bytes 1966088 | tf_op jit(solution)/shard_map/ppermute | solution.py:295
  10.7 13.6 %collective-permute-start.2 = (bf16[2,256,640]{2,1,0:T(8,128)(2,1)S(1)}, bf16[2,256,640]{2,1,0:T(8,128)(2,1)S(1)}, u32[]{:S(2)}, u32[]{:S(2)}) collective-permute-start(bf16[2,256,640]{2,1,0:T(8,128)(2,1)S(1)} %fusion), channel_id=1, source_target_pairs={{0,1},{1,2},{2,3},{3,0},{4,5},{5,6},{6,7},{7,4},{8,9},{9,10},{10,1... | collective-permute-start | bytes 1966088 | tf_op jit(solution)/shard_map/ppermute | solution.py:295
  11.1 20.1 %collective-permute-start.10 = (bf16[2,64,640]{2,1,0:T(8,128)(2,1)S(1)}, bf16[2,64,640]{2,1,0:T(8,128)(2,1)}, u32[]{:S(2)}, u32[]{:S(2)}) collective-permute-start(bf16[2,64,640]{2,1,0:T(8,128)(2,1)S(1)} %get-tuple-element.474), channel_id=1, source_target_pairs={{1,0},{2,1},{3,2},{4,3},{5,4},{6,5},{7,6},{8,7},{9,8},{10,9},{11,1... | collective-permute-start | bytes 491528 | tf_op jit(solution)/shard_map/ppermute | solution.py:341
  22.3 9.4 %collective-permute-start.9 = (bf16[2,64,640]{2,1,0:T(8,128)(2,1)S(1)}, bf16[2,64,640]{2,1,0:T(8,128)(2,1)}, u32[]{:S(2)}, u32[]{:S(2)}) collective-permute-start(bf16[2,64,640]{2,1,0:T(8,128)(2,1)S(1)} %get-tuple-element.475), channel_id=1, source_target_pairs={{0,1},{1,2},{2,3},{3,4},{4,5},{5,6},{6,7},{7,8},{8,9},{9,10},{10,1... | collective-permute-start | bytes 491528 | tf_op jit(solution)/shard_map/ppermute | solution.py:340
  24.2 8.4 %collective-permute-start.5 = (bf16[1,256,640]{2,1,0:T(8,128)(2,1)S(1)}, bf16[1,256,640]{2,1,0:T(8,128)(2,1)S(1)}, u32[]{:S(2)}, u32[]{:S(2)}) collective-permute-start(bf16[1,256,640]{2,1,0:T(8,128)(2,1)S(1)} %slice.43), channel_id=1, source_target_pairs={{0,3},{1,0},{2,1},{3,2},{4,7},{5,4},{6,5},{7,6},{8,11},{9,8},{10,9... | collective-permute-start | bytes 983048 | tf_op jit(solution)/shard_map/ppermute | solution.py:295
  28.0 8.4 %collective-permute-start.4 = (bf16[1,256,640]{2,1,0:T(8,128)(2,1)S(1)}, bf16[1,256,640]{2,1,0:T(8,128)(2,1)S(1)}, u32[]{:S(2)}, u32[]{:S(2)}) collective-permute-start(bf16[1,256,640]{2,1,0:T(8,128)(2,1)S(1)} %slice.42), channel_id=1, source_target_pairs={{0,1},{1,2},{2,3},{3,0},{4,5},{5,6},{6,7},{7,4},{8,9},{9,10},{10,1... | collective-permute-start | bytes 983048 | tf_op jit(solution)/shard_map/ppermute | solution.py:295
  28.1 1.7 copy-start.6
  36.4 55.6 %collective-permute-start.18 = (bf16[9,640,640]{2,1,0:T(8,128)(2,1)}, bf16[9,640,640]{2,1,0:T(8,128)(2,1)}, u32[]{:S(2)}, u32[]{:S(2)}) collective-permute-start(bf16[9,640,640]{2,1,0:T(8,128)(2,1)} %bitcast.16), channel_id=1, source_target_pairs={{0,16},{16,0},{32,48},{48,32},{64,80},{80,64},{96,112},{112,96},{1... | collective-permute-start | bytes 22118408 | tf_op jit(solution)/shard_map/ppermute | solution.py:315
  36.6 17.7 %collective-permute-start.15 = (bf16[2,2,256,640]{3,2,1,0:T(8,128)(2,1)S(1)}, bf16[2,2,256,640]{3,2,1,0:T(8,128)(2,1)S(1)}, u32[]{:S(2)}, u32[]{:S(2)}) collective-permute-start(bf16[2,2,256,640]{3,2,1,0:T(8,128)(2,1)S(1)} %pad_maximum_fusion.3.far_ref), channel_id=1, source_target_pairs={{0,12},{1,13},{2,14},{3,15},{4,0},{5,1},{6,2},{7,3},{8,4},{9,5},{1... | collective-permute-start | bytes 3932168 | tf_op jit(solution)/shard_map/ppermute | solution.py:295
  37.8 17.7 %collective-permute-start.14 = (bf16[2,2,256,640]{3,2,1,0:T(8,128)(2,1)S(1)}, bf16[2,2,256,640]{3,2,1,0:T(8,128)(2,1)S(1)}, u32[]{:S(2)}, u32[]{:S(2)}) collective-permute-start(bf16[2,2,256,640]{3,2,1,0:T(8,128)(2,1)S(1)} %pad_maximum_fusion.2.near_ref), channel_id=1, source_target_pairs={{0,4},{1,5},{2,6},{3,7},{4,8},{5,9},{6,10},{7,11},{8,12},{9,13},{1... | collective-permute-start | bytes 3932168 | tf_op jit(solution)/shard_map/ppermute | solution.py:295
  47.4 22.2 %collective-permute-start.12 = (bf16[2,2,256,640]{3,2,1,0:T(8,128)(2,1)S(1)}, bf16[2,2,256,640]{3,2,1,0:T(8,128)(2,1)S(1)}, u32[]{:S(2)}, u32[]{:S(2)}) collective-permute-start(bf16[2,2,256,640]{3,2,1,0:T(8,128)(2,1)S(1)} %pad_maximum_fusion.3.far_ref), channel_id=1, source_target_pairs={{0,4},{1,5},{2,6},{3,7},{4,8},{5,9},{6,10},{7,11},{8,12},{9,13},{1... | collective-permute-start | bytes 3932168 | tf_op jit(solution)/shard_map/ppermute | solution.py:295
  47.5 22.1 %collective-permute-start.13 = (bf16[2,2,256,640]{3,2,1,0:T(8,128)(2,1)S(1)}, bf16[2,2,256,640]{3,2,1,0:T(8,128)(2,1)S(1)}, u32[]{:S(2)}, u32[]{:S(2)}) collective-permute-start(bf16[2,2,256,640]{3,2,1,0:T(8,128)(2,1)S(1)} %pad_maximum_fusion.2.near_ref), channel_id=1, source_target_pairs={{0,12},{1,13},{2,14},{3,15},{4,0},{5,1},{6,2},{7,3},{8,4},{9,5},{1... | collective-permute-start | bytes 3932168 | tf_op jit(solution)/shard_map/ppermute | solution.py:295
  54.3 28.1 %collective-permute-start.20 = (bf16[2,2,256,640]{3,2,1,0:T(8,128)(2,1)S(1)}, bf16[2,2,256,640]{3,2,1,0:T(8,128)(2,1)S(1)}, u32[]{:S(2)}, u32[]{:S(2)}) collective-permute-start(bf16[2,2,256,640]{3,2,1,0:T(8,128)(2,1)S(1)} %collective-permute-done.15.far_ref), channel_id=1, source_target_pairs={{0,12},{1,13},{2,14},{3,15},{4,0},{5,1},{6,2},{7,3},{8,4},{9,5},{1... | collective-permute-start | bytes 3932168 | tf_op jit(solution)/shard_map/ppermute | solution.py:295
  55.5 28.1 %collective-permute-start.19 = (bf16[2,2,256,640]{3,2,1,0:T(8,128)(2,1)S(1)}, bf16[2,2,256,640]{3,2,1,0:T(8,128)(2,1)S(1)}, u32[]{:S(2)}, u32[]{:S(2)}) collective-permute-start(bf16[2,2,256,640]{3,2,1,0:T(8,128)(2,1)S(1)} %collective-permute-done.14.near_ref), channel_id=1, source_target_pairs={{0,4},{1,5},{2,6},{3,7},{4,8},{5,9},{6,10},{7,11},{8,12},{9,13},{1... | collective-permute-start | bytes 3932168 | tf_op jit(solution)/shard_map/ppermute | solution.py:295
  69.5 22.4 %collective-permute-start.16 = (bf16[640,640]{1,0:T(8,128)(2,1)}, bf16[640,640]{1,0:T(8,128)(2,1)}, u32[]{:S(2)}, u32[]{:S(2)}) collective-permute-start(bf16[640,640]{1,0:T(8,128)(2,1)} %bitcast.17), channel_id=1, source_target_pairs={{0,16},{16,0},{32,48},{48,32},{64,80},{80,64},{96,112},{112,96},{1... | collective-permute-start | bytes 2457608 | tf_op jit(solution)/shard_map/ppermute | solution.py:315
  69.6 22.3 %collective-permute-start.17 = (bf16[640,640]{1,0:T(8,128)(2,1)}, bf16[640,640]{1,0:T(8,128)(2,1)S(1)}, u32[]{:S(2)}, u32[]{:S(2)}) collective-permute-start(bf16[640,640]{1,0:T(8,128)(2,1)} %bitcast.18), channel_id=1, source_target_pairs={{0,16},{16,0},{32,48},{48,32},{64,80},{80,64},{96,112},{112,96},{1... | collective-permute-start | bytes 2457608 | tf_op jit(solution)/shard_map/ppermute | solution.py:315
  92.0 0.9 copy-start.9
  127.1 12.0 %collective-permute-start = (bf16[256,640]{1,0:T(8,128)(2,1)S(1)}, bf16[256,640]{1,0:T(8,128)(2,1)S(1)}, u32[]{:S(2)}, u32[]{:S(2)}) collective-permute-start(bf16[256,640]{1,0:T(8,128)(2,1)S(1)} %param.1), channel_id=1, source_target_pairs={{0,32},{16,48},{32,64},{48,80},{64,96},{80,112},{1,33},{17,49},{33... | collective-permute-start | bytes 983048 | tf_op jit(solution)/shard_map/while/body/eval_jaxpr/cond/branch_1_fun/ppermute | solution.py:364
  173.4 11.5 %collective-permute-start = (bf16[256,640]{1,0:T(8,128)(2,1)S(1)}, bf16[256,640]{1,0:T(8,128)(2,1)S(1)}, u32[]{:S(2)}, u32[]{:S(2)}) collective-permute-start(bf16[256,640]{1,0:T(8,128)(2,1)S(1)} %param.1), channel_id=1, source_target_pairs={{0,32},{16,48},{32,64},{48,80},{64,96},{80,112},{1,33},{17,49},{33... | collective-permute-start | bytes 983048 | tf_op jit(solution)/shard_map/while/body/eval_jaxpr/cond/branch_1_fun/ppermute | solution.py:364
  219.2 11.0 %collective-permute-start = (bf16[256,640]{1,0:T(8,128)(2,1)S(1)}, bf16[256,640]{1,0:T(8,128)(2,1)S(1)}, u32[]{:S(2)}, u32[]{:S(2)}) collective-permute-start(bf16[256,640]{1,0:T(8,128)(2,1)S(1)} %param.1), channel_id=1, source_target_pairs={{0,32},{16,48},{32,64},{48,80},{64,96},{80,112},{1,33},{17,49},{33... | collective-permute-start | bytes 983048 | tf_op jit(solution)/shard_map/while/body/eval_jaxpr/cond/branch_1_fun/ppermute | solution.py:364
  264.6 12.1 %copy-start.1 = (bf16[2,4,64,640]{3,2,1,0:T(8,128)(2,1)S(1)}, bf16[2,4,64,640]{3,2,1,0:T(8,128)(2,1)}, u32[]{:S(2)}) copy-start(bf16[2,4,64,640]{3,2,1,0:T(8,128)(2,1)} %param.14) | copy-start | bytes 1966084
  264.7 1.5 collective-permute-start.21
  266.2 2.7 collective-permute-start.22
  266.9 2.0 collective-permute-start.24
  267.6 8.4 %collective-permute-start.23 = (bf16[2,4,8,640]{3,2,1,0:T(8,128)(2,1)S(1)}, bf16[2,4,8,640]{3,2,1,0:T(8,128)(2,1)S(1)}, u32[]{:S(2)}, u32[]{:S(2)}) collective-permute-start(bf16[2,4,8,640]{3,2,1,0:T(8,128)(2,1)S(1)} %get-tuple-element.469), channel_id=1, source_target_pairs={{96,32},{112,48},{97,33},{113,49},{98,34},{114,50},{99,35},{115,51... | collective-permute-start | bytes 245768 | tf_op jit(solution)/shard_map/ppermute | solution.py:377

commit v5 on v4

--- a/solution.py
+++ b/solution.py
@@ -337,12 +337,10 @@
     wk, wv = [jnp.stack(ordered(own[name], other[name])) for name in ("key", "value")]
     back, ahead = ring_near(raw, 0)
     far = ring_far(back, ahead, 0)
-    upper = lax.ppermute(edges[:, 1], "patch", [(i, i + 1) for i in range(15)])
-    lower = lax.ppermute(edges[:, 0], "patch", [(i + 1, i) for i in range(15)])
-    back, ahead, far, wk, wv, gains, upper, lower, conv_sent = lax.optimization_barrier(
-        (back, ahead, far, wk, wv, gains, upper, lower, own["conv"])
-    )
-    other["conv"] = swap(conv_sent)
+    back, ahead, far, wk, wv, gains, sent = lax.optimization_barrier(
+        (back, ahead, far, wk, wv, gains, own["conv"])
+    )
+    other["conv"] = swap(sent)
     row = jnp.stack([raw, back]), jnp.stack([jnp.concatenate(far, 0), ahead])
     first = turned(row[0], 1, 1), turned(row[1], 1, -1)
     stored = [stale_call(row, gains, wk, wv)]
@@ -350,11 +348,15 @@
     second = turned(row[1], 1, 1), turned(row[0], 1, -1)
     far = turned(first[0], 1, 1), turned(first[1], 1, -1)
     stored.append(stale_call(first, gains, wk, wv))
-    second, stored, sent = lax.optimization_barrier(
-        (second, stored, {name: own[name] for name in ("query", "out")})
+    second, stored, edges = lax.optimization_barrier((second, stored, edges))
+    upper = lax.ppermute(edges[:, 1], "patch", [(i, i + 1) for i in range(15)])
+    lower = lax.ppermute(edges[:, 0], "patch", [(i + 1, i) for i in range(15)])
+    stored.append(stale_call(second, gains, wk, wv))
+    far, upper, lower, stored, sent = lax.optimization_barrier(
+        (far, upper, lower, stored, {name: own[name] for name in ("query", "out")})
     )
     other |= {name: swap(value) for name, value in sent.items()}
-    stored += [stale_call(pieces, gains, wk, wv) for pieces in (second, far)]
+    stored.append(stale_call(far, gains, wk, wv))
 
     x = lax.dynamic_index_in_dim(latent, core, 0, keepdims=False).reshape(CELLS, C)
     def two_blocks(x):

time: 277 us -> 274 us (0.989)
    ppermute x10, waiting for transfers between devices: 26 us -> 18.4 us  [turned(): return lax.ppermute(value, ('segment', 'patch'), pairs)]
  transfers between devices with their start and end apart: 27 -> 27, of which waited for: 15 -> 16; matrix products, arithmetic and copies ran while one was open for 1% -> 1% of each run, Pallas kernels for 12% -> 12%
where the time goes in v5:
time: 274 us
  Pallas kernels  171 us (62%)
  waiting for transfers between devices  58.6 us (21%)
  starting transfers between devices  35.3 us (13%)
  other arithmetic  5.69 us (2%)
    pallas_call x4, Pallas kernels, block_call(): pl.pallas_call(block_kernel, out_shape=jax.ShapeDtypeStruct((CELLS, C), B...  137 us
    pallas_call x4, Pallas kernels, stale_call(): pl.pallas_call(stale_kernel, grid=(2,), out_shape=[jax.ShapeDtypeStruct((...  34 us
    ppermute x3, waiting for transfers between devices, hop(): return lax.ppermute(x, 'segment', [(i, i + 2) for i in range(6)])  25.2 us
    ppermute x10, waiting for transfers between devices, turned(): return lax.ppermute(value, ('segment', 'patch'), pairs)  18.4 us
    ppermute x10, starting transfers between devices, turned(): return lax.ppermute(value, ('segment', 'patch'), pairs)  14.8 us
    ppermute x3, starting transfers between devices, hop(): return lax.ppermute(x, 'segment', [(i, i + 2) for i in range(6)])  10.2 us
    ppermute x3, waiting for transfers between devices, shards(): lax.ppermute(both[:, :, (3 + d) % 4], 'segment', [(6, (6 + 2 * d) % 8), (...  7.08 us
  transfers between devices with their start and end apart: 27, of which 16 were waited for; matrix products, arithmetic and copies ran while one was open for 1% of the time, Pallas kernels for 12%

profile of v5, /device:TPU:18, one launch (start us, length us, event | category | flops | bytes accessed | tf_op | source)
XLA Modules:
  0.0 273.5 jit_solution(6820729011706451480)
XLA Ops:
  0.0 1.2 fusion.2
  1.2 0.1 collective-permute-start.1
  1.4 1.8 collective-permute-done.1
  3.2 0.2 select_bitcast_fusion.4
  3.4 0.1 fusion
  3.5 0.2 collective-permute-start.6
  3.7 0.4 collective-permute-start.7
  4.1 4.0 %collective-permute-start.3 = (bf16[2,256,640]{2,1,0:T(8,128)(2,1)S(1)}, bf16[2,256,640]{2,1,0:T(8,128)(2,1)S(1)}, u32[]{:S(2)}, u32[]{:S(2)}) collective-permute-start(bf16[2,256,640]{2,1,0:T(8,128)(2,1)S(1)} %fusion), channel_id=1, source_target_pairs={{0,3},{1,0},{2,1},{3,2},{4,7},{5,4},{6,5},{7,6},{8,11},{9,8},{10,9... | collective-permute-start | bytes 1966088 | tf_op jit(solution)/shard_map/ppermute | solution.py:295
  8.1 1.2 collective-permute-done.8
  9.3 0.2 collective-permute-start.9
  9.4 1.0 collective-permute-done.9
  10.5 5.7 %collective-permute-done.3 = bf16[2,256,640]{2,1,0:T(8,128)(2,1)S(1)} collective-permute-done((bf16[2,256,640]{2,1,0:T(8,128)(2,1)S(1)}, bf16[2,256,640]{2,1,0:T(8,128)(2,1)S(1)}, u32[]{:S(2)}, u32[]{:S(2)}) %collective-permute-start.3) | collective-permute-done | bytes 655392 | tf_op jit(solution)/shard_map/ppermute | solution.py:295
  16.2 3.8 %collective-permute-start.5 = (bf16[1,256,640]{2,1,0:T(8,128)(2,1)S(1)}, bf16[1,256,640]{2,1,0:T(8,128)(2,1)S(1)}, u32[]{:S(2)}, u32[]{:S(2)}) collective-permute-start(bf16[1,256,640]{2,1,0:T(8,128)(2,1)S(1)} %slice.43), channel_id=1, source_target_pairs={{0,3},{1,0},{2,1},{3,2},{4,7},{5,4},{6,5},{7,6},{8,11},{9,8},{10,9... | collective-permute-start | bytes 983048 | tf_op jit(solution)/shard_map/ppermute | solution.py:295
  20.0 0.1 collective-permute-start.4
  20.2 0.3 select_bitcast_fusion.1
  20.5 0.6 copy-done.7
  21.1 0.3 copy-done.9
  21.3 1.3 pad_maximum_fusion.1.wv_ref
  22.7 1.4 pad_maximum_fusion.wk_ref
  24.1 0.5 collective-permute-done.5
  24.6 3.8 %collective-permute-done.4 = bf16[1,256,640]{2,1,0:T(8,128)(2,1)S(1)} collective-permute-done((bf16[1,256,640]{2,1,0:T(8,128)(2,1)S(1)}, bf16[1,256,640]{2,1,0:T(8,128)(2,1)S(1)}, u32[]{:S(2)}, u32[]{:S(2)}) %collective-permute-start.4) | collective-permute-done | bytes 327712 | tf_op jit(solution)/shard_map/ppermute | solution.py:295
  28.5 0.1 pad_maximum_fusion.3.far_ref
  28.6 0.5 collective-permute-start.12
  29.1 0.1 pad_maximum_fusion.2.near_ref
  29.3 1.6 collective-permute-start.10
  30.9 8.5 %stale.4 = (bf16[2,5,1024,128]{3,2,1,0:T(8,128)(2,1)}, bf16[2,5,128,1024]{3,2,1,0:T(8,128)(2,1)}) custom-call(bf16[2,2,256,640]{3,2,1,0:T(8,128)(2,1)S(1)} %pad_maximum_fusion.2.near_ref, bf16[2,2,256,640]{3,2,1,0:T(8,128)(2,1)S(1)} %pad_maximum_fusion.3.far_ref, f32[2,640]{1,0:T(2,128)S(1)} %pad_maximum_fusion.6.ga_ref, ...), custom_call_target="tpu_custom_call" | custom-call | flops 3355443200 | bytes 7864320 | tf_op jit(solution)/shard_map/stale/pallas_call | solution.py:68
  39.4 2.5 collective-permute-start.14
  41.9 4.4 %collective-permute-done.12.far_ref = bf16[2,2,256,640]{3,2,1,0:T(8,128)(2,1)S(1)} collective-permute-done((bf16[2,2,256,640]{3,2,1,0:T(8,128)(2,1)S(1)}, bf16[2,2,256,640]{3,2,1,0:T(8,128)(2,1)S(1)}, u32[]{:S(2)}, u32[]{:S(2)}) %collective-permute-start.12) | collective-permute-done | bytes 1310752 | tf_op jit(solution)/shard_map/ppermute | solution.py:295
  46.3 0.5 collective-permute-start.13
  46.7 0.2 collective-permute-done.10.near_ref
  47.0 1.8 collective-permute-start.11
  48.8 8.4 %stale.5 = (bf16[2,5,1024,128]{3,2,1,0:T(8,128)(2,1)}, bf16[2,5,128,1024]{3,2,1,0:T(8,128)(2,1)}) custom-call(bf16[2,2,256,640]{3,2,1,0:T(8,128)(2,1)S(1)} %collective-permute-done.10.near_ref, bf16[2,2,256,640]{3,2,1,0:T(8,128)(2,1)S(1)} %collective-permute-done.12.far_ref, f32[2,640]{1,0:T(2,128)S(1)} %pad_maximum_fusion.6.ga_ref, ...), custom_call_target="tpu_custom_call" | custom-call | flops 3355443200 | bytes 7864320 | tf_op jit(solution)/shard_map/stale/pallas_call | solution.py:68
  57.3 3.7 %collective-permute-done.14.near_ref = bf16[2,2,256,640]{3,2,1,0:T(8,128)(2,1)S(1)} collective-permute-done((bf16[2,2,256,640]{3,2,1,0:T(8,128)(2,1)S(1)}, bf16[2,2,256,640]{3,2,1,0:T(8,128)(2,1)S(1)}, u32[]{:S(2)}, u32[]{:S(2)}) %collective-permute-start.14) | collective-permute-done | bytes 1310752 | tf_op jit(solution)/shard_map/ppermute | solution.py:295
  61.0 2.7 collective-permute-start.17
  63.8 3.3 %collective-permute-start.16 = (bf16[2,64,640]{2,1,0:T(8,128)(2,1)S(1)}, bf16[2,64,640]{2,1,0:T(8,128)(2,1)S(1)}, u32[]{:S(2)}, u32[]{:S(2)}) collective-permute-start(bf16[2,64,640]{2,1,0:T(8,128)(2,1)S(1)} %get-tuple-element.493), channel_id=1, source_target_pairs={{0,1},{1,2},{2,3},{3,4},{4,5},{5,6},{6,7},{7,8},{8,9},{9,10},{10,1... | collective-permute-start | bytes 491528 | tf_op jit(solution)/shard_map/ppermute | solution.py:352
  67.1 8.4 %stale.6 = (bf16[2,5,1024,128]{3,2,1,0:T(8,128)(2,1)}, bf16[2,5,128,1024]{3,2,1,0:T(8,128)(2,1)}) custom-call(bf16[2,2,256,640]{3,2,1,0:T(8,128)(2,1)S(1)} %collective-permute-done.14.near_ref, bf16[2,2,256,640]{3,2,1,0:T(8,128)(2,1)S(1)} %collective-permute-done.15.far_ref, f32[2,640]{1,0:T(2,128)S(1)} %pad_maximum_fusion.6.ga_ref, ...), custom_call_target="tpu_custom_call" | custom-call | flops 3355443200 | bytes 7864320 | tf_op jit(solution)/shard_map/stale/pallas_call | solution.py:68
  75.5 0.4 collective-permute-done.17
  75.9 2.1 collective-permute-done.16
  78.0 0.7 collective-permute-start.18
  78.7 0.1 collective-permute-start.19
  78.9 8.7 %stale.7 = (bf16[2,5,1024,128]{3,2,1,0:T(8,128)(2,1)}, bf16[2,5,128,1024]{3,2,1,0:T(8,128)(2,1)}) custom-call(bf16[2,2,256,640]{3,2,1,0:T(8,128)(2,1)S(1)} %collective-permute-done.11.near_ref, bf16[2,2,256,640]{3,2,1,0:T(8,128)(2,1)S(1)} %collective-permute-done.13.far_ref, f32[2,640]{1,0:T(2,128)S(1)} %pad_maximum_fusion.6.ga_ref, ...), custom_call_target="tpu_custom_call" | custom-call | flops 3355443200 | bytes 7864320 | tf_op jit(solution)/shard_map/stale/pallas_call | solution.py:68
  87.6 0.9 copy-done.14
  88.5 0.3 copy-done.15
  88.8 172.6 %while.13 = (s32[]{:T(128)}, bf16[256,640]{1,0:T(8,128)(2,1)S(1)}, f32[2,640]{1,0:T(2,128)S(1)}, f32[2,640]{1,0:T(2,128)S(1)}, bf16[2,64,640]{2,1,0:T(8,128)(2,1...) while((s32[]{:T(128)}, bf16[256,640]{1,0:T(8,128)(2,1)S(1)}, ...), condition=%wide.region_3.4_spmd, body=%wide.region_0.3_spmd.sunk | while | flops 25999998976 | bytes 46621728 | solution.py:371
  88.8 34.2 %blocks.5 = bf16[256,640]{1,0:T(8,128)(2,1)S(1)} custom-call(bf16[256,640]{1,0:T(8,128)(2,1)S(1)} %get-tuple-element.674.refs_0_, f32[2,640]{1,0:T(2,128)S(1)} %get-tuple-element.701.refs_1_, f32[2,640]{1,0:T(2,128)S(1)} %get-tuple-element.702.refs_2_, bf16[2,64,640]{2,1,0:T(8,128)(2,1)} %get-tuple-element.703.refs_3_, ...), custom_call_target="tpu_custom_call" | custom-call | flops 25999998976 | bytes 44000000 | tf_op jit(solution)/shard_map/while/body/eval_jaxpr/blocks/pallas_call | solution.py:244
  123.0 12.3 %conditional.2 = (bf16[256,640]{1,0:T(8,128)(2,1)S(1)}) conditional(s32[]{:T(128)} %convert_element_type.13, bf16[256,640]{1,0:T(8,128)(2,1)S(1)} %blocks.5, bf16[256,640]{1,0:T(8,128)(2,1)S(1)} %blocks.5), branch_computations={%region_1.1_spmd, %region_2.2_spmd} | conditional | bytes 1966128 | solution.py:369
  123.0 3.4 %collective-permute-start = (bf16[256,640]{1,0:T(8,128)(2,1)S(1)}, bf16[256,640]{1,0:T(8,128)(2,1)S(1)}, u32[]{:S(2)}, u32[]{:S(2)}) collective-permute-start(bf16[256,640]{1,0:T(8,128)(2,1)S(1)} %param.1), channel_id=1, source_target_pairs={{0,32},{16,48},{32,64},{48,80},{64,96},{80,112},{1,33},{17,49},{33... | collective-permute-start | bytes 983048 | tf_op jit(solution)/shard_map/while/body/eval_jaxpr/cond/branch_1_fun/ppermute | solution.py:366
  126.4 8.9 %collective-permute-done = bf16[256,640]{1,0:T(8,128)(2,1)S(1)} collective-permute-done((bf16[256,640]{1,0:T(8,128)(2,1)S(1)}, bf16[256,640]{1,0:T(8,128)(2,1)S(1)}, u32[]{:S(2)}, u32[]{:S(2)}) %collective-permute-start) | collective-permute-done | bytes 327712 | tf_op jit(solution)/shard_map/while/body/eval_jaxpr/cond/branch_1_fun/ppermute | solution.py:366
  135.4 34.2 %blocks.5 = bf16[256,640]{1,0:T(8,128)(2,1)S(1)} custom-call(bf16[256,640]{1,0:T(8,128)(2,1)S(1)} %get-tuple-element.674.refs_0_, f32[2,640]{1,0:T(2,128)S(1)} %get-tuple-element.701.refs_1_, f32[2,640]{1,0:T(2,128)S(1)} %get-tuple-element.702.refs_2_, bf16[2,64,640]{2,1,0:T(8,128)(2,1)} %get-tuple-element.703.refs_3_, ...), custom_call_target="tpu_custom_call" | custom-call | flops 25999998976 | bytes 44000000 | tf_op jit(solution)/shard_map/while/body/eval_jaxpr/blocks/pallas_call | solution.py:244
  169.6 11.8 %conditional.2 = (bf16[256,640]{1,0:T(8,128)(2,1)S(1)}) conditional(s32[]{:T(128)} %convert_element_type.13, bf16[256,640]{1,0:T(8,128)(2,1)S(1)} %blocks.5, bf16[256,640]{1,0:T(8,128)(2,1)S(1)} %blocks.5), branch_computations={%region_1.1_spmd, %region_2.2_spmd} | conditional | bytes 1966128 | solution.py:369
  169.6 3.4 %collective-permute-start = (bf16[256,640]{1,0:T(8,128)(2,1)S(1)}, bf16[256,640]{1,0:T(8,128)(2,1)S(1)}, u32[]{:S(2)}, u32[]{:S(2)}) collective-permute-start(bf16[256,640]{1,0:T(8,128)(2,1)S(1)} %param.1), channel_id=1, source_target_pairs={{0,32},{16,48},{32,64},{48,80},{64,96},{80,112},{1,33},{17,49},{33... | collective-permute-start | bytes 983048 | tf_op jit(solution)/shard_map/while/body/eval_jaxpr/cond/branch_1_fun/ppermute | solution.py:366
  173.0 8.4 %collective-permute-done = bf16[256,640]{1,0:T(8,128)(2,1)S(1)} collective-permute-done((bf16[256,640]{1,0:T(8,128)(2,1)S(1)}, bf16[256,640]{1,0:T(8,128)(2,1)S(1)}, u32[]{:S(2)}, u32[]{:S(2)}) %collective-permute-start) | collective-permute-done | bytes 327712 | tf_op jit(solution)/shard_map/while/body/eval_jaxpr/cond/branch_1_fun/ppermute | solution.py:366
  181.5 34.2 %blocks.5 = bf16[256,640]{1,0:T(8,128)(2,1)S(1)} custom-call(bf16[256,640]{1,0:T(8,128)(2,1)S(1)} %get-tuple-element.674.refs_0_, f32[2,640]{1,0:T(2,128)S(1)} %get-tuple-element.701.refs_1_, f32[2,640]{1,0:T(2,128)S(1)} %get-tuple-element.702.refs_2_, bf16[2,64,640]{2,1,0:T(8,128)(2,1)} %get-tuple-element.703.refs_3_, ...), custom_call_target="tpu_custom_call" | custom-call | flops 25999998976 | bytes 44000000 | tf_op jit(solution)/shard_map/while/body/eval_jaxpr/blocks/pallas_call | solution.py:244
  215.7 11.4 %conditional.2 = (bf16[256,640]{1,0:T(8,128)(2,1)S(1)}) conditional(s32[]{:T(128)} %convert_element_type.13, bf16[256,640]{1,0:T(8,128)(2,1)S(1)} %blocks.5, bf16[256,640]{1,0:T(8,128)(2,1)S(1)} %blocks.5), branch_computations={%region_1.1_spmd, %region_2.2_spmd} | conditional | bytes 1966128 | solution.py:369
  215.7 3.4 %collective-permute-start = (bf16[256,640]{1,0:T(8,128)(2,1)S(1)}, bf16[256,640]{1,0:T(8,128)(2,1)S(1)}, u32[]{:S(2)}, u32[]{:S(2)}) collective-permute-start(bf16[256,640]{1,0:T(8,128)(2,1)S(1)} %param.1), channel_id=1, source_target_pairs={{0,32},{16,48},{32,64},{48,80},{64,96},{80,112},{1,33},{17,49},{33... | collective-permute-start | bytes 983048 | tf_op jit(solution)/shard_map/while/body/eval_jaxpr/cond/branch_1_fun/ppermute | solution.py:366
  219.1 7.9 %collective-permute-done = bf16[256,640]{1,0:T(8,128)(2,1)S(1)} collective-permute-done((bf16[256,640]{1,0:T(8,128)(2,1)S(1)}, bf16[256,640]{1,0:T(8,128)(2,1)S(1)}, u32[]{:S(2)}, u32[]{:S(2)}) %collective-permute-start) | collective-permute-done | bytes 327712 | tf_op jit(solution)/shard_map/while/body/eval_jaxpr/cond/branch_1_fun/ppermute | solution.py:366
  227.2 34.2 %blocks.5 = bf16[256,640]{1,0:T(8,128)(2,1)S(1)} custom-call(bf16[256,640]{1,0:T(8,128)(2,1)S(1)} %get-tuple-element.674.refs_0_, f32[2,640]{1,0:T(2,128)S(1)} %get-tuple-element.701.refs_1_, f32[2,640]{1,0:T(2,128)S(1)} %get-tuple-element.702.refs_2_, bf16[2,64,640]{2,1,0:T(8,128)(2,1)} %get-tuple-element.703.refs_3_, ...), custom_call_target="tpu_custom_call" | custom-call | flops 25999998976 | bytes 44000000 | tf_op jit(solution)/shard_map/while/body/eval_jaxpr/blocks/pallas_call | solution.py:244
  261.5 0.1 collective-permute-start.21
  261.6 1.4 collective-permute-done.21
  263.1 0.7 collective-permute-start.22
  263.7 0.7 collective-permute-start.24
  264.4 1.3 collective-permute-start.23
  265.7 7.1 %collective-permute-done.23 = bf16[2,4,8,640]{3,2,1,0:T(8,128)(2,1)S(1)} collective-permute-done((bf16[2,4,8,640]{3,2,1,0:T(8,128)(2,1)S(1)}, bf16[2,4,8,640]{3,2,1,0:T(8,128)(2,1)S(1)}, u32[]{:S(2)}, u32[]{:S(2)}) %collective-permute-start.23) | collective-permute-done | bytes 81952 | tf_op jit(solution)/shard_map/ppermute | solution.py:379
  272.8 0.7 fusion.13
  (68 shorter events, 0.7 us)
Async XLA Ops:
  0.0 78.8 %copy-start = (bf16[2,4,64,640]{3,2,1,0:T(8,128)(2,1)S(1)}, bf16[2,4,64,640]{3,2,1,0:T(8,128)(2,1)}, u32[]{:S(2)}) copy-start(bf16[2,4,64,640]{3,2,1,0:T(8,128)(2,1)} %param.14) | copy-start | bytes 1966084
  0.0 3.2 %copy-start.3 = (bf16[1,2,2,64,640]{4,3,2,1,0:T(8,128)(2,1)S(1)}, bf16[1,2,2,64,640]{4,3,2,1,0:T(8,128)(2,1)}, u32[]{:S(2)}) copy-start(bf16[1,2,2,64,640]{4,3,2,1,0:T(8,128)(2,1)} %param.16) | copy-start | bytes 983044
  0.0 3.2 %copy-start.2 = (bf16[1,2,4,64,640]{4,3,2,1,0:T(8,128)(2,1)S(1)}, bf16[1,2,4,64,640]{4,3,2,1,0:T(8,128)(2,1)}, u32[]{:S(2)}) copy-start(bf16[1,2,4,64,640]{4,3,2,1,0:T(8,128)(2,1)} %param.15) | copy-start | bytes 1966084
  1.2 1.9 collective-permute-start.1
  1.3 2.2 copy-start.4
  1.3 2.4 copy-start.5
  1.3 6.8 %copy-start.11 = (f32[1,640]{1,0:T(1,128)S(1)}, f32[1,640]{1,0:T(1,128)}, u32[]{:S(2)}) copy-start(f32[1,640]{1,0:T(1,128)} %param.17) | copy-start | bytes 7684
  1.4 7.9 %copy-start.10 = (f32[1,640]{1,0:T(1,128)S(1)}, f32[1,640]{1,0:T(1,128)}, u32[]{:S(2)}) copy-start(f32[1,640]{1,0:T(1,128)} %param.22) | copy-start | bytes 7684
  3.5 16.7 %collective-permute-start.6 = (bf16[640,640]{1,0:T(8,128)(2,1)S(1)}, bf16[640,640]{1,0:T(8,128)(2,1)S(1)}, u32[]{:S(2)}, u32[]{:S(2)}) collective-permute-start(bf16[640,640]{1,0:T(8,128)(2,1)S(1)} %bitcast.84), channel_id=1, source_target_pairs={{0,16},{16,0},{32,48},{48,32},{64,80},{80,64},{96,112},{112,96},{1... | collective-permute-start | bytes 2457608 | tf_op jit(solution)/shard_map/ppermute | solution.py:315
  3.7 16.5 %collective-permute-start.7 = (bf16[640,640]{1,0:T(8,128)(2,1)S(1)}, bf16[640,640]{1,0:T(8,128)(2,1)S(1)}, u32[]{:S(2)}, u32[]{:S(2)}) collective-permute-start(bf16[640,640]{1,0:T(8,128)(2,1)S(1)} %bitcast.86), channel_id=1, source_target_pairs={{0,16},{16,0},{32,48},{48,32},{64,80},{80,64},{96,112},{112,96},{1... | collective-permute-start | bytes 2457608 | tf_op jit(solution)/shard_map/ppermute | solution.py:315
  4.1 12.1 %collective-permute-start.3 = (bf16[2,256,640]{2,1,0:T(8,128)(2,1)S(1)}, bf16[2,256,640]{2,1,0:T(8,128)(2,1)S(1)}, u32[]{:S(2)}, u32[]{:S(2)}) collective-permute-start(bf16[2,256,640]{2,1,0:T(8,128)(2,1)S(1)} %fusion), channel_id=1, source_target_pairs={{0,3},{1,0},{2,1},{3,2},{4,7},{5,4},{6,5},{7,6},{8,11},{9,8},{10,9... | collective-permute-start | bytes 1966088 | tf_op jit(solution)/shard_map/ppermute | solution.py:295
  8.1 11.9 %collective-permute-start.2 = (bf16[2,256,640]{2,1,0:T(8,128)(2,1)S(1)}, bf16[2,256,640]{2,1,0:T(8,128)(2,1)S(1)}, u32[]{:S(2)}, u32[]{:S(2)}) collective-permute-start(bf16[2,256,640]{2,1,0:T(8,128)(2,1)S(1)} %fusion), channel_id=1, source_target_pairs={{0,1},{1,2},{2,3},{3,0},{4,5},{5,6},{6,7},{7,4},{8,9},{9,10},{10,1... | collective-permute-start | bytes 1966088 | tf_op jit(solution)/shard_map/ppermute | solution.py:295
  8.1 1.2 collective-permute-start.8
  9.3 1.2 collective-permute-start.9
  16.2 8.4 %collective-permute-start.5 = (bf16[1,256,640]{2,1,0:T(8,128)(2,1)S(1)}, bf16[1,256,640]{2,1,0:T(8,128)(2,1)S(1)}, u32[]{:S(2)}, u32[]{:S(2)}) collective-permute-start(bf16[1,256,640]{2,1,0:T(8,128)(2,1)S(1)} %slice.43), channel_id=1, source_target_pairs={{0,3},{1,0},{2,1},{3,2},{4,7},{5,4},{6,5},{7,6},{8,11},{9,8},{10,9... | collective-permute-start | bytes 983048 | tf_op jit(solution)/shard_map/ppermute | solution.py:295
  20.0 8.4 %collective-permute-start.4 = (bf16[1,256,640]{2,1,0:T(8,128)(2,1)S(1)}, bf16[1,256,640]{2,1,0:T(8,128)(2,1)S(1)}, u32[]{:S(2)}, u32[]{:S(2)}) collective-permute-start(bf16[1,256,640]{2,1,0:T(8,128)(2,1)S(1)} %slice.42), channel_id=1, source_target_pairs={{0,1},{1,2},{2,3},{3,0},{4,5},{5,6},{6,7},{7,4},{8,9},{9,10},{10,1... | collective-permute-start | bytes 983048 | tf_op jit(solution)/shard_map/ppermute | solution.py:295
  20.1 0.9 copy-start.7
  20.2 1.2 copy-start.9
  28.4 59.2 %collective-permute-start.20 = (bf16[9,640,640]{2,1,0:T(8,128)(2,1)}, bf16[9,640,640]{2,1,0:T(8,128)(2,1)}, u32[]{:S(2)}, u32[]{:S(2)}) collective-permute-start(bf16[9,640,640]{2,1,0:T(8,128)(2,1)} %bitcast.13), channel_id=1, source_target_pairs={{0,16},{16,0},{32,48},{48,32},{64,80},{80,64},{96,112},{112,96},{1... | collective-permute-start | bytes 22118408 | tf_op jit(solution)/shard_map/ppermute | solution.py:315
  28.6 17.7 %collective-permute-start.12 = (bf16[2,2,256,640]{3,2,1,0:T(8,128)(2,1)S(1)}, bf16[2,2,256,640]{3,2,1,0:T(8,128)(2,1)S(1)}, u32[]{:S(2)}, u32[]{:S(2)}) collective-permute-start(bf16[2,2,256,640]{3,2,1,0:T(8,128)(2,1)S(1)} %pad_maximum_fusion.3.far_ref), channel_id=1, source_target_pairs={{0,12},{1,13},{2,14},{3,15},{4,0},{5,1},{6,2},{7,3},{8,4},{9,5},{1... | collective-permute-start | bytes 3932168 | tf_op jit(solution)/shard_map/ppermute | solution.py:295
  29.3 17.7 %collective-permute-start.10 = (bf16[2,2,256,640]{3,2,1,0:T(8,128)(2,1)S(1)}, bf16[2,2,256,640]{3,2,1,0:T(8,128)(2,1)S(1)}, u32[]{:S(2)}, u32[]{:S(2)}) collective-permute-start(bf16[2,2,256,640]{3,2,1,0:T(8,128)(2,1)S(1)} %pad_maximum_fusion.2.near_ref), channel_id=1, source_target_pairs={{0,4},{1,5},{2,6},{3,7},{4,8},{5,9},{6,10},{7,11},{8,12},{9,13},{1... | collective-permute-start | bytes 3932168 | tf_op jit(solution)/shard_map/ppermute | solution.py:295
  39.4 21.6 %collective-permute-start.14 = (bf16[2,2,256,640]{3,2,1,0:T(8,128)(2,1)S(1)}, bf16[2,2,256,640]{3,2,1,0:T(8,128)(2,1)S(1)}, u32[]{:S(2)}, u32[]{:S(2)}) collective-permute-start(bf16[2,2,256,640]{3,2,1,0:T(8,128)(2,1)S(1)} %pad_maximum_fusion.3.far_ref), channel_id=1, source_target_pairs={{0,4},{1,5},{2,6},{3,7},{4,8},{5,9},{6,10},{7,11},{8,12},{9,13},{1... | collective-permute-start | bytes 3932168 | tf_op jit(solution)/shard_map/ppermute | solution.py:295
  41.9 19.1 %collective-permute-start.15 = (bf16[2,2,256,640]{3,2,1,0:T(8,128)(2,1)S(1)}, bf16[2,2,256,640]{3,2,1,0:T(8,128)(2,1)S(1)}, u32[]{:S(2)}, u32[]{:S(2)}) collective-permute-start(bf16[2,2,256,640]{3,2,1,0:T(8,128)(2,1)S(1)} %pad_maximum_fusion.2.near_ref), channel_id=1, source_target_pairs={{0,12},{1,13},{2,14},{3,15},{4,0},{5,1},{6,2},{7,3},{8,4},{9,5},{1... | collective-permute-start | bytes 3932168 | tf_op jit(solution)/shard_map/ppermute | solution.py:295
  46.3 31.7 %collective-permute-start.13 = (bf16[2,2,256,640]{3,2,1,0:T(8,128)(2,1)S(1)}, bf16[2,2,256,640]{3,2,1,0:T(8,128)(2,1)S(1)}, u32[]{:S(2)}, u32[]{:S(2)}) collective-permute-start(bf16[2,2,256,640]{3,2,1,0:T(8,128)(2,1)S(1)} %collective-permute-done.12.far_ref), channel_id=1, source_target_pairs={{0,12},{1,13},{2,14},{3,15},{4,0},{5,1},{6,2},{7,3},{8,4},{9,5},{1... | collective-permute-start | bytes 3932168 | tf_op jit(solution)/shard_map/ppermute | solution.py:295
  47.0 31.1 %collective-permute-start.11 = (bf16[2,2,256,640]{3,2,1,0:T(8,128)(2,1)S(1)}, bf16[2,2,256,640]{3,2,1,0:T(8,128)(2,1)S(1)}, u32[]{:S(2)}, u32[]{:S(2)}) collective-permute-start(bf16[2,2,256,640]{3,2,1,0:T(8,128)(2,1)S(1)} %collective-permute-done.10.near_ref), channel_id=1, source_target_pairs={{0,4},{1,5},{2,6},{3,7},{4,8},{5,9},{6,10},{7,11},{8,12},{9,13},{1... | collective-permute-start | bytes 3932168 | tf_op jit(solution)/shard_map/ppermute | solution.py:295
  61.0 14.8 %collective-permute-start.17 = (bf16[2,64,640]{2,1,0:T(8,128)(2,1)S(1)}, bf16[2,64,640]{2,1,0:T(8,128)(2,1)S(1)}, u32[]{:S(2)}, u32[]{:S(2)}) collective-permute-start(bf16[2,64,640]{2,1,0:T(8,128)(2,1)S(1)} %get-tuple-element.492), channel_id=1, source_target_pairs={{1,0},{2,1},{3,2},{4,3},{5,4},{6,5},{7,6},{8,7},{9,8},{10,9},{11,1... | collective-permute-start | bytes 491528 | tf_op jit(solution)/shard_map/ppermute | solution.py:353
  63.7 14.3 %copy-start.12 = (bf16[1,640,640]{2,1,0:T(8,128)(2,1)S(1)}, bf16[1,640,640]{2,1,0:T(8,128)(2,1)}, u32[]{:S(2)}) copy-start(bf16[1,640,640]{2,1,0:T(8,128)(2,1)} %param.18) | copy-start | bytes 2457604
  63.7 15.0 %copy-start.13 = (bf16[1,640,640]{2,1,0:T(8,128)(2,1)S(1)}, bf16[1,640,640]{2,1,0:T(8,128)(2,1)}, u32[]{:S(2)}) copy-start(bf16[1,640,640]{2,1,0:T(8,128)(2,1)} %param.21) | copy-start | bytes 2457604
  63.8 14.2 %collective-permute-start.16 = (bf16[2,64,640]{2,1,0:T(8,128)(2,1)S(1)}, bf16[2,64,640]{2,1,0:T(8,128)(2,1)S(1)}, u32[]{:S(2)}, u32[]{:S(2)}) collective-permute-start(bf16[2,64,640]{2,1,0:T(8,128)(2,1)S(1)} %get-tuple-element.493), channel_id=1, source_target_pairs={{0,1},{1,2},{2,3},{3,4},{4,5},{5,6},{6,7},{7,8},{8,9},{9,10},{10,1... | collective-permute-start | bytes 491528 | tf_op jit(solution)/shard_map/ppermute | solution.py:352
  75.9 11.7 %copy-start.16 = (bf16[2,64,640]{2,1,0:T(8,128)(2,1)}, bf16[2,64,640]{2,1,0:T(8,128)(2,1)S(1)}, u32[]{:S(2)}) copy-start(bf16[2,64,640]{2,1,0:T(8,128)(2,1)S(1)} %collective-permute-done.17) | copy-start | bytes 491524
  78.0 9.6 %copy-start.17 = (bf16[2,64,640]{2,1,0:T(8,128)(2,1)}, bf16[2,64,640]{2,1,0:T(8,128)(2,1)S(1)}, u32[]{:S(2)}) copy-start(bf16[2,64,640]{2,1,0:T(8,128)(2,1)S(1)} %collective-permute-done.16) | copy-start | bytes 491524
  78.0 9.6 %collective-permute-start.18 = (bf16[640,640]{1,0:T(8,128)(2,1)S(1)}, bf16[640,640]{1,0:T(8,128)(2,1)S(1)}, u32[]{:S(2)}, u32[]{:S(2)}) collective-permute-start(bf16[640,640]{1,0:T(8,128)(2,1)S(1)} %bitcast.90), channel_id=1, source_target_pairs={{0,16},{16,0},{32,48},{48,32},{64,80},{80,64},{96,112},{112,96},{1... | collective-permute-start | bytes 2457608 | tf_op jit(solution)/shard_map/ppermute | solution.py:315
  78.7 8.9 %collective-permute-start.19 = (bf16[640,640]{1,0:T(8,128)(2,1)S(1)}, bf16[640,640]{1,0:T(8,128)(2,1)S(1)}, u32[]{:S(2)}, u32[]{:S(2)}) collective-permute-start(bf16[640,640]{1,0:T(8,128)(2,1)S(1)} %bitcast.92), channel_id=1, source_target_pairs={{0,16},{16,0},{32,48},{48,32},{64,80},{80,64},{96,112},{112,96},{1... | collective-permute-start | bytes 2457608 | tf_op jit(solution)/shard_map/ppermute | solution.py:315
  78.8 10.0 %copy-start.6 = (bf16[1,640,640]{2,1,0:T(8,128)(2,1)S(1)}, bf16[1,640,640]{2,1,0:T(8,128)(2,1)}, u32[]{:S(2)}) copy-start(bf16[1,640,640]{2,1,0:T(8,128)(2,1)} %param.20) | copy-start | bytes 2457604
  78.9 10.0 %copy-start.8 = (bf16[640,640]{1,0:T(8,128)(2,1)S(1)}, bf16[640,640]{1,0:T(8,128)(2,1)}, u32[]{:S(2)}) copy-start(bf16[640,640]{1,0:T(8,128)(2,1)} %copy-done.7) | copy-start | bytes 2457604
  87.6 0.9 copy-start.14
  87.6 1.2 copy-start.15
  123.0 12.3 %collective-permute-start = (bf16[256,640]{1,0:T(8,128)(2,1)S(1)}, bf16[256,640]{1,0:T(8,128)(2,1)S(1)}, u32[]{:S(2)}, u32[]{:S(2)}) collective-permute-start(bf16[256,640]{1,0:T(8,128)(2,1)S(1)} %param.1), channel_id=1, source_target_pairs={{0,32},{16,48},{32,64},{48,80},{64,96},{80,112},{1,33},{17,49},{33... | collective-permute-start | bytes 983048 | tf_op jit(solution)/shard_map/while/body/eval_jaxpr/cond/branch_1_fun/ppermute | solution.py:366
  169.6 11.8 %collective-permute-start = (bf16[256,640]{1,0:T(8,128)(2,1)S(1)}, bf16[256,640]{1,0:T(8,128)(2,1)S(1)}, u32[]{:S(2)}, u32[]{:S(2)}) collective-permute-start(bf16[256,640]{1,0:T(8,128)(2,1)S(1)} %param.1), channel_id=1, source_target_pairs={{0,32},{16,48},{32,64},{48,80},{64,96},{80,112},{1,33},{17,49},{33... | collective-permute-start | bytes 983048 | tf_op jit(solution)/shard_map/while/body/eval_jaxpr/cond/branch_1_fun/ppermute | solution.py:366
  215.7 11.4 %collective-permute-start = (bf16[256,640]{1,0:T(8,128)(2,1)S(1)}, bf16[256,640]{1,0:T(8,128)(2,1)S(1)}, u32[]{:S(2)}, u32[]{:S(2)}) collective-permute-start(bf16[256,640]{1,0:T(8,128)(2,1)S(1)} %param.1), channel_id=1, source_target_pairs={{0,32},{16,48},{32,64},{48,80},{64,96},{80,112},{1,33},{17,49},{33... | collective-permute-start | bytes 983048 | tf_op jit(solution)/shard_map/while/body/eval_jaxpr/cond/branch_1_fun/ppermute | solution.py:366
  261.4 12.1 %copy-start.1 = (bf16[2,4,64,640]{3,2,1,0:T(8,128)(2,1)S(1)}, bf16[2,4,64,640]{3,2,1,0:T(8,128)(2,1)}, u32[]{:S(2)}) copy-start(bf16[2,4,64,640]{3,2,1,0:T(8,128)(2,1)} %param.14) | copy-start | bytes 1966084
  261.5 1.5 collective-permute-start.21
  263.1 2.7 collective-permute-start.22
  263.7 2.0 collective-permute-start.24
  264.4 8.4 %collective-permute-start.23 = (bf16[2,4,8,640]{3,2,1,0:T(8,128)(2,1)S(1)}, bf16[2,4,8,640]{3,2,1,0:T(8,128)(2,1)S(1)}, u32[]{:S(2)}, u32[]{:S(2)}) collective-permute-start(bf16[2,4,8,640]{3,2,1,0:T(8,128)(2,1)S(1)} %get-tuple-element.487), channel_id=1, source_target_pairs={{96,32},{112,48},{97,33},{113,49},{98,34},{114,50},{99,35},{115,51... | collective-permute-start | bytes 245768 | tf_op jit(solution)/shard_map/ppermute | solution.py:379

commit v6 on v5

--- a/solution.py
+++ b/solution.py
@@ -344,8 +344,8 @@
     row = jnp.stack([raw, back]), jnp.stack([jnp.concatenate(far, 0), ahead])
     first = turned(row[0], 1, 1), turned(row[1], 1, -1)
     stored = [stale_call(row, gains, wk, wv)]
-    row, stored = lax.optimization_barrier((row, stored))
     second = turned(row[1], 1, 1), turned(row[0], 1, -1)
+    first, stored = lax.optimization_barrier((first, stored))
     far = turned(first[0], 1, 1), turned(first[1], 1, -1)
     stored.append(stale_call(first, gains, wk, wv))
     second, stored, edges = lax.optimization_barrier((second, stored, edges))

time: 274 us -> 274 us (level)
  no operation moved by 1% of the time
where the time goes in v6:
time: 274 us; the launch traced here: 273 us
  Pallas kernels  171 us (62%)
  waiting for transfers between devices  58.8 us (21%)
  starting transfers between devices  35.1 us (13%)
  other arithmetic  5.69 us (2%)
    pallas_call x4, Pallas kernels, block_call(): pl.pallas_call(block_kernel, out_shape=jax.ShapeDtypeStruct((CELLS, C), B...  137 us
    pallas_call x4, Pallas kernels, stale_call(): pl.pallas_call(stale_kernel, grid=(2,), out_shape=[jax.ShapeDtypeStruct((...  34 us
    ppermute x3, waiting for transfers between devices, hop(): return lax.ppermute(x, 'segment', [(i, i + 2) for i in range(6)])  25.2 us
    ppermute x10, waiting for transfers between devices, turned(): return lax.ppermute(value, ('segment', 'patch'), pairs)  18.7 us
    ppermute x10, starting transfers between devices, turned(): return lax.ppermute(value, ('segment', 'patch'), pairs)  14.6 us
    ppermute x3, starting transfers between devices, hop(): return lax.ppermute(x, 'segment', [(i, i + 2) for i in range(6)])  10.2 us
    ppermute x3, waiting for transfers between devices, shards(): lax.ppermute(both[:, :, (3 + d) % 4], 'segment', [(6, (6 + 2 * d) % 8), (...  7.07 us
  transfers between devices with their start and end apart: 27, of which 16 were waited for; matrix products, arithmetic and copies ran while one was open for 1% of the time, Pallas kernels for 12%

profile of v6, /device:TPU:18, one launch (start us, length us, event | category | flops | bytes accessed | tf_op | source)
XLA Modules:
  0.0 273.5 jit_solution(13793630460025545671)
XLA Ops:
  0.0 1.2 fusion.2
  1.2 0.1 collective-permute-start.1
  1.4 1.8 collective-permute-done.1
  3.2 0.2 select_bitcast_fusion.4
  3.4 0.1 fusion
  3.5 0.2 collective-permute-start.6
  3.7 0.4 collective-permute-start.7
  4.1 4.0 %collective-permute-start.3 = (bf16[2,256,640]{2,1,0:T(8,128)(2,1)S(1)}, bf16[2,256,640]{2,1,0:T(8,128)(2,1)S(1)}, u32[]{:S(2)}, u32[]{:S(2)}) collective-permute-start(bf16[2,256,640]{2,1,0:T(8,128)(2,1)S(1)} %fusion), channel_id=1, source_target_pairs={{0,3},{1,0},{2,1},{3,2},{4,7},{5,4},{6,5},{7,6},{8,11},{9,8},{10,9... | collective-permute-start | bytes 1966088 | tf_op jit(solution)/shard_map/ppermute | solution.py:295
  8.1 1.2 collective-permute-done.8
  9.3 0.2 collective-permute-start.9
  9.4 1.0 collective-permute-done.9
  10.5 5.7 %collective-permute-done.3 = bf16[2,256,640]{2,1,0:T(8,128)(2,1)S(1)} collective-permute-done((bf16[2,256,640]{2,1,0:T(8,128)(2,1)S(1)}, bf16[2,256,640]{2,1,0:T(8,128)(2,1)S(1)}, u32[]{:S(2)}, u32[]{:S(2)}) %collective-permute-start.3) | collective-permute-done | bytes 655392 | tf_op jit(solution)/shard_map/ppermute | solution.py:295
  16.2 3.8 %collective-permute-start.5 = (bf16[1,256,640]{2,1,0:T(8,128)(2,1)S(1)}, bf16[1,256,640]{2,1,0:T(8,128)(2,1)S(1)}, u32[]{:S(2)}, u32[]{:S(2)}) collective-permute-start(bf16[1,256,640]{2,1,0:T(8,128)(2,1)S(1)} %slice.43), channel_id=1, source_target_pairs={{0,3},{1,0},{2,1},{3,2},{4,7},{5,4},{6,5},{7,6},{8,11},{9,8},{10,9... | collective-permute-start | bytes 983048 | tf_op jit(solution)/shard_map/ppermute | solution.py:295
  20.0 0.1 collective-permute-start.4
  20.2 0.3 select_bitcast_fusion.1
  20.5 0.6 copy-done.7
  21.1 0.3 copy-done.9
  21.3 1.3 pad_maximum_fusion.1.wv_ref
  22.7 1.4 pad_maximum_fusion.wk_ref
  24.1 0.5 collective-permute-done.5
  24.6 3.8 %collective-permute-done.4 = bf16[1,256,640]{2,1,0:T(8,128)(2,1)S(1)} collective-permute-done((bf16[1,256,640]{2,1,0:T(8,128)(2,1)S(1)}, bf16[1,256,640]{2,1,0:T(8,128)(2,1)S(1)}, u32[]{:S(2)}, u32[]{:S(2)}) %collective-permute-start.4) | collective-permute-done | bytes 327712 | tf_op jit(solution)/shard_map/ppermute | solution.py:295
  28.5 0.1 pad_maximum_fusion.3.far_ref
  28.6 0.5 collective-permute-start.11
  29.1 0.1 pad_maximum_fusion.2.near_ref
  29.3 1.6 collective-permute-start.10
  30.9 2.5 collective-permute-start.14
  33.4 8.5 %stale.4 = (bf16[2,5,1024,128]{3,2,1,0:T(8,128)(2,1)}, bf16[2,5,128,1024]{3,2,1,0:T(8,128)(2,1)}) custom-call(bf16[2,2,256,640]{3,2,1,0:T(8,128)(2,1)S(1)} %pad_maximum_fusion.2.near_ref, bf16[2,2,256,640]{3,2,1,0:T(8,128)(2,1)S(1)} %pad_maximum_fusion.3.far_ref, f32[2,640]{1,0:T(2,128)S(1)} %pad_maximum_fusion.6.ga_ref, ...), custom_call_target="tpu_custom_call" | custom-call | flops 3355443200 | bytes 7864320 | tf_op jit(solution)/shard_map/stale/pallas_call | solution.py:68
  41.9 4.4 %collective-permute-done.11.far_ref = bf16[2,2,256,640]{3,2,1,0:T(8,128)(2,1)S(1)} collective-permute-done((bf16[2,2,256,640]{3,2,1,0:T(8,128)(2,1)S(1)}, bf16[2,2,256,640]{3,2,1,0:T(8,128)(2,1)S(1)}, u32[]{:S(2)}, u32[]{:S(2)}) %collective-permute-start.11) | collective-permute-done | bytes 1310752 | tf_op jit(solution)/shard_map/ppermute | solution.py:295
  46.3 0.7 collective-permute-done.10.near_ref
  47.0 1.8 collective-permute-start.12
  48.8 0.2 collective-permute-start.13
  49.0 8.4 %stale.5 = (bf16[2,5,1024,128]{3,2,1,0:T(8,128)(2,1)}, bf16[2,5,128,1024]{3,2,1,0:T(8,128)(2,1)}) custom-call(bf16[2,2,256,640]{3,2,1,0:T(8,128)(2,1)S(1)} %collective-permute-done.10.near_ref, bf16[2,2,256,640]{3,2,1,0:T(8,128)(2,1)S(1)} %collective-permute-done.11.far_ref, f32[2,640]{1,0:T(2,128)S(1)} %pad_maximum_fusion.6.ga_ref, ...), custom_call_target="tpu_custom_call" | custom-call | flops 3355443200 | bytes 7864320 | tf_op jit(solution)/shard_map/stale/pallas_call | solution.py:68
  57.5 3.5 %collective-permute-done.14.near_ref = bf16[2,2,256,640]{3,2,1,0:T(8,128)(2,1)S(1)} collective-permute-done((bf16[2,2,256,640]{3,2,1,0:T(8,128)(2,1)S(1)}, bf16[2,2,256,640]{3,2,1,0:T(8,128)(2,1)S(1)}, u32[]{:S(2)}, u32[]{:S(2)}) %collective-permute-start.14) | collective-permute-done | bytes 1310752 | tf_op jit(solution)/shard_map/ppermute | solution.py:295
  61.0 2.7 collective-permute-start.17
  63.8 3.3 %collective-permute-start.16 = (bf16[2,64,640]{2,1,0:T(8,128)(2,1)S(1)}, bf16[2,64,640]{2,1,0:T(8,128)(2,1)S(1)}, u32[]{:S(2)}, u32[]{:S(2)}) collective-permute-start(bf16[2,64,640]{2,1,0:T(8,128)(2,1)S(1)} %get-tuple-element.493), channel_id=1, source_target_pairs={{0,1},{1,2},{2,3},{3,4},{4,5},{5,6},{6,7},{7,8},{8,9},{9,10},{10,1... | collective-permute-start | bytes 491528 | tf_op jit(solution)/shard_map/ppermute | solution.py:352
  67.1 8.4 %stale.6 = (bf16[2,5,1024,128]{3,2,1,0:T(8,128)(2,1)}, bf16[2,5,128,1024]{3,2,1,0:T(8,128)(2,1)}) custom-call(bf16[2,2,256,640]{3,2,1,0:T(8,128)(2,1)S(1)} %collective-permute-done.14.near_ref, bf16[2,2,256,640]{3,2,1,0:T(8,128)(2,1)S(1)} %collective-permute-done.15.far_ref, f32[2,640]{1,0:T(2,128)S(1)} %pad_maximum_fusion.6.ga_ref, ...), custom_call_target="tpu_custom_call" | custom-call | flops 3355443200 | bytes 7864320 | tf_op jit(solution)/shard_map/stale/pallas_call | solution.py:68
  75.5 0.4 collective-permute-done.17
  75.9 2.1 collective-permute-done.16
  78.0 0.7 collective-permute-start.18
  78.7 0.1 collective-permute-start.19
  78.9 8.7 %stale.7 = (bf16[2,5,1024,128]{3,2,1,0:T(8,128)(2,1)}, bf16[2,5,128,1024]{3,2,1,0:T(8,128)(2,1)}) custom-call(bf16[2,2,256,640]{3,2,1,0:T(8,128)(2,1)S(1)} %collective-permute-done.12.near_ref, bf16[2,2,256,640]{3,2,1,0:T(8,128)(2,1)S(1)} %collective-permute-done.13.far_ref, f32[2,640]{1,0:T(2,128)S(1)} %pad_maximum_fusion.6.ga_ref, ...), custom_call_target="tpu_custom_call" | custom-call | flops 3355443200 | bytes 7864320 | tf_op jit(solution)/shard_map/stale/pallas_call | solution.py:68
  87.6 0.9 copy-done.14
  88.5 0.3 copy-done.15
  88.8 172.6 %while.13 = (s32[]{:T(128)}, bf16[256,640]{1,0:T(8,128)(2,1)S(1)}, f32[2,640]{1,0:T(2,128)S(1)}, f32[2,640]{1,0:T(2,128)S(1)}, bf16[2,64,640]{2,1,0:T(8,128)(2,1...) while((s32[]{:T(128)}, bf16[256,640]{1,0:T(8,128)(2,1)S(1)}, ...), condition=%wide.region_3.4_spmd, body=%wide.region_0.3_spmd.sunk | while | flops 25999998976 | bytes 46621728 | solution.py:371
  88.8 34.2 %blocks.5 = bf16[256,640]{1,0:T(8,128)(2,1)S(1)} custom-call(bf16[256,640]{1,0:T(8,128)(2,1)S(1)} %get-tuple-element.674.refs_0_, f32[2,640]{1,0:T(2,128)S(1)} %get-tuple-element.701.refs_1_, f32[2,640]{1,0:T(2,128)S(1)} %get-tuple-element.702.refs_2_, bf16[2,64,640]{2,1,0:T(8,128)(2,1)} %get-tuple-element.703.refs_3_, ...), custom_call_target="tpu_custom_call" | custom-call | flops 25999998976 | bytes 44000000 | tf_op jit(solution)/shard_map/while/body/eval_jaxpr/blocks/pallas_call | solution.py:244
  123.0 12.3 %conditional.2 = (bf16[256,640]{1,0:T(8,128)(2,1)S(1)}) conditional(s32[]{:T(128)} %convert_element_type.13, bf16[256,640]{1,0:T(8,128)(2,1)S(1)} %blocks.5, bf16[256,640]{1,0:T(8,128)(2,1)S(1)} %blocks.5), branch_computations={%region_1.1_spmd, %region_2.2_spmd} | conditional | bytes 1966128 | solution.py:369
  123.0 3.4 %collective-permute-start = (bf16[256,640]{1,0:T(8,128)(2,1)S(1)}, bf16[256,640]{1,0:T(8,128)(2,1)S(1)}, u32[]{:S(2)}, u32[]{:S(2)}) collective-permute-start(bf16[256,640]{1,0:T(8,128)(2,1)S(1)} %param.1), channel_id=1, source_target_pairs={{0,32},{16,48},{32,64},{48,80},{64,96},{80,112},{1,33},{17,49},{33... | collective-permute-start | bytes 983048 | tf_op jit(solution)/shard_map/while/body/eval_jaxpr/cond/branch_1_fun/ppermute | solution.py:366
  126.4 8.9 %collective-permute-done = bf16[256,640]{1,0:T(8,128)(2,1)S(1)} collective-permute-done((bf16[256,640]{1,0:T(8,128)(2,1)S(1)}, bf16[256,640]{1,0:T(8,128)(2,1)S(1)}, u32[]{:S(2)}, u32[]{:S(2)}) %collective-permute-start) | collective-permute-done | bytes 327712 | tf_op jit(solution)/shard_map/while/body/eval_jaxpr/cond/branch_1_fun/ppermute | solution.py:366
  135.4 34.2 %blocks.5 = bf16[256,640]{1,0:T(8,128)(2,1)S(1)} custom-call(bf16[256,640]{1,0:T(8,128)(2,1)S(1)} %get-tuple-element.674.refs_0_, f32[2,640]{1,0:T(2,128)S(1)} %get-tuple-element.701.refs_1_, f32[2,640]{1,0:T(2,128)S(1)} %get-tuple-element.702.refs_2_, bf16[2,64,640]{2,1,0:T(8,128)(2,1)} %get-tuple-element.703.refs_3_, ...), custom_call_target="tpu_custom_call" | custom-call | flops 25999998976 | bytes 44000000 | tf_op jit(solution)/shard_map/while/body/eval_jaxpr/blocks/pallas_call | solution.py:244
  169.6 11.8 %conditional.2 = (bf16[256,640]{1,0:T(8,128)(2,1)S(1)}) conditional(s32[]{:T(128)} %convert_element_type.13, bf16[256,640]{1,0:T(8,128)(2,1)S(1)} %blocks.5, bf16[256,640]{1,0:T(8,128)(2,1)S(1)} %blocks.5), branch_computations={%region_1.1_spmd, %region_2.2_spmd} | conditional | bytes 1966128 | solution.py:369
  169.6 3.4 %collective-permute-start = (bf16[256,640]{1,0:T(8,128)(2,1)S(1)}, bf16[256,640]{1,0:T(8,128)(2,1)S(1)}, u32[]{:S(2)}, u32[]{:S(2)}) collective-permute-start(bf16[256,640]{1,0:T(8,128)(2,1)S(1)} %param.1), channel_id=1, source_target_pairs={{0,32},{16,48},{32,64},{48,80},{64,96},{80,112},{1,33},{17,49},{33... | collective-permute-start | bytes 983048 | tf_op jit(solution)/shard_map/while/body/eval_jaxpr/cond/branch_1_fun/ppermute | solution.py:366
  173.0 8.4 %collective-permute-done = bf16[256,640]{1,0:T(8,128)(2,1)S(1)} collective-permute-done((bf16[256,640]{1,0:T(8,128)(2,1)S(1)}, bf16[256,640]{1,0:T(8,128)(2,1)S(1)}, u32[]{:S(2)}, u32[]{:S(2)}) %collective-permute-start) | collective-permute-done | bytes 327712 | tf_op jit(solution)/shard_map/while/body/eval_jaxpr/cond/branch_1_fun/ppermute | solution.py:366
  181.5 34.2 %blocks.5 = bf16[256,640]{1,0:T(8,128)(2,1)S(1)} custom-call(bf16[256,640]{1,0:T(8,128)(2,1)S(1)} %get-tuple-element.674.refs_0_, f32[2,640]{1,0:T(2,128)S(1)} %get-tuple-element.701.refs_1_, f32[2,640]{1,0:T(2,128)S(1)} %get-tuple-element.702.refs_2_, bf16[2,64,640]{2,1,0:T(8,128)(2,1)} %get-tuple-element.703.refs_3_, ...), custom_call_target="tpu_custom_call" | custom-call | flops 25999998976 | bytes 44000000 | tf_op jit(solution)/shard_map/while/body/eval_jaxpr/blocks/pallas_call | solution.py:244
  215.7 11.4 %conditional.2 = (bf16[256,640]{1,0:T(8,128)(2,1)S(1)}) conditional(s32[]{:T(128)} %convert_element_type.13, bf16[256,640]{1,0:T(8,128)(2,1)S(1)} %blocks.5, bf16[256,640]{1,0:T(8,128)(2,1)S(1)} %blocks.5), branch_computations={%region_1.1_spmd, %region_2.2_spmd} | conditional | bytes 1966128 | solution.py:369
  215.7 3.4 %collective-permute-start = (bf16[256,640]{1,0:T(8,128)(2,1)S(1)}, bf16[256,640]{1,0:T(8,128)(2,1)S(1)}, u32[]{:S(2)}, u32[]{:S(2)}) collective-permute-start(bf16[256,640]{1,0:T(8,128)(2,1)S(1)} %param.1), channel_id=1, source_target_pairs={{0,32},{16,48},{32,64},{48,80},{64,96},{80,112},{1,33},{17,49},{33... | collective-permute-start | bytes 983048 | tf_op jit(solution)/shard_map/while/body/eval_jaxpr/cond/branch_1_fun/ppermute | solution.py:366
  219.1 7.9 %collective-permute-done = bf16[256,640]{1,0:T(8,128)(2,1)S(1)} collective-permute-done((bf16[256,640]{1,0:T(8,128)(2,1)S(1)}, bf16[256,640]{1,0:T(8,128)(2,1)S(1)}, u32[]{:S(2)}, u32[]{:S(2)}) %collective-permute-start) | collective-permute-done | bytes 327712 | tf_op jit(solution)/shard_map/while/body/eval_jaxpr/cond/branch_1_fun/ppermute | solution.py:366
  227.1 34.2 %blocks.5 = bf16[256,640]{1,0:T(8,128)(2,1)S(1)} custom-call(bf16[256,640]{1,0:T(8,128)(2,1)S(1)} %get-tuple-element.674.refs_0_, f32[2,640]{1,0:T(2,128)S(1)} %get-tuple-element.701.refs_1_, f32[2,640]{1,0:T(2,128)S(1)} %get-tuple-element.702.refs_2_, bf16[2,64,640]{2,1,0:T(8,128)(2,1)} %get-tuple-element.703.refs_3_, ...), custom_call_target="tpu_custom_call" | custom-call | flops 25999998976 | bytes 44000000 | tf_op jit(solution)/shard_map/while/body/eval_jaxpr/blocks/pallas_call | solution.py:244
  261.5 0.1 collective-permute-start.21
  261.6 1.4 collective-permute-done.21
  263.0 0.7 collective-permute-start.22
  263.7 0.7 collective-permute-start.24
  264.4 1.3 collective-permute-start.23
  265.7 7.1 %collective-permute-done.23 = bf16[2,4,8,640]{3,2,1,0:T(8,128)(2,1)S(1)} collective-permute-done((bf16[2,4,8,640]{3,2,1,0:T(8,128)(2,1)S(1)}, bf16[2,4,8,640]{3,2,1,0:T(8,128)(2,1)S(1)}, u32[]{:S(2)}, u32[]{:S(2)}) %collective-permute-start.23) | collective-permute-done | bytes 81952 | tf_op jit(solution)/shard_map/ppermute | solution.py:379
  272.8 0.7 fusion.13
  (68 shorter events, 0.7 us)
Async XLA Ops:
  0.0 78.8 %copy-start = (bf16[2,4,64,640]{3,2,1,0:T(8,128)(2,1)S(1)}, bf16[2,4,64,640]{3,2,1,0:T(8,128)(2,1)}, u32[]{:S(2)}) copy-start(bf16[2,4,64,640]{3,2,1,0:T(8,128)(2,1)} %param.14) | copy-start | bytes 1966084
  0.0 3.2 %copy-start.3 = (bf16[1,2,2,64,640]{4,3,2,1,0:T(8,128)(2,1)S(1)}, bf16[1,2,2,64,640]{4,3,2,1,0:T(8,128)(2,1)}, u32[]{:S(2)}) copy-start(bf16[1,2,2,64,640]{4,3,2,1,0:T(8,128)(2,1)} %param.16) | copy-start | bytes 983044
  0.0 3.2 %copy-start.2 = (bf16[1,2,4,64,640]{4,3,2,1,0:T(8,128)(2,1)S(1)}, bf16[1,2,4,64,640]{4,3,2,1,0:T(8,128)(2,1)}, u32[]{:S(2)}) copy-start(bf16[1,2,4,64,640]{4,3,2,1,0:T(8,128)(2,1)} %param.15) | copy-start | bytes 1966084
  1.2 1.9 collective-permute-start.1
  1.3 2.2 copy-start.4
  1.3 2.4 copy-start.5
  1.3 6.8 %copy-start.11 = (f32[1,640]{1,0:T(1,128)S(1)}, f32[1,640]{1,0:T(1,128)}, u32[]{:S(2)}) copy-start(f32[1,640]{1,0:T(1,128)} %param.17) | copy-start | bytes 7684
  1.4 7.9 %copy-start.10 = (f32[1,640]{1,0:T(1,128)S(1)}, f32[1,640]{1,0:T(1,128)}, u32[]{:S(2)}) copy-start(f32[1,640]{1,0:T(1,128)} %param.22) | copy-start | bytes 7684
  3.5 16.7 %collective-permute-start.6 = (bf16[640,640]{1,0:T(8,128)(2,1)S(1)}, bf16[640,640]{1,0:T(8,128)(2,1)S(1)}, u32[]{:S(2)}, u32[]{:S(2)}) collective-permute-start(bf16[640,640]{1,0:T(8,128)(2,1)S(1)} %bitcast.84), channel_id=1, source_target_pairs={{0,16},{16,0},{32,48},{48,32},{64,80},{80,64},{96,112},{112,96},{1... | collective-permute-start | bytes 2457608 | tf_op jit(solution)/shard_map/ppermute | solution.py:315
  3.7 16.5 %collective-permute-start.7 = (bf16[640,640]{1,0:T(8,128)(2,1)S(1)}, bf16[640,640]{1,0:T(8,128)(2,1)S(1)}, u32[]{:S(2)}, u32[]{:S(2)}) collective-permute-start(bf16[640,640]{1,0:T(8,128)(2,1)S(1)} %bitcast.86), channel_id=1, source_target_pairs={{0,16},{16,0},{32,48},{48,32},{64,80},{80,64},{96,112},{112,96},{1... | collective-permute-start | bytes 2457608 | tf_op jit(solution)/shard_map/ppermute | solution.py:315
  4.1 12.1 %collective-permute-start.3 = (bf16[2,256,640]{2,1,0:T(8,128)(2,1)S(1)}, bf16[2,256,640]{2,1,0:T(8,128)(2,1)S(1)}, u32[]{:S(2)}, u32[]{:S(2)}) collective-permute-start(bf16[2,256,640]{2,1,0:T(8,128)(2,1)S(1)} %fusion), channel_id=1, source_target_pairs={{0,3},{1,0},{2,1},{3,2},{4,7},{5,4},{6,5},{7,6},{8,11},{9,8},{10,9... | collective-permute-start | bytes 1966088 | tf_op jit(solution)/shard_map/ppermute | solution.py:295
  8.1 11.9 %collective-permute-start.2 = (bf16[2,256,640]{2,1,0:T(8,128)(2,1)S(1)}, bf16[2,256,640]{2,1,0:T(8,128)(2,1)S(1)}, u32[]{:S(2)}, u32[]{:S(2)}) collective-permute-start(bf16[2,256,640]{2,1,0:T(8,128)(2,1)S(1)} %fusion), channel_id=1, source_target_pairs={{0,1},{1,2},{2,3},{3,0},{4,5},{5,6},{6,7},{7,4},{8,9},{9,10},{10,1... | collective-permute-start | bytes 1966088 | tf_op jit(solution)/shard_map/ppermute | solution.py:295
  8.1 1.2 collective-permute-start.8
  9.3 1.2 collective-permute-start.9
  16.2 8.4 %collective-permute-start.5 = (bf16[1,256,640]{2,1,0:T(8,128)(2,1)S(1)}, bf16[1,256,640]{2,1,0:T(8,128)(2,1)S(1)}, u32[]{:S(2)}, u32[]{:S(2)}) collective-permute-start(bf16[1,256,640]{2,1,0:T(8,128)(2,1)S(1)} %slice.43), channel_id=1, source_target_pairs={{0,3},{1,0},{2,1},{3,2},{4,7},{5,4},{6,5},{7,6},{8,11},{9,8},{10,9... | collective-permute-start | bytes 983048 | tf_op jit(solution)/shard_map/ppermute | solution.py:295
  20.0 8.4 %collective-permute-start.4 = (bf16[1,256,640]{2,1,0:T(8,128)(2,1)S(1)}, bf16[1,256,640]{2,1,0:T(8,128)(2,1)S(1)}, u32[]{:S(2)}, u32[]{:S(2)}) collective-permute-start(bf16[1,256,640]{2,1,0:T(8,128)(2,1)S(1)} %slice.42), channel_id=1, source_target_pairs={{0,1},{1,2},{2,3},{3,0},{4,5},{5,6},{6,7},{7,4},{8,9},{9,10},{10,1... | collective-permute-start | bytes 983048 | tf_op jit(solution)/shard_map/ppermute | solution.py:295
  20.1 0.9 copy-start.7
  20.2 1.2 copy-start.9
  28.4 59.2 %collective-permute-start.20 = (bf16[9,640,640]{2,1,0:T(8,128)(2,1)}, bf16[9,640,640]{2,1,0:T(8,128)(2,1)}, u32[]{:S(2)}, u32[]{:S(2)}) collective-permute-start(bf16[9,640,640]{2,1,0:T(8,128)(2,1)} %bitcast.13), channel_id=1, source_target_pairs={{0,16},{16,0},{32,48},{48,32},{64,80},{80,64},{96,112},{112,96},{1... | collective-permute-start | bytes 22118408 | tf_op jit(solution)/shard_map/ppermute | solution.py:315
  28.6 17.7 %collective-permute-start.11 = (bf16[2,2,256,640]{3,2,1,0:T(8,128)(2,1)S(1)}, bf16[2,2,256,640]{3,2,1,0:T(8,128)(2,1)S(1)}, u32[]{:S(2)}, u32[]{:S(2)}) collective-permute-start(bf16[2,2,256,640]{3,2,1,0:T(8,128)(2,1)S(1)} %pad_maximum_fusion.3.far_ref), channel_id=1, source_target_pairs={{0,12},{1,13},{2,14},{3,15},{4,0},{5,1},{6,2},{7,3},{8,4},{9,5},{1... | collective-permute-start | bytes 3932168 | tf_op jit(solution)/shard_map/ppermute | solution.py:295
  29.3 17.7 %collective-permute-start.10 = (bf16[2,2,256,640]{3,2,1,0:T(8,128)(2,1)S(1)}, bf16[2,2,256,640]{3,2,1,0:T(8,128)(2,1)S(1)}, u32[]{:S(2)}, u32[]{:S(2)}) collective-permute-start(bf16[2,2,256,640]{3,2,1,0:T(8,128)(2,1)S(1)} %pad_maximum_fusion.2.near_ref), channel_id=1, source_target_pairs={{0,4},{1,5},{2,6},{3,7},{4,8},{5,9},{6,10},{7,11},{8,12},{9,13},{1... | collective-permute-start | bytes 3932168 | tf_op jit(solution)/shard_map/ppermute | solution.py:295
  30.9 30.1 %collective-permute-start.14 = (bf16[2,2,256,640]{3,2,1,0:T(8,128)(2,1)S(1)}, bf16[2,2,256,640]{3,2,1,0:T(8,128)(2,1)S(1)}, u32[]{:S(2)}, u32[]{:S(2)}) collective-permute-start(bf16[2,2,256,640]{3,2,1,0:T(8,128)(2,1)S(1)} %pad_maximum_fusion.3.far_ref), channel_id=1, source_target_pairs={{0,4},{1,5},{2,6},{3,7},{4,8},{5,9},{6,10},{7,11},{8,12},{9,13},{1... | collective-permute-start | bytes 3932168 | tf_op jit(solution)/shard_map/ppermute | solution.py:295
  33.4 27.6 %collective-permute-start.15 = (bf16[2,2,256,640]{3,2,1,0:T(8,128)(2,1)S(1)}, bf16[2,2,256,640]{3,2,1,0:T(8,128)(2,1)S(1)}, u32[]{:S(2)}, u32[]{:S(2)}) collective-permute-start(bf16[2,2,256,640]{3,2,1,0:T(8,128)(2,1)S(1)} %pad_maximum_fusion.2.near_ref), channel_id=1, source_target_pairs={{0,12},{1,13},{2,14},{3,15},{4,0},{5,1},{6,2},{7,3},{8,4},{9,5},{1... | collective-permute-start | bytes 3932168 | tf_op jit(solution)/shard_map/ppermute | solution.py:295
  47.0 31.0 %collective-permute-start.12 = (bf16[2,2,256,640]{3,2,1,0:T(8,128)(2,1)S(1)}, bf16[2,2,256,640]{3,2,1,0:T(8,128)(2,1)S(1)}, u32[]{:S(2)}, u32[]{:S(2)}) collective-permute-start(bf16[2,2,256,640]{3,2,1,0:T(8,128)(2,1)S(1)} %collective-permute-done.10.near_ref), channel_id=1, source_target_pairs={{0,4},{1,5},{2,6},{3,7},{4,8},{5,9},{6,10},{7,11},{8,12},{9,13},{1... | collective-permute-start | bytes 3932168 | tf_op jit(solution)/shard_map/ppermute | solution.py:295
  48.8 29.2 %collective-permute-start.13 = (bf16[2,2,256,640]{3,2,1,0:T(8,128)(2,1)S(1)}, bf16[2,2,256,640]{3,2,1,0:T(8,128)(2,1)S(1)}, u32[]{:S(2)}, u32[]{:S(2)}) collective-permute-start(bf16[2,2,256,640]{3,2,1,0:T(8,128)(2,1)S(1)} %collective-permute-done.11.far_ref), channel_id=1, source_target_pairs={{0,12},{1,13},{2,14},{3,15},{4,0},{5,1},{6,2},{7,3},{8,4},{9,5},{1... | collective-permute-start | bytes 3932168 | tf_op jit(solution)/shard_map/ppermute | solution.py:295
  61.0 14.8 %collective-permute-start.17 = (bf16[2,64,640]{2,1,0:T(8,128)(2,1)S(1)}, bf16[2,64,640]{2,1,0:T(8,128)(2,1)S(1)}, u32[]{:S(2)}, u32[]{:S(2)}) collective-permute-start(bf16[2,64,640]{2,1,0:T(8,128)(2,1)S(1)} %get-tuple-element.492), channel_id=1, source_target_pairs={{1,0},{2,1},{3,2},{4,3},{5,4},{6,5},{7,6},{8,7},{9,8},{10,9},{11,1... | collective-permute-start | bytes 491528 | tf_op jit(solution)/shard_map/ppermute | solution.py:353
  63.7 14.3 %copy-start.12 = (bf16[1,640,640]{2,1,0:T(8,128)(2,1)S(1)}, bf16[1,640,640]{2,1,0:T(8,128)(2,1)}, u32[]{:S(2)}) copy-start(bf16[1,640,640]{2,1,0:T(8,128)(2,1)} %param.18) | copy-start | bytes 2457604
  63.7 15.0 %copy-start.13 = (bf16[1,640,640]{2,1,0:T(8,128)(2,1)S(1)}, bf16[1,640,640]{2,1,0:T(8,128)(2,1)}, u32[]{:S(2)}) copy-start(bf16[1,640,640]{2,1,0:T(8,128)(2,1)} %param.21) | copy-start | bytes 2457604
  63.8 14.2 %collective-permute-start.16 = (bf16[2,64,640]{2,1,0:T(8,128)(2,1)S(1)}, bf16[2,64,640]{2,1,0:T(8,128)(2,1)S(1)}, u32[]{:S(2)}, u32[]{:S(2)}) collective-permute-start(bf16[2,64,640]{2,1,0:T(8,128)(2,1)S(1)} %get-tuple-element.493), channel_id=1, source_target_pairs={{0,1},{1,2},{2,3},{3,4},{4,5},{5,6},{6,7},{7,8},{8,9},{9,10},{10,1... | collective-permute-start | bytes 491528 | tf_op jit(solution)/shard_map/ppermute | solution.py:352
  75.9 11.7 %copy-start.16 = (bf16[2,64,640]{2,1,0:T(8,128)(2,1)}, bf16[2,64,640]{2,1,0:T(8,128)(2,1)S(1)}, u32[]{:S(2)}) copy-start(bf16[2,64,640]{2,1,0:T(8,128)(2,1)S(1)} %collective-permute-done.17) | copy-start | bytes 491524
  78.0 9.6 %copy-start.17 = (bf16[2,64,640]{2,1,0:T(8,128)(2,1)}, bf16[2,64,640]{2,1,0:T(8,128)(2,1)S(1)}, u32[]{:S(2)}) copy-start(bf16[2,64,640]{2,1,0:T(8,128)(2,1)S(1)} %collective-permute-done.16) | copy-start | bytes 491524
  78.0 9.6 %collective-permute-start.18 = (bf16[640,640]{1,0:T(8,128)(2,1)S(1)}, bf16[640,640]{1,0:T(8,128)(2,1)S(1)}, u32[]{:S(2)}, u32[]{:S(2)}) collective-permute-start(bf16[640,640]{1,0:T(8,128)(2,1)S(1)} %bitcast.90), channel_id=1, source_target_pairs={{0,16},{16,0},{32,48},{48,32},{64,80},{80,64},{96,112},{112,96},{1... | collective-permute-start | bytes 2457608 | tf_op jit(solution)/shard_map/ppermute | solution.py:315
  78.7 8.9 %collective-permute-start.19 = (bf16[640,640]{1,0:T(8,128)(2,1)S(1)}, bf16[640,640]{1,0:T(8,128)(2,1)S(1)}, u32[]{:S(2)}, u32[]{:S(2)}) collective-permute-start(bf16[640,640]{1,0:T(8,128)(2,1)S(1)} %bitcast.92), channel_id=1, source_target_pairs={{0,16},{16,0},{32,48},{48,32},{64,80},{80,64},{96,112},{112,96},{1... | collective-permute-start | bytes 2457608 | tf_op jit(solution)/shard_map/ppermute | solution.py:315
  78.9 10.0 %copy-start.6 = (bf16[1,640,640]{2,1,0:T(8,128)(2,1)S(1)}, bf16[1,640,640]{2,1,0:T(8,128)(2,1)}, u32[]{:S(2)}) copy-start(bf16[1,640,640]{2,1,0:T(8,128)(2,1)} %param.20) | copy-start | bytes 2457604
  78.9 10.0 %copy-start.8 = (bf16[640,640]{1,0:T(8,128)(2,1)S(1)}, bf16[640,640]{1,0:T(8,128)(2,1)}, u32[]{:S(2)}) copy-start(bf16[640,640]{1,0:T(8,128)(2,1)} %copy-done.7) | copy-start | bytes 2457604
  87.6 0.9 copy-start.14
  87.6 1.2 copy-start.15
  123.0 12.3 %collective-permute-start = (bf16[256,640]{1,0:T(8,128)(2,1)S(1)}, bf16[256,640]{1,0:T(8,128)(2,1)S(1)}, u32[]{:S(2)}, u32[]{:S(2)}) collective-permute-start(bf16[256,640]{1,0:T(8,128)(2,1)S(1)} %param.1), channel_id=1, source_target_pairs={{0,32},{16,48},{32,64},{48,80},{64,96},{80,112},{1,33},{17,49},{33... | collective-permute-start | bytes 983048 | tf_op jit(solution)/shard_map/while/body/eval_jaxpr/cond/branch_1_fun/ppermute | solution.py:366
  169.6 11.8 %collective-permute-start = (bf16[256,640]{1,0:T(8,128)(2,1)S(1)}, bf16[256,640]{1,0:T(8,128)(2,1)S(1)}, u32[]{:S(2)}, u32[]{:S(2)}) collective-permute-start(bf16[256,640]{1,0:T(8,128)(2,1)S(1)} %param.1), channel_id=1, source_target_pairs={{0,32},{16,48},{32,64},{48,80},{64,96},{80,112},{1,33},{17,49},{33... | collective-permute-start | bytes 983048 | tf_op jit(solution)/shard_map/while/body/eval_jaxpr/cond/branch_1_fun/ppermute | solution.py:366
  215.7 11.3 %collective-permute-start = (bf16[256,640]{1,0:T(8,128)(2,1)S(1)}, bf16[256,640]{1,0:T(8,128)(2,1)S(1)}, u32[]{:S(2)}, u32[]{:S(2)}) collective-permute-start(bf16[256,640]{1,0:T(8,128)(2,1)S(1)} %param.1), channel_id=1, source_target_pairs={{0,32},{16,48},{32,64},{48,80},{64,96},{80,112},{1,33},{17,49},{33... | collective-permute-start | bytes 983048 | tf_op jit(solution)/shard_map/while/body/eval_jaxpr/cond/branch_1_fun/ppermute | solution.py:366
  261.4 12.1 %copy-start.1 = (bf16[2,4,64,640]{3,2,1,0:T(8,128)(2,1)S(1)}, bf16[2,4,64,640]{3,2,1,0:T(8,128)(2,1)}, u32[]{:S(2)}) copy-start(bf16[2,4,64,640]{3,2,1,0:T(8,128)(2,1)} %param.14) | copy-start | bytes 1966084
  261.5 1.5 collective-permute-start.21
  263.0 2.7 collective-permute-start.22
  263.7 2.0 collective-permute-start.24
  264.4 8.4 %collective-permute-start.23 = (bf16[2,4,8,640]{3,2,1,0:T(8,128)(2,1)S(1)}, bf16[2,4,8,640]{3,2,1,0:T(8,128)(2,1)S(1)}, u32[]{:S(2)}, u32[]{:S(2)}) collective-permute-start(bf16[2,4,8,640]{3,2,1,0:T(8,128)(2,1)S(1)} %get-tuple-element.487), channel_id=1, source_target_pairs={{96,32},{112,48},{97,33},{113,49},{98,34},{114,50},{99,35},{115,51... | collective-permute-start | bytes 245768 | tf_op jit(solution)/shard_map/ppermute | solution.py:379
